TPU v7x, 512 devices: a whole 4x8x8 slice. The times are simulated.
512 devices in a mesh: row: 16 (over y, core), col: 32 (over z, x).
Axes of the slice: x: 4, y: 8, z: 8, core: 2. Of those that a mesh axis runs over, the one named last changes fastest.
Arguments:
- query_matrix: bfloat16 [128, 512, 768], P('row', 'col'), may hold values from -6 to 16.133757
- key_matrix: bfloat16 [128, 512, 768], P('row', 'col'), may hold values from -6 to 6
- value_matrix: bfloat16 [128, 512, 768], P('row', 'col'), may hold values from -6 to 6
- tissue: int32 [128, 512], replicated, may hold values 0 or 1
- dilation_levels: int32 [16], replicated, may hold values from 0 to 2
- segment_levels: int32 [16], replicated, may hold values from 0 to 2
- output_matrix: bfloat16 [768, 768], replicated, may hold values from -0.21875 to 0.21875
Outputs:
- encoded: bfloat16 [128, 512, 768], P('row', 'col')
Inputs may be any that keep to these rules, and one draw needn't show every extreme that they name: 1 marks a tissue tile, 0 background. Head h uses the dilation 8 * 2^dilation_levels[h]. Head h uses segments of 512 / 2^segment_levels[h] tiles of a grid row.
All inputs are finite; a program needn't handle non-finite values.
Results may differ from a plain program's by a relative error of at most 0.0055.
Values may be sent and summed in bfloat16 or wider, within the bound.
No kernel may reach another device: no remote copies, remote signals or barrier semaphores. Data moves between devices by JAX's collectives and lax.ppermute only.
A program may use at most 64 MiB of HBM per device.

v0:
```python
import math

import jax
import jax.numpy as jnp
import numpy as np
from jax import lax
from jax.sharding import PartitionSpec as P

HEAD_COUNT = 16
R = 8
DILATION_MIN = 8


NEG_FILL = -1e30


def padded_2(x, sides, width):
    for axis, dim in sides:
        peers, length = (lax.axis_size(axis), x.shape[dim])
        up = [(i, (i + 1) % peers) for i in range(peers - 1)]
        down = [(j, i) for i, j in up]
        last = lax.slice_in_dim(x, length - width, length, axis=dim)
        first = lax.slice_in_dim(x, 0, width, axis=dim)
        before = lax.ppermute(last, axis, up)
        after = lax.ppermute(first, axis, down)
        x = jnp.concatenate([before, x, after], axis=dim)
    return x


def window_static(device_rows, device_columns):
    region_rows = np.arange(device_rows + 2 * R) - R
    query_rows = np.arange(device_rows)
    region_cols = np.arange(device_columns + 2 * R) - R
    query_cols = np.arange(device_columns)
    near_rows = np.abs(region_rows[None, :] - query_rows[:, None]) <= R
    near_cols = np.abs(region_cols[None, :] - query_cols[:, None]) <= R
    same_rows = region_rows[None, :] == query_rows[:, None]
    same_cols = region_cols[None, :] == query_cols[:, None]
    near_both = near_rows[:, None, :, None] & near_cols[None, :, None, :]
    self_both = same_rows[:, None, :, None] & same_cols[None, :, None, :]
    return (near_both, self_both)


def window_part(queries, key_region, value_region, permitted_mask, group_size):
    head_dimension = queries.shape[-1] // HEAD_COUNT
    scale = 1.0 / math.sqrt(head_dimension)
    numerators, maxima, totals = ([], [], [])
    for head_first in range(0, HEAD_COUNT, group_size):
        lower = head_first * head_dimension
        upper = (head_first + group_size) * head_dimension
        query_grp = queries[:, lower:upper].reshape(queries.shape[0], group_size, head_dimension)
        key_grp = key_region[:, lower:upper].reshape(
            key_region.shape[0], group_size, head_dimension
        )
        value_grp = value_region[:, lower:upper].reshape(
            value_region.shape[0], group_size, head_dimension
        )
        scores = (
            jnp.einsum("qhd,khd->hqk", query_grp, key_grp, preferred_element_type=jnp.float32)
            * scale
        )
        scores = jnp.where(permitted_mask[None], scores, NEG_FILL)
        highest = jnp.max(scores, axis=-1)
        exp_terms = jnp.exp(scores - highest[..., None])
        totals.append(jnp.sum(exp_terms, axis=-1))
        numerators.append(
            jnp.einsum(
                "hqk,khd->qhd",
                exp_terms.astype(jnp.bfloat16),
                value_grp,
                preferred_element_type=jnp.float32,
            )
        )
        maxima.append(highest)
    return (
        jnp.concatenate(numerators, axis=1),
        jnp.concatenate(maxima, axis=0).T,
        jnp.concatenate(totals, axis=0).T,
    )


def dilation_valid_mask(
    tissue,
    row_indices,
    head_indices,
    column_indices,
    dilation_levels,
    segment_levels,
    selected_count,
    column_total,
):
    key_columns = (
        jnp.arange(selected_count, dtype=jnp.int32)[None, :] * DILATION_MIN
        + (head_indices % DILATION_MIN)[:, None]
    )
    tissue_keys = tissue[row_indices[:, None], key_columns]
    dilation_stride = jnp.left_shift(jnp.int32(DILATION_MIN), dilation_levels[head_indices])
    segment = jnp.right_shift(jnp.int32(column_total), segment_levels[head_indices])
    phase_ok = key_columns % dilation_stride[:, None] == (head_indices % dilation_stride)[:, None]
    key_seg = key_columns // segment[:, None]
    query_seg = column_indices[None, :] // segment[:, None]
    same_seg = key_seg[:, None, :] == query_seg[:, :, None]
    return same_seg & ((tissue_keys == 1) & phase_ok)[:, None, :]


def dilation_in_grid(queries, keys_sel, values_sel, permitted_mask):
    scale = 1.0 / math.sqrt(queries.shape[-1])
    scores = (
        jnp.einsum("rchw,rshw->rhcs", queries, keys_sel, preferred_element_type=jnp.float32) * scale
    )
    scores = jnp.where(permitted_mask, scores, NEG_FILL)
    highest = jnp.max(scores, axis=-1)
    exp_terms = jnp.where(permitted_mask, jnp.exp(scores - highest[..., None]), 0.0)
    totals = jnp.sum(exp_terms, axis=-1)
    softmax_numer = jnp.einsum(
        "rhcs,rshw->rchw",
        exp_terms.astype(jnp.bfloat16),
        values_sel,
        preferred_element_type=jnp.float32,
    )
    return (softmax_numer, highest, totals)


def merge_partials(
    neighbour_numer, neighbour_max, neighbour_sum, dilation_numer, dilation_score_max, dilation_sum
):
    running_maximum = jnp.maximum(neighbour_max, dilation_score_max)
    neighbour_rescale = jnp.exp(neighbour_max - running_maximum)
    dilation_rescale = jnp.exp(dilation_score_max - running_maximum)
    softmax_numer = (
        neighbour_rescale[..., None] * neighbour_numer
        + dilation_rescale[..., None] * dilation_numer
    )
    softmax_denom = neighbour_rescale * neighbour_sum + dilation_rescale * dilation_sum
    return softmax_numer / softmax_denom[..., None]


def per_device(
    query_matrix, key_matrix, value_matrix, tissue, dilation_levels, segment_levels, output_matrix
):
    device_rows, device_columns, model_width = query_matrix.shape
    head_dimension = model_width // HEAD_COUNT
    col_count = lax.axis_size("col")
    column_total = device_columns * col_count
    selected_count = column_total // DILATION_MIN
    local_selection = device_columns // DILATION_MIN
    row_offset = lax.axis_index("row") * device_rows
    column_offset = lax.axis_index("col") * device_columns
    packed = jnp.concatenate([key_matrix, value_matrix], axis=-1)
    padded = padded_2(packed, (("row", 0), ("col", 1)), R)
    key_region = padded[:, :, :model_width].reshape(-1, model_width)
    value_region = padded[:, :, model_width:].reshape(-1, model_width)
    tissue_pad = jnp.pad(tissue, R)
    tissue_reg = lax.dynamic_slice(
        tissue_pad, (row_offset, column_offset), (device_rows + 2 * R, device_columns + 2 * R)
    )
    near_both, self_both = window_static(device_rows, device_columns)
    permitted_mask = jnp.asarray(near_both) & (tissue_reg[None, None] == 1) | jnp.asarray(self_both)
    permitted_mask = permitted_mask.reshape(device_rows * device_columns, -1)
    neighbour_numer, neighbour_max, neighbour_sum = window_part(
        query_matrix.reshape(-1, model_width), key_region, value_region, permitted_mask, 2
    )
    phase_table = np.arange(HEAD_COUNT)[None, :] % DILATION_MIN == np.arange(DILATION_MIN)[:, None]
    phase_table = jnp.asarray(phase_table)[None, None, :, :, None]
    key_phases = key_matrix.reshape(
        device_rows, local_selection, DILATION_MIN, HEAD_COUNT, head_dimension
    )
    value_phases = value_matrix.reshape(
        device_rows, local_selection, DILATION_MIN, HEAD_COUNT, head_dimension
    )
    zero_entry = jnp.zeros((), jnp.bfloat16)
    key_selected = jnp.sum(
        jnp.where(phase_table, key_phases, zero_entry), axis=2, dtype=jnp.bfloat16
    ).reshape(device_rows, local_selection, model_width)
    value_selected = jnp.sum(
        jnp.where(phase_table, value_phases, zero_entry), axis=2, dtype=jnp.bfloat16
    ).reshape(device_rows, local_selection, model_width)
    token_count = device_rows * HEAD_COUNT
    k_all, v_all = (
        lax.all_gather(key_selected, "col", axis=1, tiled=True),
        lax.all_gather(value_selected, "col", axis=1, tiled=True),
    )
    key_grid = k_all.reshape(device_rows, selected_count, HEAD_COUNT, head_dimension)
    value_grid = v_all.reshape(device_rows, selected_count, HEAD_COUNT, head_dimension)
    item_ids = jnp.arange(token_count, dtype=jnp.int32)
    column_indices = column_offset + jnp.arange(device_columns, dtype=jnp.int32)
    dilation_permitted = dilation_valid_mask(
        tissue,
        row_offset + item_ids // HEAD_COUNT,
        item_ids % HEAD_COUNT,
        column_indices,
        dilation_levels,
        segment_levels,
        selected_count,
        column_total,
    )
    dilation_permitted = dilation_permitted.reshape(
        device_rows, HEAD_COUNT, device_columns, selected_count
    )
    query_grid = query_matrix.reshape(device_rows, device_columns, HEAD_COUNT, head_dimension)
    grid_numer, grid_max, grid_sum = dilation_in_grid(
        query_grid, key_grid, value_grid, dilation_permitted
    )
    dilation_numer = grid_numer.reshape(-1, HEAD_COUNT, head_dimension)
    dilation_score_max = grid_max.transpose(0, 2, 1).reshape(-1, HEAD_COUNT)
    dilation_sum = grid_sum.transpose(0, 2, 1).reshape(-1, HEAD_COUNT)
    attended = (
        merge_partials(
            neighbour_numer,
            neighbour_max,
            neighbour_sum,
            dilation_numer,
            dilation_score_max,
            dilation_sum,
        )
        .reshape(-1, model_width)
        .astype(jnp.bfloat16)
    )
    encoded = jnp.dot(attended, output_matrix, preferred_element_type=jnp.float32).astype(
        jnp.bfloat16
    )
    return encoded.reshape(device_rows, device_columns, model_width)


def solution(mesh):
    in_specs = (
        P("row", "col", None),
        P("row", "col", None),
        P("row", "col", None),
        P(),
        P(),
        P(),
        P(),
    )
    out_specs = P("row", "col", None)
    return jax.shard_map(
        per_device, mesh=mesh, in_specs=in_specs, out_specs=out_specs, check_vma=False
    )
```

profile of v0, /device:TPU:56, one launch (start us, length us, event | category | flops | bytes accessed | tf_op | source)
XLA Modules:
  0.0 276.5 jit_solution(2129543870219069759)
XLA Ops:
  0.0 1.1 constant_dynamic-update-slice_fusion.1
  1.1 0.9 constant_dynamic-update-slice_fusion
  2.0 2.7 collective-permute-start.1
  4.7 2.4 collective-permute-start
  7.2 1.9 fusion.111
  9.1 10.0 %fusion.98 = s32[128]{0:T(128)S(1)} fusion(s32[]{:T(128)} %bitcast.62, s32[]{:T(128)} %bitcast.63, s32[]{:T(128)} %bitcast.64, s32[]{:T(128)} %bitcast.65, s32[]{:T(128)} %bitcast.66, s32[]{:T(128)} %bitcast.68, s32[]{:T(128)} %bitcast.67, s32[]{:T(128)} %bitcast.53, s32[]{:T(128)} %bitcast.54, s32[]{:T(128)} %bitcast.55, s32[]{:T(128)} %bitcast.56, ...), kind=kLoop, calls=%fused_computation.190 | loop fusion | flops 5120 | bytes 576 | tf_op jit(solution)/shard_map/shift_left | solution.py:97
  19.3 1.6 reshape.570
  20.9 1.6 reshape.584
  22.5 0.7 fusion.112
  23.2 10.0 %fusion.97 = s32[128]{0:T(128)S(1)} fusion(s32[]{:T(128)} %bitcast.45, s32[]{:T(128)} %bitcast.46, s32[]{:T(128)} %bitcast.47, s32[]{:T(128)} %bitcast.48, s32[]{:T(128)} %bitcast.49, s32[]{:T(128)} %bitcast.51, s32[]{:T(128)} %bitcast.50, s32[]{:T(128)} %bitcast.28, s32[]{:T(128)} %bitcast.30, s32[]{:T(128)} %bitcast.32, s32[]{:T(128)} %bitcast.34, ...), kind=kLoop, calls=%fused_computation.189 | loop fusion | flops 5120 | bytes 576 | tf_op jit(solution)/shard_map/shift_right_arithmetic | solution.py:98
  33.5 65.0 %gather_fusion = s32[8192]{0:T(1024)S(1)} fusion(s32[128,512]{1,0:T(8,128)S(1)} %copy-done.1, s32[8192]{0:T(1024)S(1)} %reshape.613), kind=kCustom, calls=%fused_computation | custom fusion | bytes 131072 | tf_op jit(solution)/shard_map/gather | solution.py:96
  98.6 0.8 fusion.110
  99.4 1.0 select_reduce_fusion.1
  100.6 0.8 add_select_fusion.1
  101.4 1.4 add_select_fusion
  102.8 2.2 and_or_fusion
  105.0 0.7 fusion.79
  105.7 55.9 %all_gather.6 = bf16[8,64,768]{2,0,1:T(8,128)(2,1)S(1)} all-gather(bf16[8,2,768]{2,0,1:T(8,128)(2,1)S(1)} %copy.179), channel_id=1, replica_groups=mesh['row'=16,'col'=32] {'col'}, dimensions={1}, use_global_device_ids=true | all-gather | bytes 811008 | tf_op jit(solution)/shard_map/all_gather | solution.py:180
  162.2 1.6 copy.180
  163.9 2.0 fusion.113
  165.9 1.3 pad_maximum_fusion.1
  167.3 1.1 fusion.109
  168.4 3.9 %collective-permute-start.2 = (bf16[24,8,1536]{2,1,0:T(8,128)(2,1)}, bf16[24,8,1536]{2,1,0:T(8,128)(2,1)}, u32[]{:S(2)}, u32[]{:S(2)}) collective-permute-start(bf16[24,8,1536]{2,1,0:T(8,128)(2,1)} %get-tuple-element.28), channel_id=1, source_target_pairs={{0,1},{1,2},{2,3},{3,4},{4,5},{5,6},{6,7},{7,8},{8,9},{9,10},{10,1... | collective-permute-start | bytes 1769480 | tf_op jit(solution)/shard_map/ppermute | solution.py:24
  172.2 1.3 collective-permute-start.3
  173.5 1.1 fusion.26
  174.6 1.5 copy.227
  176.0 1.4 copy.225
  177.5 0.7 copy.223
  178.2 0.7 copy.221
  178.9 0.7 copy.219
  179.6 0.7 copy.217
  180.3 0.7 copy.215
  181.0 0.7 copy.213
  183.5 51.7 %all_gather.7 = bf16[8,64,768]{2,0,1:T(8,128)(2,1)S(1)} all-gather(bf16[8,2,768]{2,0,1:T(8,128)(2,1)S(1)} %copy.199), channel_id=1, replica_groups=mesh['row'=16,'col'=32] {'col'}, dimensions={1}, use_global_device_ids=true | all-gather | bytes 811008 | tf_op jit(solution)/shard_map/all_gather | solution.py:181
  235.2 1.6 copy.200
  236.8 2.4 convolution_bitcast_fusion
  240.0 0.9 copy.202
  240.9 1.7 pad_maximum_fusion
  242.8 1.2 fusion.108
  244.0 1.7 copy.235
  245.7 1.7 copy.234
  247.4 1.7 copy.233
  249.2 0.8 copy.232
  249.9 0.8 copy.231
  250.7 0.8 copy.230
  251.5 0.8 copy.229
  252.3 0.8 copy.228
  253.2 1.2 fusion.107
  254.4 1.7 copy.226
  256.1 1.1 copy.224
  257.1 1.1 copy.222
  259.7 1.2 fusion.25
  260.8 0.8 fusion.28
  263.0 0.8 fusion.32
  265.1 0.8 fusion.36
  266.2 0.9 fusion.120
  267.1 0.9 fusion.121
  268.1 1.4 concatenate.24
  269.5 0.9 fusion.40
  270.4 1.6 fusion.19
  272.0 0.9 fusion.18
  272.9 1.4 concatenate.27
  274.3 1.0 broadcast_multiply_fusion
  275.4 1.0 convolution_convert_fusion
  (132 shorter events, 8.4 us)
Async XLA Ops:
  0.0 275.4 %copy-start = (bf16[768,768]{1,0:T(8,128)(2,1)S(1)}, bf16[768,768]{1,0:T(8,128)(2,1)}, u32[]{:S(2)}) copy-start(bf16[768,768]{1,0:T(8,128)(2,1)} %param.16) | copy-start | bytes 3538948
  0.0 22.5 %copy-start.23 = (s32[16]{0:T(128)S(1)}, s32[16]{0:T(128)}, u32[]{:S(2)}) copy-start(s32[16]{0:T(128)} %param.15) | copy-start | bytes 196
  0.0 33.5 %copy-start.1 = (s32[128,512]{1,0:T(8,128)S(1)}, s32[128,512]{1,0:T(8,128)}, u32[]{:S(2)}) copy-start(s32[128,512]{1,0:T(8,128)} %param.13) | copy-start | bytes 786436
  2.0 163.9 %collective-permute-start.1 = (bf16[8,16,1536]{2,1,0:T(8,128)(2,1)S(1)}, bf16[8,16,1536]{2,1,0:T(8,128)(2,1)}, u32[]{:S(2)}, u32[]{:S(2)}) collective-permute-start(bf16[8,16,1536]{2,1,0:T(8,128)(2,1)S(1)} %constant_dynamic-update-slice_fusion), channel_id=1, source_target_pairs={{32,0},{64,32},{96,64},{128,96},{160,128},{192,160},{224,192},{256... | collective-permute-start | bytes 1179656 | tf_op jit(solution)/shard_map/ppermute | solution.py:25
  4.7 161.2 %collective-permute-start = (bf16[8,16,1536]{2,1,0:T(8,128)(2,1)S(1)}, bf16[8,16,1536]{2,1,0:T(8,128)(2,1)}, u32[]{:S(2)}, u32[]{:S(2)}) collective-permute-start(bf16[8,16,1536]{2,1,0:T(8,128)(2,1)S(1)} %constant_dynamic-update-slice_fusion), channel_id=1, source_target_pairs={{0,32},{32,64},{64,96},{96,128},{128,160},{160,192},{192,224},{224... | collective-permute-start | bytes 1179656 | tf_op jit(solution)/shard_map/ppermute | solution.py:24
  33.5 65.1 %copy-start.4 = (bf16[8,16,768]{2,1,0:T(8,128)(2,1)S(1)}, bf16[8,16,768]{2,1,0:T(8,128)(2,1)}, u32[]{:S(2)}) copy-start(bf16[8,16,768]{2,1,0:T(8,128)(2,1)} %param.10) | copy-start | bytes 589828
  33.5 65.9 %copy-start.40 = (pred[8,16]{1,0:T(8,128)(4,1)S(1)}, pred[8,16]{1,0:T(8,128)(4,1)}, u32[]{:S(2)}) copy-start(pred[8,16]{1,0:T(8,128)(4,1)} %constant.110.clone) | copy-start | bytes 388
  101.4 73.2 %copy-start.5 = (s32[8,16,64]{2,1,0:T(8,128)}, s32[8,16,64]{2,1,0:T(8,128)S(1)}, u32[]{:S(2)}) copy-start(s32[8,16,64]{2,1,0:T(8,128)S(1)} %add_select_fusion.1) | copy-start | bytes 98308
  162.2 1.7 copy-start.6
  165.9 16.7 %copy-start.7 = (f32[8,16,16]{2,1,0:T(8,128)}, f32[8,16,16]{2,1,0:T(8,128)S(1)}, u32[]{:S(2)}) copy-start(f32[8,16,16]{2,1,0:T(8,128)S(1)} %get-tuple-element.72) | copy-start | bytes 24580
  167.2 10.3 %copy-start.22 = (bf16[128,96]{1,0:T(8,128)(2,1)S(1)}, bf16[128,96]{1,0:T(8,128)(2,1)}, u32[]{:S(2)}) copy-start(bf16[128,96]{1,0:T(8,128)(2,1)} %get-tuple-element.32) | copy-start | bytes 73732
  167.2 11.0 %copy-start.21 = (bf16[128,96]{1,0:T(8,128)(2,1)S(1)}, bf16[128,96]{1,0:T(8,128)(2,1)}, u32[]{:S(2)}) copy-start(bf16[128,96]{1,0:T(8,128)(2,1)} %get-tuple-element.33) | copy-start | bytes 73732
  167.2 11.7 %copy-start.20 = (bf16[128,96]{1,0:T(8,128)(2,1)S(1)}, bf16[128,96]{1,0:T(8,128)(2,1)}, u32[]{:S(2)}) copy-start(bf16[128,96]{1,0:T(8,128)(2,1)} %get-tuple-element.34) | copy-start | bytes 73732
  167.2 12.4 %copy-start.19 = (bf16[128,96]{1,0:T(8,128)(2,1)S(1)}, bf16[128,96]{1,0:T(8,128)(2,1)}, u32[]{:S(2)}) copy-start(bf16[128,96]{1,0:T(8,128)(2,1)} %get-tuple-element.35) | copy-start | bytes 73732
  167.2 13.1 %copy-start.18 = (bf16[128,96]{1,0:T(8,128)(2,1)S(1)}, bf16[128,96]{1,0:T(8,128)(2,1)}, u32[]{:S(2)}) copy-start(bf16[128,96]{1,0:T(8,128)(2,1)} %get-tuple-element.36) | copy-start | bytes 73732
  167.3 14.4 %copy-start.3 = (pred[8,16,24,32]{3,2,1,0:T(8,128)(4,1)S(1)}, pred[8,16,24,32]{3,2,1,0:T(8,128)(4,1)}, u32[]{:S(2)}) copy-start(pred[8,16,24,32]{3,2,1,0:T(8,128)(4,1)} %and_or_fusion) | copy-start | bytes 294916
  167.3 15.2 %copy-start.17 = (bf16[8,2,16,48]{3,2,1,0:T(8,128)(2,1)S(1)}, bf16[8,2,16,48]{3,2,1,0:T(8,128)(2,1)}, u32[]{:S(2)}) copy-start(bf16[8,2,16,48]{3,2,1,0:T(8,128)(2,1)} %get-tuple-element.6) | copy-start | bytes 73732
  168.4 72.5 %collective-permute-start.2 = (bf16[24,8,1536]{2,1,0:T(8,128)(2,1)}, bf16[24,8,1536]{2,1,0:T(8,128)(2,1)}, u32[]{:S(2)}, u32[]{:S(2)}) collective-permute-start(bf16[24,8,1536]{2,1,0:T(8,128)(2,1)} %get-tuple-element.28), channel_id=1, source_target_pairs={{0,1},{1,2},{2,3},{3,4},{4,5},{5,6},{6,7},{7,8},{8,9},{9,10},{10,1... | collective-permute-start | bytes 1769480 | tf_op jit(solution)/shard_map/ppermute | solution.py:24
  172.2 68.7 %collective-permute-start.3 = (bf16[24,8,1536]{2,1,0:T(8,128)(2,1)}, bf16[24,8,1536]{2,1,0:T(8,128)(2,1)}, u32[]{:S(2)}, u32[]{:S(2)}) collective-permute-start(bf16[24,8,1536]{2,1,0:T(8,128)(2,1)} %get-tuple-element.29), channel_id=1, source_target_pairs={{1,0},{2,1},{3,2},{4,3},{5,4},{6,5},{7,6},{8,7},{9,8},{10,9},{11,1... | collective-permute-start | bytes 1769480 | tf_op jit(solution)/shard_map/ppermute | solution.py:25
  253.2 5.8 %copy-start.31 = (bf16[128,96]{0,1:T(8,128)(2,1)S(1)}, bf16[128,96]{0,1:T(8,128)(2,1)}, u32[]{:S(2)}) copy-start(bf16[128,96]{0,1:T(8,128)(2,1)} %copy.213) | copy-start | bytes 73732
  254.4 4.9 %copy-start.30 = (bf16[128,96]{0,1:T(8,128)(2,1)S(1)}, bf16[128,96]{0,1:T(8,128)(2,1)}, u32[]{:S(2)}) copy-start(bf16[128,96]{0,1:T(8,128)(2,1)} %copy.215) | copy-start | bytes 73732
  258.9 2.8 copy-start.15
  259.3 3.0 %copy-start.33 = (f32[2,128]{1,0:T(2,128)}, f32[2,128]{1,0:T(2,128)S(1)}, u32[]{:S(2)}) copy-start(f32[2,128]{1,0:T(2,128)S(1)} %get-tuple-element.74) | copy-start | bytes 3076
  259.3 2.7 copy-start.29
  259.6 3.0 %copy-start.34 = (f32[2,128]{1,0:T(2,128)}, f32[2,128]{1,0:T(2,128)S(1)}, u32[]{:S(2)}) copy-start(f32[2,128]{1,0:T(2,128)S(1)} %get-tuple-element.76) | copy-start | bytes 3076
  259.7 2.7 copy-start.28
  260.8 1.9 copy-start.14
  261.9 1.8 copy-start.13
  262.3 2.1 copy-start.35
  262.3 1.7 copy-start.27
  262.7 2.1 copy-start.36
  262.7 1.7 copy-start.26
  263.0 1.9 copy-start.12
  264.1 1.9 copy-start.11
  264.4 0.7 copy-start.37
  264.4 1.8 copy-start.25
  264.8 1.4 copy-start.38
  264.8 2.3 copy-start.8
  264.8 2.3 copy-start.24
  265.9 4.5 %copy-start.10 = (bf16[768,96]{0,1:T(8,128)(2,1)S(1)}, bf16[768,96]{0,1:T(8,128)(2,1)}, u32[]{:S(2)}) copy-start(bf16[768,96]{0,1:T(8,128)(2,1)} %copy.234) | copy-start | bytes 442372
  266.2 0.9 copy-start.16
  266.2 5.8 %copy-start.9 = (bf16[768,96]{0,1:T(8,128)(2,1)S(1)}, bf16[768,96]{0,1:T(8,128)(2,1)}, u32[]{:S(2)}) copy-start(bf16[768,96]{0,1:T(8,128)(2,1)} %copy.235) | copy-start | bytes 442372
  267.1 7.1 %copy-start.32 = (f32[128,16]{0,1:T(8,128)S(1)}, f32[128,16]{0,1:T(8,128)}, u32[]{:S(2)}) copy-start(f32[128,16]{0,1:T(8,128)} %reshape.588) | copy-start | bytes 24580
  268.1 3.9 %copy-start.39 = (f32[2,128]{1,0:T(2,128)S(1)}, f32[2,128]{1,0:T(2,128)}, u32[]{:S(2)}) copy-start(f32[2,128]{1,0:T(2,128)} %get-tuple-element.88) | copy-start | bytes 3076
  268.1 7.3 %copy-start.2 = (f32[128,768]{0,1:T(8,128)S(1)}, f32[128,768]{0,1:T(8,128)}, u32[]{:S(2)}) copy-start(f32[128,768]{0,1:T(8,128)} %copy.202) | copy-start | bytes 1179652
where the time goes:
time: 278 us; the launch traced here: 276 us
  local copies, waits for them, and re-layouts  109 us (39%)
  blocking collectives  108 us (39%)
  other arithmetic  34.9 us (13%)
  matrix products  14.1 us (5%)
  starting transfers between devices  10.2 us (4%)
    gather x1, local copies, waits for them, and re-layouts, dilation_valid_mask(): tissue_keys = tissue[row_indices[:, None], key_columns]  65 us
    all_gather x1, blocking collectives, per_device(): lax.all_gather(key_selected, 'col', axis=1, tiled=True)  55.9 us
    all_gather x1, blocking collectives, per_device(): lax.all_gather(value_selected, 'col', axis=1, tiled=True)  51.7 us
    unnamed x107, local copies, waits for them, and re-layouts  21.9 us
    shift_left x1, other arithmetic, dilation_valid_mask(): jnp.left_shift(jnp.int32(DILATION_MIN), dilation_levels[head_indices])  10 us
    shift_right_arithmetic x1, other arithmetic, dilation_valid_mask(): jnp.right_shift(jnp.int32(column_total), segment_levels[head_indices])  10 us
    ppermute x2, starting transfers between devices, padded_2(): before = lax.ppermute(last, axis, up)  6.23 us
  transfers between devices with their start and end apart: 4, of which 0 were waited for; matrix products, arithmetic and copies ran while one was open for 43% of the time, Pallas kernels for 0%

commit v1 on v0

v1 whole, which is shorter than its diff:
```python
import math

import jax
import jax.numpy as jnp
from jax import lax
from jax.experimental import pallas as pl
from jax.experimental.pallas import tpu as pltpu
from jax.sharding import PartitionSpec as P

HEAD_COUNT = 16
R = 8
STEP = 8
NEG = -1e30
GROUPS = 4
GROUP_HEADS = HEAD_COUNT // GROUPS
WIN = 256
WIN_START = (0, 128, 384, 512)
LOG2E = 1.4426950408889634
STATS = 3


def iota(shape, dim):
    return lax.broadcasted_iota(jnp.int32, shape, dim)


def pack_kernel(q_ref, k_ref, v_ref, send_ref, right_ref, left_ref):
    rows, cols, width = q_ref.shape
    dh = width // HEAD_COUNT
    phase = (iota((STEP, width), 1) // dh) % STEP == iota((STEP, width), 0)
    sub = iota((STEP, width), 0)
    for i, ref in enumerate((k_ref, v_ref)):
        right_ref[i] = ref[:, cols - R :, :]
        left_ref[i] = ref[:, :R, :]
    for r in range(rows):
        tile = jnp.zeros((STEP, width), jnp.float32)
        for i, ref in enumerate((k_ref, v_ref)):
            for j in range(2):
                block = ref[r, j * STEP : (j + 1) * STEP, :].astype(jnp.float32)
                picked = jnp.sum(jnp.where(phase, block, 0.0), axis=0, keepdims=True)
                tile = jnp.where(sub == 2 * i + j, picked, tile)
        tile = tile.astype(jnp.bfloat16)
        for g in range(GROUPS):
            w0 = WIN_START[g]
            send_ref[r * GROUPS + g, :cols, :] = q_ref[r, :, w0 : w0 + WIN]
            send_ref[r * GROUPS + g, cols:, :] = tile[:, w0 : w0 + WIN]


def dilated_kernel(pos_ref, dil_ref, seg_ref, x_ref, tissue_ref, out_ref):
    peers, block_rows, _ = x_ref.shape
    cols = block_rows - STEP
    total_cols = peers * cols
    dh = 48
    group = pos_ref[2]
    odd = group % 2
    keys = peers * STEP
    log_cols = total_cols.bit_length() - 1
    q_all = x_ref[:, :cols, :].reshape(total_cols, WIN)
    kv = x_ref[:, cols:, :].reshape(keys, WIN)
    v_all = pltpu.roll(kv.astype(jnp.float32), keys - 2, 0).astype(jnp.bfloat16)
    lane = iota((1, WIN), 1)
    base = odd * 64
    row = tissue_ref[pl.ds(pos_ref[0], 1), :].astype(jnp.float32)
    row = jnp.broadcast_to(row, (STEP, total_cols)).astype(jnp.bfloat16)
    slot = iota((total_cols, GROUP_HEADS * keys), 1)
    slot_col = (
        ((slot % keys) // STEP) * cols
        + (slot % STEP) * STEP
        + (group * GROUP_HEADS + slot // keys) % STEP
    )
    pick = jnp.where(slot_col == iota((total_cols, GROUP_HEADS * keys), 0), 1.0, 0.0)
    slot_tissue = jnp.dot(row, pick.astype(jnp.bfloat16), preferred_element_type=jnp.float32)[:1]
    key_slot = iota((1, keys), 1)
    query_col = iota((total_cols, 1), 0)
    out = jnp.zeros((total_cols, WIN), jnp.float32)
    stat_base = jnp.where(odd == 1, 0, GROUP_HEADS * dh)
    for hh in range(GROUP_HEADS):
        head = group * GROUP_HEADS + hh
        key_col = (key_slot // STEP) * cols + (key_slot % STEP) * STEP + head % STEP
        period = jnp.left_shift(STEP, dil_ref[head]) - 1
        shift = log_cols - seg_ref[head]
        ok = (key_slot % STEP < 2) & ((key_col & period) == (head & period))
        ok = ok & (slot_tissue[:, hh * keys : (hh + 1) * keys] > 0.5)
        key_seg = jnp.where(ok, jnp.right_shift(key_col, shift), -1)
        mask = key_seg == jnp.right_shift(query_col, shift)
        mine = (lane >= base + hh * dh) & (lane < base + (hh + 1) * dh)
        q_head = jnp.where(mine, q_all, jnp.zeros((), jnp.bfloat16))
        s = lax.dot_general(
            q_head, kv, (((1,), (1,)), ((), ())), preferred_element_type=jnp.float32
        ) * (LOG2E / math.sqrt(dh))
        s = jnp.where(mask, s, NEG)
        top = jnp.max(s, axis=1, keepdims=True)
        p = jnp.where(mask, jnp.exp2(s - top), 0.0)
        total = jnp.sum(p, axis=1, keepdims=True)
        numer = jnp.dot(p.astype(jnp.bfloat16), v_all, preferred_element_type=jnp.float32)
        some = total > 0.0
        safe = jnp.where(some, total, 1.0)
        lse = jnp.where(some, top + jnp.log2(safe), NEG)
        out = jnp.where(mine, numer / safe, out)
        rest = lse
        for part in range(STATS):
            piece = rest.astype(jnp.bfloat16).astype(jnp.float32)
            rest = rest - piece
            out = jnp.where(lane == stat_base + part * GROUP_HEADS + hh, piece, out)
    out_ref[...] = out.astype(jnp.bfloat16).reshape(out_ref.shape)


def window_kernel(pos_ref, q_ref, up_ref, own_ref, down_ref, tissue_ref, out_ref, lse_ref, bias_ref, s_ref, p_ref):
    rows, cols, width = q_ref.shape
    queries = rows * cols
    dh = width // HEAD_COUNT
    wide = cols + 2 * R
    keys = rows * wide
    grid_rows, grid_cols = tissue_ref.shape
    row0, col0 = pos_ref[0], pos_ref[1]
    q_id = iota((queries, keys), 0)
    k_id = iota((queries, keys), 1)
    q_row, q_col = q_id // cols, q_id % cols
    k_row, k_col = k_id // wide, k_id % wide - R
    near_cols = jnp.abs(k_col - q_col) <= R
    spread = jnp.where(iota((grid_cols, keys), 0) == col0 - R + iota((grid_cols, keys), 1) % wide, 1.0, 0.0)
    spread = spread.astype(jnp.bfloat16)
    for b in range(3):
        first = row0 + (b - 1) * rows
        inside = (first >= 0) & (first < grid_rows)
        at = pl.multiple_of(jnp.clip(first, 0, grid_rows - rows), rows)
        tiles = tissue_ref[pl.ds(at, rows), :].astype(jnp.float32).astype(jnp.bfloat16)
        by_row = jnp.dot(tiles, spread, preferred_element_type=jnp.float32)
        mine = iota((rows, keys), 1) // wide == iota((rows, keys), 0)
        flat = jnp.sum(jnp.where(mine, by_row, 0.0), axis=0, keepdims=True)
        live = (flat > 0.5) & inside
        ok = near_cols & (jnp.abs(k_row + (b - 1) * rows - q_row) <= R) & live
        if b == 1:
            ok = ok | ((k_row == q_row) & (k_col == q_col))
        bias_ref[:, b * keys : (b + 1) * keys] = jnp.where(ok, 0.0, NEG)
    lane = iota((1, WIN), 1)
    chunk = 64
    for g in range(GROUPS):
        w0 = WIN_START[g]
        off = g * GROUP_HEADS * dh - w0
        q_win = q_ref[:, :, w0 : w0 + WIN].reshape(queries, WIN)
        stack = []
        for hh in range(GROUP_HEADS):
            mine = (lane >= off + hh * dh) & (lane < off + (hh + 1) * dh)
            stack.append(jnp.where(mine, q_win, jnp.zeros((), jnp.bfloat16)))
        stack = jnp.concatenate(stack, axis=0)
        for b, ref in enumerate((up_ref, own_ref, down_ref)):
            k_win = ref[0, :, :, w0 : w0 + WIN].reshape(keys, WIN)
            s_ref[:, b * keys : (b + 1) * keys] = lax.dot_general(
                stack, k_win, (((1,), (1,)), ((), ())), preferred_element_type=jnp.float32
            )
        tops, totals = [], []
        for c0 in range(0, GROUP_HEADS * queries, chunk):
            b0 = c0 % queries
            s = s_ref[c0 : c0 + chunk, :] * (LOG2E / math.sqrt(dh)) + bias_ref[b0 : b0 + chunk, :]
            top = jnp.max(s, axis=1, keepdims=True)
            p = jnp.exp2(s - top)
            tops.append(top)
            totals.append(jnp.sum(p, axis=1, keepdims=True))
            p_ref[c0 : c0 + chunk, :] = p.astype(jnp.bfloat16)
        numer = jnp.zeros((GROUP_HEADS * queries, WIN), jnp.float32)
        for b, ref in enumerate((up_ref, own_ref, down_ref)):
            v_win = ref[1, :, :, w0 : w0 + WIN].reshape(keys, WIN)
            numer += jnp.dot(
                p_ref[:, b * keys : (b + 1) * keys], v_win, preferred_element_type=jnp.float32
            )
        top = jnp.concatenate(tops, axis=0)
        total = jnp.concatenate(totals, axis=0)
        numer = numer / total
        lse = top + jnp.log2(total)
        out = jnp.zeros((queries, WIN), jnp.float32)
        lse_wide = jnp.zeros((queries, WIN), jnp.float32)
        for hh in range(GROUP_HEADS):
            mine = (lane >= off + hh * dh) & (lane < off + (hh + 1) * dh)
            at = slice(hh * queries, (hh + 1) * queries)
            out = jnp.where(mine, numer[at], out)
            lse_wide = jnp.where(mine, lse[at], lse_wide)
        out_ref[:, g * WIN : (g + 1) * WIN] = out
        lse_ref[:, g * WIN : (g + 1) * WIN] = lse_wide


def merge_kernel(win_ref, lse_ref, back_ref, weight_ref, out_ref):
    rows, cols, width = out_ref.shape
    queries = rows * cols
    dh = width // HEAD_COUNT
    back = back_ref[...].reshape(rows, GROUPS, cols, WIN)
    src = iota((WIN, WIN), 0)
    dst = iota((WIN, WIN), 1)
    pieces = []
    for g in range(GROUPS):
        off = g * GROUP_HEADS * dh - WIN_START[g]
        stat_base = 0 if off else GROUP_HEADS * dh
        x = back[:, g].reshape(queries, WIN)
        stat = src - stat_base
        hit = (stat >= 0) & (stat < STATS * GROUP_HEADS) & (stat % GROUP_HEADS == (dst - off) // dh)
        hit = hit & (dst >= off) & (dst < off + GROUP_HEADS * dh)
        spread = jnp.where(hit, 1.0, 0.0).astype(jnp.bfloat16)
        lse_d = jnp.dot(x, spread, preferred_element_type=jnp.float32)
        lse_w = lse_ref[:, g * WIN : (g + 1) * WIN]
        big = jnp.maximum(lse_w, lse_d)
        a = jnp.exp2(lse_w - big)
        b = jnp.exp2(lse_d - big)
        mixed = a * win_ref[:, g * WIN : (g + 1) * WIN] + b * x.astype(jnp.float32)
        pieces.append(mixed / (a + b))
    low = iota((1, 128), 1) < 64
    att = jnp.concatenate(
        [
            pieces[0][:, :128],
            jnp.where(low, pieces[0][:, 128:], pieces[1][:, :128]),
            pieces[1][:, 128:],
            pieces[2][:, :128],
            jnp.where(low, pieces[2][:, 128:], pieces[3][:, :128]),
            pieces[3][:, 128:],
        ],
        axis=1,
    ).astype(jnp.bfloat16)
    enc = jnp.dot(att, weight_ref[...], preferred_element_type=jnp.float32)
    out_ref[...] = enc.astype(jnp.bfloat16).reshape(out_ref.shape)


def call(kernel, out_shape, scratch=(), scalars=0, inputs=0, flops=0, name=None):
    vmem = pl.BlockSpec(memory_space=pltpu.VMEM)
    smem = pl.BlockSpec(memory_space=pltpu.SMEM)
    many = isinstance(out_shape, (tuple, list))
    return pl.pallas_call(
        kernel,
        out_shape=out_shape,
        in_specs=[smem] * scalars + [vmem] * inputs,
        out_specs=[vmem] * len(out_shape) if many else vmem,
        scratch_shapes=list(scratch),
        cost_estimate=pl.CostEstimate(flops=flops, transcendentals=0, bytes_accessed=1 << 20),
        compiler_params=pltpu.CompilerParams(vmem_limit_bytes=48 << 20),
        name=name,
    )


def per_device(q, k, v, tissue, dilation_levels, segment_levels, weight):
    rows, cols, width = q.shape
    peers = lax.axis_size("col")
    n_row = lax.axis_size("row")
    bf16, f32 = jnp.bfloat16, jnp.float32
    me_row, me_col = lax.axis_index("row"), lax.axis_index("col")
    shape = jax.ShapeDtypeStruct
    half = shape((2, rows, R, width), bf16)
    send, right, left = call(
        pack_kernel,
        [shape((peers, cols + STEP, WIN), bf16), half, half],
        inputs=3,
        name="pack",
    )(q, k, v)
    got = lax.all_to_all(send, "col", 0, 0, tiled=True)
    up_c = [(i, i + 1) for i in range(peers - 1)]
    up_r = [(i, i + 1) for i in range(n_row - 1)]
    from_left = lax.ppermute(right, "col", up_c)
    from_right = lax.ppermute(left, "col", [(b, a) for a, b in up_c])
    own = jnp.concatenate([from_left, jnp.stack([k, v]), from_right], axis=2)
    above = lax.ppermute(own, "row", up_r)
    below = lax.ppermute(own, "row", [(b, a) for a, b in up_r])
    pos_d = jnp.stack([me_row * rows + me_col // GROUPS, me_col * cols, me_col % GROUPS])
    back = call(
        dilated_kernel,
        shape((peers, cols, WIN), bf16),
        scalars=3,
        inputs=2,
        flops=1 << 31,
        name="dilated",
    )(pos_d, dilation_levels, segment_levels, got, tissue)
    back = lax.all_to_all(back, "col", 0, 0, tiled=True)
    keys = rows * (cols + 2 * R)
    queries = rows * cols
    stack = GROUP_HEADS * queries
    win, lse = call(
        window_kernel,
        [shape((queries, GROUPS * WIN), f32)] * 2,
        scratch=[
            pltpu.VMEM((queries, 3 * keys), f32),
            pltpu.VMEM((stack, 3 * keys), f32),
            pltpu.VMEM((stack, 3 * keys), bf16),
        ],
        scalars=1,
        inputs=5,
        flops=1 << 32,
        name="window",
    )(jnp.stack([me_row * rows, me_col * cols]), q, above, own, below, tissue)
    return call(
        merge_kernel, shape((rows, cols, width), bf16), inputs=4, flops=1 << 28, name="merge"
    )(win, lse, back, weight)


def solution(mesh):
    spec = P("row", "col", None)
    return jax.shard_map(
        per_device,
        mesh=mesh,
        in_specs=(spec, spec, spec, P(), P(), P(), P()),
        out_specs=spec,
        check_vma=False,
    )
```

time: 278 us -> 60.3 us (0.22)
  the two profiles are of different devices: /device:TPU:56 before, /device:TPU:8 now
where the time goes in v1:
time: 60.3 us; the launch traced here: 59.8 us
  starting transfers between devices  28.5 us (47%)
  waiting for transfers between devices  14.4 us (24%)
  Pallas kernels  10.7 us (18%)
  local copies, waits for them, and re-layouts  5.81 us (10%)
    all_to_all x1, starting transfers between devices, per_device(): got = lax.all_to_all(send, 'col', 0, 0, tiled=True)  15.3 us
    all_to_all x1, waiting for transfers between devices, per_device(): got = lax.all_to_all(send, 'col', 0, 0, tiled=True)  10.3 us
    unnamed x26, local copies, waits for them, and re-layouts  5.81 us
    pallas_call x1, Pallas kernels, per_device(): call(window_kernel, [shape((queries, GROUPS * WIN), f32)] * 2, scratch=[p...  5.01 us
    all_to_all x1, starting transfers between devices, per_device(): back = lax.all_to_all(back, 'col', 0, 0, tiled=True)  4.16 us
    all_to_all x1, waiting for transfers between devices, per_device(): back = lax.all_to_all(back, 'col', 0, 0, tiled=True)  4.11 us
    ppermute x1, starting transfers between devices, per_device(): from_left = lax.ppermute(right, 'col', up_c)  3.39 us
    pallas_call x1, Pallas kernels, per_device(): call(dilated_kernel, shape((peers, cols, WIN), bf16), scalars=3, inputs=2...  3.36 us
  transfers between devices with their start and end apart: 6, of which 2 were waited for; matrix products, arithmetic and copies ran while one was open for 0% of the time, Pallas kernels for 14%

profile of v1, /device:TPU:8, one launch (start us, length us, event | category | flops | bytes accessed | tf_op | source)
XLA Modules:
  0.0 59.8 jit_solution(4844714478355902464)
XLA Ops:
  0.0 0.0 copy-start.1
  0.0 0.9 %copy-done.1 = bf16[8,16,768]{2,1,0:T(8,128)(2,1)S(1)} copy-done((bf16[8,16,768]{2,1,0:T(8,128)(2,1)S(1)}, bf16[8,16,768]{2,1,0:T(8,128)(2,1)}, u32[]{:S(2)}) %copy-start.1) | copy-done | bytes 196632
  0.9 0.0 copy-start.3
  0.9 0.9 %copy-done.3 = bf16[8,16,768]{2,1,0:T(8,128)(2,1)S(1)} copy-done((bf16[8,16,768]{2,1,0:T(8,128)(2,1)S(1)}, bf16[8,16,768]{2,1,0:T(8,128)(2,1)}, u32[]{:S(2)}) %copy-start.3) | copy-done | bytes 196632
  1.9 0.0 copy-start.5
  1.9 0.9 %copy-done.5 = bf16[8,16,768]{2,1,0:T(8,128)(2,1)S(1)} copy-done((bf16[8,16,768]{2,1,0:T(8,128)(2,1)S(1)}, bf16[8,16,768]{2,1,0:T(8,128)(2,1)}, u32[]{:S(2)}) %copy-start.5) | copy-done | bytes 196632
  2.8 0.0 copy-start.2
  2.8 0.0 copy-start.4
  2.8 1.0 %pack.1 = (bf16[32,24,256]{2,1,0:T(8,128)(2,1)}, bf16[2,8,8,768]{3,2,1,0:T(8,128)(2,1)S(1)}, bf16[2,8,8,768]{3,2,1,0:T(8,128)(2,1)S(1)}) custom-call(bf16[8,16,768]{2,1,0:T(8,128)(2,1)S(1)} %copy-done.5, bf16[8,16,768]{2,1,0:T(8,128)(2,1)S(1)} %copy-done.1, bf16[8,16,768]{2,1,0:T(8,128)(2,1)S(1)} %copy-done.3), custom_call_target="tpu_custom_call" | custom-call | bytes 1048576 | tf_op jit(solution)/shard_map/pack/pallas_call | solution.py:244
  3.8 3.4 %collective-permute-start = (bf16[2,8,8,768]{3,2,1,0:T(8,128)(2,1)S(1)}, bf16[2,8,8,768]{3,2,1,0:T(8,128)(2,1)S(1)}, u32[]{:S(2)}, u32[]{:S(2)}) collective-permute-start(bf16[2,8,8,768]{3,2,1,0:T(8,128)(2,1)S(1)} %get-tuple-element.10), channel_id=1, source_target_pairs={{0,1},{1,2},{2,3},{3,4},{4,5},{5,6},{6,7},{7,8},{8,9},{9,10},{10,1... | collective-permute-start | bytes 589832 | tf_op jit(solution)/shard_map/ppermute | solution.py:253
  7.2 1.3 %collective-permute-start.1 = (bf16[2,8,8,768]{3,2,1,0:T(8,128)(2,1)S(1)}, bf16[2,8,8,768]{3,2,1,0:T(8,128)(2,1)S(1)}, u32[]{:S(2)}, u32[]{:S(2)}) collective-permute-start(bf16[2,8,8,768]{3,2,1,0:T(8,128)(2,1)S(1)} %get-tuple-element.11), channel_id=1, source_target_pairs={{1,0},{2,1},{3,2},{4,3},{5,4},{6,5},{7,6},{8,7},{9,8},{10,9},{11,1... | collective-permute-start | bytes 589832 | tf_op jit(solution)/shard_map/ppermute | solution.py:254
  8.5 0.0 copy-start.9
  8.5 0.0 copy-start.11
  8.5 0.0 copy-start.12
  8.5 15.3 %all-to-all-start = ((bf16[32,24,256]{2,1,0:T(8,128)(2,1)}), bf16[32,24,256]{2,1,0:T(8,128)(2,1)S(1)}, u32[]{:S(2)}, u32[]{:S(2)}) async-start(bf16[32,24,256]{2,1,0:T(8,128)(2,1)} %get-tuple-element.14), calls=%async_computation | async-start | bytes 786432 | tf_op jit(solution)/shard_map/all_to_all | solution.py:250
  23.8 0.0 collective-permute-done
  23.8 0.0 collective-permute-done.1
  23.9 0.0 copy-done.2
  23.9 0.0 copy-done.4
  23.9 0.1 pad_maximum_fusion.own_ref
  24.0 1.9 %collective-permute-start.3 = (bf16[2,8,32,768]{3,2,1,0:T(8,128)(2,1)S(1)}, bf16[2,8,32,768]{3,2,1,0:T(8,128)(2,1)S(1)}, u32[]{:S(2)}, u32[]{:S(2)}) collective-permute-start(bf16[2,8,32,768]{3,2,1,0:T(8,128)(2,1)S(1)} %pad_maximum_fusion.own_ref), channel_id=1, source_target_pairs={{32,0},{64,32},{96,64},{128,96},{160,128},{192,160},{224,192},{256... | collective-permute-start | bytes 2359304 | tf_op jit(solution)/shard_map/ppermute | solution.py:257
  25.9 2.4 %collective-permute-start.2 = (bf16[2,8,32,768]{3,2,1,0:T(8,128)(2,1)S(1)}, bf16[2,8,32,768]{3,2,1,0:T(8,128)(2,1)}, u32[]{:S(2)}, u32[]{:S(2)}) collective-permute-start(bf16[2,8,32,768]{3,2,1,0:T(8,128)(2,1)S(1)} %pad_maximum_fusion.own_ref), channel_id=1, source_target_pairs={{0,32},{32,64},{64,96},{96,128},{128,160},{160,192},{192,224},{224... | collective-permute-start | bytes 2359304 | tf_op jit(solution)/shard_map/ppermute | solution.py:256
  28.3 0.1 pad_add_fusion.1.pos_ref
  28.4 0.0 copy-start.6
  28.4 10.3 %all-to-all-done.x_ref = bf16[32,24,256]{2,1,0:T(8,128)(2,1)S(1)} async-done(((bf16[32,24,256]{2,1,0:T(8,128)(2,1)}), bf16[32,24,256]{2,1,0:T(8,128)(2,1)S(1)}, u32[]{:S(2)}, u32[]{:S(2)}) %all-to-all-start) | async-done | bytes 393248 | tf_op jit(solution)/shard_map/all_to_all | solution.py:250
  38.7 0.0 copy-done.9
  38.7 0.0 copy-done.11
  38.7 0.0 copy-done.12
  38.7 3.4 %dilated.1 = bf16[32,16,256]{2,1,0:T(8,128)(2,1)} custom-call(s32[3]{0:T(128)S(1)} %pad_add_fusion.1.pos_ref, s32[16]{0:T(128)S(1)} %copy-done.11, s32[16]{0:T(128)S(1)} %copy-done.12, bf16[32,24,256]{2,1,0:T(8,128)(2,1)S(1)} %all-to-all-done.x_ref, s32[128,512]{1,0:T(8,128)S(1)} %copy-done.9), custom_call_target="tpu_custom_call" | custom-call | flops 2147483648 | bytes 1048576 | tf_op jit(solution)/shard_map/dilated/pallas_call | solution.py:259
  42.1 4.2 %all-to-all-start.1 = ((bf16[32,16,256]{2,1,0:T(8,128)(2,1)}), bf16[32,16,256]{2,1,0:T(8,128)(2,1)S(1)}, u32[]{:S(2)}, u32[]{:S(2)}) async-start(bf16[32,16,256]{2,1,0:T(8,128)(2,1)} %dilated.1), calls=%async_computation.1 | async-start | bytes 524288 | tf_op jit(solution)/shard_map/all_to_all | solution.py:267
  46.2 0.1 pad_add_fusion.pos_ref
  46.3 0.0 copy-start
  46.3 0.0 collective-permute-done.3.down_ref
  46.3 0.0 copy-start.7
  46.3 0.9 %copy-done.7 = bf16[2,8,32,768]{3,2,1,0:T(8,128)(2,1)} copy-done((bf16[2,8,32,768]{3,2,1,0:T(8,128)(2,1)}, bf16[2,8,32,768]{3,2,1,0:T(8,128)(2,1)S(1)}, u32[]{:S(2)}) %copy-start.7) | copy-done | bytes 786456
  47.2 0.0 collective-permute-done.2.up_ref
  47.2 0.0 copy-done.6
  47.2 0.0 copy-start.8
  47.2 1.1 %copy-done.8 = bf16[2,8,32,768]{3,2,1,0:T(8,128)(2,1)S(1)} copy-done((bf16[2,8,32,768]{3,2,1,0:T(8,128)(2,1)S(1)}, bf16[2,8,32,768]{3,2,1,0:T(8,128)(2,1)}, u32[]{:S(2)}) %copy-start.8) | copy-done | bytes 786456
  48.4 0.0 copy-start.10
  48.4 0.9 %copy-done.10 = s32[128,512]{1,0:T(8,128)S(1)} copy-done((s32[128,512]{1,0:T(8,128)S(1)}, s32[128,512]{1,0:T(8,128)}, u32[]{:S(2)}) %copy-start.10) | copy-done | bytes 262168
  49.3 5.0 %window.1 = (f32[128,1024]{1,0:T(8,128)S(1)}, f32[128,1024]{1,0:T(8,128)S(1)}) custom-call(s32[2]{0:T(128)S(1)} %pad_add_fusion.pos_ref, bf16[8,16,768]{2,1,0:T(8,128)(2,1)S(1)} %copy-done.6, bf16[2,8,32,768]{3,2,1,0:T(8,128)(2,1)} %collective-permute-done.2.up_ref, bf16[2,8,32,768]{3,2,1,0:T(8,128)(2,1)S(1)} %pad_maximum_fusion.own_ref, ...), custom_call_target="tpu_custom_call" | custom-call | flops 4294967296 | bytes 1048576 | tf_op jit(solution)/shard_map/window/pallas_call | solution.py:271
  54.3 4.1 %all-to-all-done.1.back_ref = bf16[32,16,256]{2,1,0:T(8,128)(2,1)S(1)} async-done(((bf16[32,16,256]{2,1,0:T(8,128)(2,1)}), bf16[32,16,256]{2,1,0:T(8,128)(2,1)S(1)}, u32[]{:S(2)}, u32[]{:S(2)}) %all-to-all-start.1) | async-done | bytes 262176 | tf_op jit(solution)/shard_map/all_to_all | solution.py:267
  58.4 0.0 copy-done
  58.4 1.3 %merge.1 = bf16[8,16,768]{2,1,0:T(8,128)(2,1)} custom-call(f32[128,1024]{1,0:T(8,128)S(1)} %get-tuple-element.12.win_ref, f32[128,1024]{1,0:T(8,128)S(1)} %get-tuple-element.13.lse_ref, bf16[32,16,256]{2,1,0:T(8,128)(2,1)S(1)} %all-to-all-done.1.back_ref, bf16[768,768]{1,0:T(8,128)(2,1)S(1)} %copy-done), custom_call_target="tpu_custom_call" | custom-call | flops 268435456 | bytes 1048576 | tf_op jit(solution)/shard_map/merge/pallas_call | solution.py:284
Async XLA Ops:
  0.0 0.9 %copy-start.1 = (bf16[8,16,768]{2,1,0:T(8,128)(2,1)S(1)}, bf16[8,16,768]{2,1,0:T(8,128)(2,1)}, u32[]{:S(2)}) copy-start(bf16[8,16,768]{2,1,0:T(8,128)(2,1)} %k_ref.1) | copy-start | bytes 589828
  0.9 0.9 %copy-start.3 = (bf16[8,16,768]{2,1,0:T(8,128)(2,1)S(1)}, bf16[8,16,768]{2,1,0:T(8,128)(2,1)}, u32[]{:S(2)}) copy-start(bf16[8,16,768]{2,1,0:T(8,128)(2,1)} %v_ref.1) | copy-start | bytes 589828
  1.9 0.9 %copy-start.5 = (bf16[8,16,768]{2,1,0:T(8,128)(2,1)S(1)}, bf16[8,16,768]{2,1,0:T(8,128)(2,1)}, u32[]{:S(2)}) copy-start(bf16[8,16,768]{2,1,0:T(8,128)(2,1)} %q_ref.3) | copy-start | bytes 589828
  2.8 21.1 %copy-start.2 = (bf16[8,16,768]{2,1,0:T(8,128)(2,1)S(1)}, bf16[8,16,768]{2,1,0:T(8,128)(2,1)}, u32[]{:S(2)}) copy-start(bf16[8,16,768]{2,1,0:T(8,128)(2,1)} %k_ref.1) | copy-start | bytes 589828
  2.8 21.1 %copy-start.4 = (bf16[8,16,768]{2,1,0:T(8,128)(2,1)S(1)}, bf16[8,16,768]{2,1,0:T(8,128)(2,1)}, u32[]{:S(2)}) copy-start(bf16[8,16,768]{2,1,0:T(8,128)(2,1)} %v_ref.1) | copy-start | bytes 589828
  3.8 20.0 %collective-permute-start = (bf16[2,8,8,768]{3,2,1,0:T(8,128)(2,1)S(1)}, bf16[2,8,8,768]{3,2,1,0:T(8,128)(2,1)S(1)}, u32[]{:S(2)}, u32[]{:S(2)}) collective-permute-start(bf16[2,8,8,768]{3,2,1,0:T(8,128)(2,1)S(1)} %get-tuple-element.10), channel_id=1, source_target_pairs={{0,1},{1,2},{2,3},{3,4},{4,5},{5,6},{6,7},{7,8},{8,9},{9,10},{10,1... | collective-permute-start | bytes 589832 | tf_op jit(solution)/shard_map/ppermute | solution.py:253
  7.2 16.6 %collective-permute-start.1 = (bf16[2,8,8,768]{3,2,1,0:T(8,128)(2,1)S(1)}, bf16[2,8,8,768]{3,2,1,0:T(8,128)(2,1)S(1)}, u32[]{:S(2)}, u32[]{:S(2)}) collective-permute-start(bf16[2,8,8,768]{3,2,1,0:T(8,128)(2,1)S(1)} %get-tuple-element.11), channel_id=1, source_target_pairs={{1,0},{2,1},{3,2},{4,3},{5,4},{6,5},{7,6},{8,7},{9,8},{10,9},{11,1... | collective-permute-start | bytes 589832 | tf_op jit(solution)/shard_map/ppermute | solution.py:254
  8.5 30.2 %copy-start.9 = (s32[128,512]{1,0:T(8,128)S(1)}, s32[128,512]{1,0:T(8,128)}, u32[]{:S(2)}) copy-start(s32[128,512]{1,0:T(8,128)} %tissue_ref.3) | copy-start | bytes 786436
  8.5 30.2 %copy-start.11 = (s32[16]{0:T(128)S(1)}, s32[16]{0:T(128)}, u32[]{:S(2)}) copy-start(s32[16]{0:T(128)} %dil_ref.1) | copy-start | bytes 196
  8.5 30.2 %copy-start.12 = (s32[16]{0:T(128)S(1)}, s32[16]{0:T(128)}, u32[]{:S(2)}) copy-start(s32[16]{0:T(128)} %seg_ref.1) | copy-start | bytes 196
  8.5 30.1 %all-to-all-start = ((bf16[32,24,256]{2,1,0:T(8,128)(2,1)}), bf16[32,24,256]{2,1,0:T(8,128)(2,1)S(1)}, u32[]{:S(2)}, u32[]{:S(2)}) async-start(bf16[32,24,256]{2,1,0:T(8,128)(2,1)} %get-tuple-element.14), calls=%async_computation | async-start | bytes 786432 | tf_op jit(solution)/shard_map/all_to_all | solution.py:250
  24.0 22.4 %collective-permute-start.3 = (bf16[2,8,32,768]{3,2,1,0:T(8,128)(2,1)S(1)}, bf16[2,8,32,768]{3,2,1,0:T(8,128)(2,1)S(1)}, u32[]{:S(2)}, u32[]{:S(2)}) collective-permute-start(bf16[2,8,32,768]{3,2,1,0:T(8,128)(2,1)S(1)} %pad_maximum_fusion.own_ref), channel_id=1, source_target_pairs={{32,0},{64,32},{96,64},{128,96},{160,128},{192,160},{224,192},{256... | collective-permute-start | bytes 2359304 | tf_op jit(solution)/shard_map/ppermute | solution.py:257
  25.9 21.3 %collective-permute-start.2 = (bf16[2,8,32,768]{3,2,1,0:T(8,128)(2,1)S(1)}, bf16[2,8,32,768]{3,2,1,0:T(8,128)(2,1)}, u32[]{:S(2)}, u32[]{:S(2)}) collective-permute-start(bf16[2,8,32,768]{3,2,1,0:T(8,128)(2,1)S(1)} %pad_maximum_fusion.own_ref), channel_id=1, source_target_pairs={{0,32},{32,64},{64,96},{96,128},{128,160},{160,192},{192,224},{224... | collective-permute-start | bytes 2359304 | tf_op jit(solution)/shard_map/ppermute | solution.py:256
  28.4 18.8 %copy-start.6 = (bf16[8,16,768]{2,1,0:T(8,128)(2,1)S(1)}, bf16[8,16,768]{2,1,0:T(8,128)(2,1)}, u32[]{:S(2)}) copy-start(bf16[8,16,768]{2,1,0:T(8,128)(2,1)} %q_ref.3) | copy-start | bytes 589828
  42.1 16.4 %all-to-all-start.1 = ((bf16[32,16,256]{2,1,0:T(8,128)(2,1)}), bf16[32,16,256]{2,1,0:T(8,128)(2,1)S(1)}, u32[]{:S(2)}, u32[]{:S(2)}) async-start(bf16[32,16,256]{2,1,0:T(8,128)(2,1)} %dilated.1), calls=%async_computation.1 | async-start | bytes 524288 | tf_op jit(solution)/shard_map/all_to_all | solution.py:267
  46.3 12.1 %copy-start = (bf16[768,768]{1,0:T(8,128)(2,1)S(1)}, bf16[768,768]{1,0:T(8,128)(2,1)}, u32[]{:S(2)}) copy-start(bf16[768,768]{1,0:T(8,128)(2,1)} %weight_ref.1) | copy-start | bytes 3538948
  46.3 0.9 %copy-start.7 = (bf16[2,8,32,768]{3,2,1,0:T(8,128)(2,1)}, bf16[2,8,32,768]{3,2,1,0:T(8,128)(2,1)S(1)}, u32[]{:S(2)}) copy-start(bf16[2,8,32,768]{3,2,1,0:T(8,128)(2,1)S(1)} %collective-permute-done.3.down_ref) | copy-start | bytes 2359300
  47.2 1.1 %copy-start.8 = (bf16[2,8,32,768]{3,2,1,0:T(8,128)(2,1)S(1)}, bf16[2,8,32,768]{3,2,1,0:T(8,128)(2,1)}, u32[]{:S(2)}) copy-start(bf16[2,8,32,768]{3,2,1,0:T(8,128)(2,1)} %copy-done.7) | copy-start | bytes 2359300
  48.4 0.9 %copy-start.10 = (s32[128,512]{1,0:T(8,128)S(1)}, s32[128,512]{1,0:T(8,128)}, u32[]{:S(2)}) copy-start(s32[128,512]{1,0:T(8,128)} %tissue_ref.3) | copy-start | bytes 786436

commit v2 on v1

v2 whole, which is shorter than its diff:
```python
import math

import jax
import jax.numpy as jnp
from jax import lax
from jax.experimental import pallas as pl
from jax.experimental.pallas import tpu as pltpu
from jax.sharding import PartitionSpec as P

HEAD_COUNT = 16
R = 8
STEP = 8
NEG = -1e30
GROUPS = 4
GROUP_HEADS = HEAD_COUNT // GROUPS
WIN = 256
WIN_START = (0, 128, 384, 512)
LOG2E = 1.4426950408889634
STATS = 3


def iota(shape, dim):
    return lax.broadcasted_iota(jnp.int32, shape, dim)


def canonical(x, g):
    full = 3 * (g // 2) + 2 * (g % 2)
    half = 3 * (g // 2) + 1
    return x[:, full * 128 : (full + 1) * 128], x[:, half * 128 : (half + 1) * 128]


def pack_kernel(
    dil_ref, seg_ref, q_hbm, k_hbm, v_hbm, t_hbm, send_ref, right_ref, left_ref, keyseg_ref,
    q_ref, k_ref, v_ref, t_ref, sem,
):
    rows, cols, width = q_ref.shape
    total_cols = t_ref.shape[1]
    dh = width // HEAD_COUNT
    keys = total_cols // cols * STEP
    row0 = pl.multiple_of(lax.axis_index("row") * rows, rows)
    me_col = lax.axis_index("col")
    copies = [
        pltpu.make_async_copy(t_hbm.at[pl.ds(row0, rows), :], t_ref, sem.at[0]),
        pltpu.make_async_copy(k_hbm, k_ref, sem.at[1]),
        pltpu.make_async_copy(v_hbm, v_ref, sem.at[2]),
        pltpu.make_async_copy(q_hbm, q_ref, sem.at[3]),
    ]
    for copy in copies:
        copy.start()
    slot = iota((total_cols, keys), 1)
    pick = (iota((total_cols, keys), 0) == (slot // STEP) * cols + (slot % STEP) * STEP) & (slot % STEP < 2)
    pick = jnp.where(pick, 1.0, 0.0).astype(jnp.bfloat16)
    group = me_col % GROUPS
    sub = iota((STEP, total_cols), 0)
    copies[0].wait()
    tissue = jnp.sum(
        jnp.where(sub == me_col // GROUPS, t_ref[...].astype(jnp.float32), 0.0), axis=0, keepdims=True
    )
    tissue = jnp.broadcast_to(tissue, (STEP, total_cols))
    for bit in range(3):
        shifted = pltpu.roll(tissue, total_cols - (1 << bit), 1)
        tissue = jnp.where(((group * GROUP_HEADS + sub) >> bit) & 1 == 1, shifted, tissue)
    slot_tissue = jnp.dot(tissue.astype(jnp.bfloat16), pick, preferred_element_type=jnp.float32)
    key_slot = iota((1, keys), 1)
    for hh in range(GROUP_HEADS):
        head = group * GROUP_HEADS + hh
        key_col = (key_slot // STEP) * cols + (key_slot % STEP) * STEP + head % STEP
        period = jnp.left_shift(STEP, dil_ref[head]) - 1
        ok = (key_slot % STEP < 2) & ((key_col & period) == (head & period))
        ok = ok & (slot_tissue[hh : hh + 1] > 0.5)
        shift = total_cols.bit_length() - 1 - seg_ref[head]
        keyseg_ref[hh : hh + 1, :] = jnp.where(ok, jnp.right_shift(key_col, shift), -1)
    phase = (iota((STEP, width), 1) // dh) % STEP == iota((STEP, width), 0)
    sub = iota((STEP, width), 0)
    copies[1].wait()
    copies[2].wait()
    tiles = []
    for i, ref in enumerate((k_ref, v_ref)):
        right_ref[i] = ref[:, cols - R :, :]
        left_ref[i] = ref[:, :R, :]
    for r in range(rows):
        tile = jnp.zeros((STEP, width), jnp.float32)
        for i, ref in enumerate((k_ref, v_ref)):
            for j in range(2):
                block = ref[r, j * STEP : (j + 1) * STEP, :].astype(jnp.float32)
                picked = jnp.sum(jnp.where(phase, block, 0.0), axis=0, keepdims=True)
                tile = jnp.where(sub % 4 == 2 * i + j, picked, tile)
        tiles.append(tile)
    copies[3].wait()
    top = iota((STEP, 128), 0) < 4
    low = iota((STEP, 128), 1) < 64
    for r in range(rows):
        for g in range(GROUPS):
            d = r * GROUPS + g
            full, half = canonical(tiles[r], g)
            half = jnp.where(low, pltpu.roll(half, 64, 1) if g % 2 else half, 0.0)
            send_ref[d, 3 * STEP :, :] = jnp.where(top, full, half).astype(jnp.bfloat16)
            full, half = canonical(q_ref[r], g)
            send_ref[d, : 2 * STEP, :] = full
            half = half.astype(jnp.float32)
            first, second = half[:STEP], half[STEP:]
            if g % 2:
                first = pltpu.roll(first, 64, 1)
            else:
                second = pltpu.roll(second, 64, 1)
            send_ref[d, 2 * STEP : 3 * STEP, :] = jnp.where(low, first, second).astype(jnp.bfloat16)


def dilated_kernel(pos_ref, seg_ref, x_ref, keyseg_ref, out_ref, s_ref, p_ref):
    peers = x_ref.shape[0]
    cols = out_ref.shape[1]
    total_cols = peers * cols
    dh = 48
    group = pos_ref[0]
    odd = group % 2
    keys = peers * STEP
    log_cols = total_cols.bit_length() - 1
    low = iota((1, 128), 1) < 64
    zero = jnp.zeros((), jnp.bfloat16)
    q_full = x_ref[:, : 2 * STEP, :].reshape(total_cols, 128)
    packed = x_ref[:, 2 * STEP : 3 * STEP, :].astype(jnp.float32)
    other = pltpu.roll(packed.reshape(peers * STEP, 128), 64, 1).reshape(peers, STEP, 128)
    q_half = jnp.concatenate([packed, other], axis=1).reshape(total_cols, 128)
    q_all = jnp.concatenate([q_full, q_half.astype(jnp.bfloat16)], axis=1)
    kv = x_ref[:, 3 * STEP :, :].astype(jnp.float32).reshape(keys, 128)
    kv2 = pltpu.roll(kv, keys - 2, 0)
    kv4 = pltpu.roll(kv, keys - 4, 0)
    kv6 = pltpu.roll(kv, keys - 6, 0)
    k_all = jnp.concatenate([kv, kv4], axis=1).astype(jnp.bfloat16)
    v_all = jnp.concatenate([kv2, kv6], axis=1).astype(jnp.bfloat16)
    lane = iota((1, WIN), 1)
    place = jnp.where(odd == 1, jnp.where(lane < 128, lane + 64, lane - 128), lane)
    chunk = 128
    out = jnp.zeros((total_cols, WIN), jnp.float32)
    stat = jnp.zeros((total_cols, 128), jnp.float32)
    stat_lane = iota((1, 128), 1)
    for hh in range(GROUP_HEADS):
        mine = (place >= hh * dh) & (place < (hh + 1) * dh) & (lane < 192)
        s_ref[hh * total_cols : (hh + 1) * total_cols, :] = lax.dot_general(
            jnp.where(mine, q_all, zero), k_all, (((1,), (1,)), ((), ())), preferred_element_type=jnp.float32
        )
    for hh in range(GROUP_HEADS):
        mine = (place >= hh * dh) & (place < (hh + 1) * dh) & (lane < 192)
        shift = log_cols - seg_ref[group * GROUP_HEADS + hh]
        keyseg = keyseg_ref[hh : hh + 1, :]
        tops, totals = [], []
        for c0 in range(0, total_cols, chunk):
            bias = jnp.where(keyseg == jnp.right_shift(c0, shift), 0.0, NEG)
            at = slice(hh * total_cols + c0, hh * total_cols + c0 + chunk)
            s = s_ref[at, :] * (LOG2E / math.sqrt(dh)) + bias
            top = jnp.maximum(jnp.max(s, axis=1, keepdims=True), 0.5 * NEG)
            p = jnp.exp2(s - top)
            tops.append(top)
            totals.append(jnp.sum(p, axis=1, keepdims=True))
            p_ref[c0 : c0 + chunk, :] = p.astype(jnp.bfloat16)
        numer = jnp.dot(p_ref[...], v_all, preferred_element_type=jnp.float32)
        total = jnp.concatenate(totals, axis=0)
        safe = jnp.maximum(total, 0.5)
        lse = jnp.where(total > 0.0, jnp.concatenate(tops, axis=0) + jnp.log2(safe), NEG)
        out = jnp.where(mine, numer * (1.0 / safe), out)
        stat = jnp.where(stat_lane % GROUP_HEADS == hh, lse, stat)
    first = stat.astype(jnp.bfloat16).astype(jnp.float32)
    second = (stat - first).astype(jnp.bfloat16).astype(jnp.float32)
    third = stat - first - second
    part = (stat_lane - 64) // GROUP_HEADS
    stat = jnp.where(part == 0, first, jnp.where(part == 1, second, third))
    stat = jnp.where(part < STATS, stat, 0.0)
    out = jnp.concatenate([out[:, :128], jnp.where(low, out[:, 128:], stat)], axis=1)
    out_ref[...] = out.astype(jnp.bfloat16).reshape(out_ref.shape)


def window_kernel(q_ref, up_ref, own_ref, down_ref, tissue_ref, out_ref, lse_ref, bias_ref, s_ref, p_ref):
    rows, cols, width = q_ref.shape
    queries = rows * cols
    dh = width // HEAD_COUNT
    wide = cols + 2 * R
    keys = rows * wide
    grid_rows, grid_cols = tissue_ref.shape
    row0, col0 = lax.axis_index("row") * rows, lax.axis_index("col") * cols
    q_id = iota((queries, keys), 0)
    k_id = iota((queries, keys), 1)
    q_row, q_col = q_id // cols, q_id % cols
    k_row, k_col = k_id // wide, k_id % wide - R
    near_cols = jnp.abs(k_col - q_col) <= R
    spread = jnp.where(iota((grid_cols, keys), 0) == col0 - R + iota((grid_cols, keys), 1) % wide, 1.0, 0.0)
    spread = spread.astype(jnp.bfloat16)
    for b in range(3):
        first = row0 + (b - 1) * rows
        inside = (first >= 0) & (first < grid_rows)
        at = pl.multiple_of(jnp.clip(first, 0, grid_rows - rows), rows)
        tiles = tissue_ref[pl.ds(at, rows), :].astype(jnp.float32).astype(jnp.bfloat16)
        by_row = jnp.dot(tiles, spread, preferred_element_type=jnp.float32)
        mine = iota((rows, keys), 1) // wide == iota((rows, keys), 0)
        flat = jnp.sum(jnp.where(mine, by_row, 0.0), axis=0, keepdims=True)
        live = (flat > 0.5) & inside
        ok = near_cols & (jnp.abs(k_row + (b - 1) * rows - q_row) <= R) & live
        if b == 1:
            ok = ok | ((k_row == q_row) & (k_col == q_col))
        bias_ref[:, b * keys : (b + 1) * keys] = jnp.where(ok, 0.0, NEG)
    lane = iota((1, WIN), 1)
    chunk = 64
    for g in range(GROUPS):
        w0 = WIN_START[g]
        off = g * GROUP_HEADS * dh - w0
        q_win = q_ref[:, :, w0 : w0 + WIN].reshape(queries, WIN)
        stack = []
        for hh in range(GROUP_HEADS):
            mine = (lane >= off + hh * dh) & (lane < off + (hh + 1) * dh)
            stack.append(jnp.where(mine, q_win, jnp.zeros((), jnp.bfloat16)))
        stack = jnp.concatenate(stack, axis=0)
        for b, ref in enumerate((up_ref, own_ref, down_ref)):
            k_win = ref[0, :, :, w0 : w0 + WIN].reshape(keys, WIN)
            s_ref[:, b * keys : (b + 1) * keys] = lax.dot_general(
                stack, k_win, (((1,), (1,)), ((), ())), preferred_element_type=jnp.float32
            )
        tops, totals = [], []
        for c0 in range(0, GROUP_HEADS * queries, chunk):
            b0 = c0 % queries
            s = s_ref[c0 : c0 + chunk, :] * (LOG2E / math.sqrt(dh)) + bias_ref[b0 : b0 + chunk, :]
            top = jnp.max(s, axis=1, keepdims=True)
            p = jnp.exp2(s - top)
            tops.append(top)
            totals.append(jnp.sum(p, axis=1, keepdims=True))
            p_ref[c0 : c0 + chunk, :] = p.astype(jnp.bfloat16)
        numer = jnp.zeros((GROUP_HEADS * queries, WIN), jnp.float32)
        for b, ref in enumerate((up_ref, own_ref, down_ref)):
            v_win = ref[1, :, :, w0 : w0 + WIN].reshape(keys, WIN)
            numer += jnp.dot(
                p_ref[:, b * keys : (b + 1) * keys], v_win, preferred_element_type=jnp.float32
            )
        top = jnp.concatenate(tops, axis=0)
        total = jnp.concatenate(totals, axis=0)
        numer = numer / total
        lse = top + jnp.log2(total)
        out = jnp.zeros((queries, WIN), jnp.float32)
        lse_wide = jnp.zeros((queries, WIN), jnp.float32)
        for hh in range(GROUP_HEADS):
            mine = (lane >= off + hh * dh) & (lane < off + (hh + 1) * dh)
            at = slice(hh * queries, (hh + 1) * queries)
            out = jnp.where(mine, numer[at], out)
            lse_wide = jnp.where(mine, lse[at], lse_wide)
        for ref, wide_block in ((out_ref, out), (lse_ref, lse_wide)):
            if g % 2:
                held = ref[:, w0 : w0 + 128]
                ref[:, w0 : w0 + 128] = jnp.where(iota((1, 128), 1) < 64, held, wide_block[:, :128])
                ref[:, w0 + 128 : w0 + WIN] = wide_block[:, 128:]
            else:
                ref[:, w0 : w0 + WIN] = wide_block


def merge_kernel(win_ref, lse_ref, back_ref, weight_ref, out_ref):
    rows, cols, width = out_ref.shape
    queries = rows * cols
    dh = width // HEAD_COUNT
    back = back_ref[...].reshape(rows, GROUPS, cols, WIN)
    src = iota((WIN, WIN), 0) - 192
    dst = iota((WIN, WIN), 1)
    stat = (src >= 0) & (src < STATS * GROUP_HEADS) & (dst < 192)
    parts = []
    for g in range(GROUPS):
        x = back[:, g].reshape(queries, WIN)
        place = jnp.where(dst < 128, dst + 64, dst - 128) if g % 2 else dst
        spread = jnp.where(stat & (src % GROUP_HEADS == place // dh), 1.0, 0.0).astype(jnp.bfloat16)
        lse_d = jnp.dot(x, spread, preferred_element_type=jnp.float32)
        pair = []
        for y in (x.astype(jnp.float32), lse_d):
            pair.append((y[:, :128], pltpu.roll(y[:, 128:], 64, 1) if g % 2 else y[:, 128:]))
        parts.append(pair)
    low = iota((1, 128), 1) < 64
    att = []
    for tile in range(width // 128):
        pair, place = 2 * (tile // 3), tile % 3
        if place == 1:
            o_d, lse_d = (jnp.where(low, parts[pair][i][1], parts[pair + 1][i][1]) for i in range(2))
        else:
            o_d, lse_d = (parts[pair + place // 2][i][0] for i in range(2))
        at = slice(tile * 128, (tile + 1) * 128)
        lse_w = lse_ref[:, at]
        big = jnp.maximum(lse_w, lse_d)
        a = jnp.exp2(lse_w - big)
        b = jnp.exp2(lse_d - big)
        att.append((a * win_ref[:, at] + b * o_d) / (a + b))
    att = jnp.concatenate(att, axis=1).astype(jnp.bfloat16)
    enc = jnp.dot(att, weight_ref[...], preferred_element_type=jnp.float32)
    out_ref[...] = enc.astype(jnp.bfloat16).reshape(out_ref.shape)


def call(kernel, out_shape, ins, scratch=(), flops=0, name=None):
    spaces = dict(s=pltpu.SMEM, v=pltpu.VMEM, a=pl.ANY)
    vmem = pl.BlockSpec(memory_space=pltpu.VMEM)
    many = isinstance(out_shape, (tuple, list))
    return pl.pallas_call(
        kernel,
        out_shape=out_shape,
        in_specs=[pl.BlockSpec(memory_space=spaces[c]) for c in ins],
        out_specs=[vmem] * len(out_shape) if many else vmem,
        scratch_shapes=list(scratch),
        cost_estimate=pl.CostEstimate(flops=flops, transcendentals=0, bytes_accessed=1 << 20),
        compiler_params=pltpu.CompilerParams(vmem_limit_bytes=20 << 20),
        name=name,
    )


def per_device(q, k, v, tissue, dilation_levels, segment_levels, weight):
    rows, cols, width = q.shape
    peers = lax.axis_size("col")
    n_row = lax.axis_size("row")
    bf16, f32 = jnp.bfloat16, jnp.float32
    shape, vmem = jax.ShapeDtypeStruct, pltpu.VMEM
    keys_d = peers * STEP
    half = shape((2, rows, R, width), bf16)
    send, right, left, keyseg = call(
        pack_kernel,
        [shape((peers, 4 * STEP, 128), bf16), half, half, shape((STEP, keys_d), jnp.int32)],
        ins="ssaaaa",
        scratch=[vmem((rows, cols, width), bf16)] * 3
        + [vmem((rows, tissue.shape[1]), jnp.int32), pltpu.SemaphoreType.DMA((4,))],
        name="pack",
    )(dilation_levels, segment_levels, q, k, v, tissue)
    got = lax.all_to_all(send, "col", 0, 0, tiled=True)
    up_c = [(i, i + 1) for i in range(peers - 1)]
    up_r = [(i, i + 1) for i in range(n_row - 1)]
    from_left = lax.ppermute(right, "col", up_c)
    from_right = lax.ppermute(left, "col", [(b, a) for a, b in up_c])
    own = jnp.concatenate([from_left, jnp.stack([k, v]), from_right], axis=2)
    above = lax.ppermute(own, "row", up_r)
    below = lax.ppermute(own, "row", [(b, a) for a, b in up_r])
    back = call(
        dilated_kernel,
        shape((peers, cols, WIN), bf16),
        ins="ssvv",
        scratch=[vmem((GROUP_HEADS * peers * cols, keys_d), f32), vmem((peers * cols, keys_d), bf16)],
        flops=1 << 31,
        name="dilated",
    )(lax.axis_index("col").reshape(1) % GROUPS, segment_levels, got, keyseg)
    back = lax.all_to_all(back, "col", 0, 0, tiled=True)
    keys = rows * (cols + 2 * R)
    queries = rows * cols
    stack = GROUP_HEADS * queries
    win, lse = call(
        window_kernel,
        [shape((queries, width), f32)] * 2,
        ins="vvvvv",
        scratch=[vmem((queries, 3 * keys), f32), vmem((stack, 3 * keys), f32), vmem((stack, 3 * keys), bf16)],
        flops=1 << 32,
        name="window",
    )(q, above, own, below, tissue)
    return call(merge_kernel, shape((rows, cols, width), bf16), ins="vvvv", flops=1 << 28, name="merge")(
        win, lse, back, weight
    )


def solution(mesh):
    spec = P("row", "col", None)
    return jax.shard_map(
        per_device,
        mesh=mesh,
        in_specs=(spec, spec, spec, P(), P(), P(), P()),
        out_specs=spec,
        check_vma=False,
    )
```

time: 60.3 us -> 62.6 us (1.038)
  the two profiles are of different devices: /device:TPU:8 before, /device:TPU:24 now
where the time goes in v2:
time: 62.6 us; the launch traced here: 62.1 us
  starting transfers between devices  28.1 us (45%)
  waiting for transfers between devices  14.5 us (23%)
  Pallas kernels  12.2 us (19%)
  local copies, waits for them, and re-layouts  7.11 us (11%)
    all_to_all x1, starting transfers between devices, per_device(): got = lax.all_to_all(send, 'col', 0, 0, tiled=True)  15.1 us
    all_to_all x1, waiting for transfers between devices, per_device(): got = lax.all_to_all(send, 'col', 0, 0, tiled=True)  7.86 us
    unnamed x28, local copies, waits for them, and re-layouts  7.11 us
    all_to_all x1, waiting for transfers between devices, per_device(): back = lax.all_to_all(back, 'col', 0, 0, tiled=True)  6.58 us
    pallas_call x1, Pallas kernels, per_device(): call(window_kernel, [shape((queries, width), f32)] * 2, ins='vvvvv', scra...  4.99 us
    all_to_all x1, starting transfers between devices, per_device(): back = lax.all_to_all(back, 'col', 0, 0, tiled=True)  3.87 us
    ppermute x1, starting transfers between devices, per_device(): from_left = lax.ppermute(right, 'col', up_c)  3.41 us
    pallas_call x1, Pallas kernels, per_device(): call(dilated_kernel, shape((peers, cols, WIN), bf16), ins='ssvv', scratch...  3.14 us
  transfers between devices with their start and end apart: 6, of which 2 were waited for; matrix products, arithmetic and copies ran while one was open for 0% of the time, Pallas kernels for 13%

profile of v2, /device:TPU:24, one launch (start us, length us, event | category | flops | bytes accessed | tf_op | source)
XLA Modules:
  0.0 62.1 jit_solution(17943402453174472176)
XLA Ops:
  0.0 0.0 copy-start.1
  0.0 0.9 %copy-done.1 = bf16[8,16,768]{2,1,0:T(8,128)(2,1)S(1)} copy-done((bf16[8,16,768]{2,1,0:T(8,128)(2,1)S(1)}, bf16[8,16,768]{2,1,0:T(8,128)(2,1)}, u32[]{:S(2)}) %copy-start.1) | copy-done | bytes 196632
  0.9 0.0 copy-start.3
  0.9 0.9 %copy-done.3 = bf16[8,16,768]{2,1,0:T(8,128)(2,1)S(1)} copy-done((bf16[8,16,768]{2,1,0:T(8,128)(2,1)S(1)}, bf16[8,16,768]{2,1,0:T(8,128)(2,1)}, u32[]{:S(2)}) %copy-start.3) | copy-done | bytes 196632
  1.9 0.0 copy-start.5
  1.9 0.9 %copy-done.5 = s32[128,512]{1,0:T(8,128)S(1)} copy-done((s32[128,512]{1,0:T(8,128)S(1)}, s32[128,512]{1,0:T(8,128)}, u32[]{:S(2)}) %copy-start.5) | copy-done | bytes 262168
  2.8 0.0 copy-start.7
  2.8 0.9 %copy-done.7 = bf16[8,16,768]{2,1,0:T(8,128)(2,1)S(1)} copy-done((bf16[8,16,768]{2,1,0:T(8,128)(2,1)S(1)}, bf16[8,16,768]{2,1,0:T(8,128)(2,1)}, u32[]{:S(2)}) %copy-start.7) | copy-done | bytes 196632
  3.7 0.0 copy-start.9
  3.7 0.7 %copy-done.9 = s32[16]{0:T(128)S(1)} copy-done((s32[16]{0:T(128)S(1)}, s32[16]{0:T(128)}, u32[]{:S(2)}) %copy-start.9) | copy-done | bytes 88
  4.4 0.0 copy-start.10
  4.4 0.7 %copy-done.10 = s32[16]{0:T(128)S(1)} copy-done((s32[16]{0:T(128)S(1)}, s32[16]{0:T(128)}, u32[]{:S(2)}) %copy-start.10) | copy-done | bytes 88
  5.0 0.0 copy-start.2
  5.0 0.0 copy-start.4
  5.0 2.8 %pack.1 = (bf16[32,32,128]{2,1,0:T(8,128)(2,1)}, bf16[2,8,8,768]{3,2,1,0:T(8,128)(2,1)S(1)}, bf16[2,8,8,768]{3,2,1,0:T(8,128)(2,1)S(1)}, s32[8,256]{1,0:T(8,128)S(1)}) custom-call(s32[16]{0:T(128)S(1)} %copy-done.9, s32[16]{0:T(128)S(1)} %copy-done.10, bf16[8,16,768]{2,1,0:T(8,128)(2,1)S(1)} %copy-done.7, bf16[8,16,768]{2,1,0:T(8,128)(2,1)S(1)} %copy-done.1, ...), custom_call_target="tpu_custom_call" | custom-call | bytes 1048576 | tf_op jit(solution)/shard_map/pack/pallas_call | solution.py:312
  7.9 0.0 copy-start.11
  7.9 3.4 %collective-permute-start = (bf16[2,8,8,768]{3,2,1,0:T(8,128)(2,1)S(1)}, bf16[2,8,8,768]{3,2,1,0:T(8,128)(2,1)S(1)}, u32[]{:S(2)}, u32[]{:S(2)}) collective-permute-start(bf16[2,8,8,768]{3,2,1,0:T(8,128)(2,1)S(1)} %get-tuple-element.11), channel_id=1, source_target_pairs={{0,1},{1,2},{2,3},{3,4},{4,5},{5,6},{6,7},{7,8},{8,9},{9,10},{10,1... | collective-permute-start | bytes 589832 | tf_op jit(solution)/shard_map/ppermute | solution.py:323
  11.3 1.3 %collective-permute-start.1 = (bf16[2,8,8,768]{3,2,1,0:T(8,128)(2,1)S(1)}, bf16[2,8,8,768]{3,2,1,0:T(8,128)(2,1)S(1)}, u32[]{:S(2)}, u32[]{:S(2)}) collective-permute-start(bf16[2,8,8,768]{3,2,1,0:T(8,128)(2,1)S(1)} %get-tuple-element.12), channel_id=1, source_target_pairs={{1,0},{2,1},{3,2},{4,3},{5,4},{6,5},{7,6},{8,7},{9,8},{10,9},{11,1... | collective-permute-start | bytes 589832 | tf_op jit(solution)/shard_map/ppermute | solution.py:324
  12.6 15.1 %all-to-all-start = ((bf16[32,32,128]{2,1,0:T(8,128)(2,1)}), bf16[32,32,128]{2,1,0:T(8,128)(2,1)S(1)}, u32[]{:S(2)}, u32[]{:S(2)}) async-start(bf16[32,32,128]{2,1,0:T(8,128)(2,1)} %get-tuple-element.15), calls=%async_computation | async-start | bytes 524288 | tf_op jit(solution)/shard_map/all_to_all | solution.py:320
  27.8 0.0 collective-permute-done
  27.8 0.0 collective-permute-done.1
  27.8 0.0 copy-done.2
  27.8 0.0 copy-done.4
  27.8 0.1 pad_maximum_fusion.own_ref
  27.9 1.9 %collective-permute-start.3 = (bf16[2,8,32,768]{3,2,1,0:T(8,128)(2,1)S(1)}, bf16[2,8,32,768]{3,2,1,0:T(8,128)(2,1)S(1)}, u32[]{:S(2)}, u32[]{:S(2)}) collective-permute-start(bf16[2,8,32,768]{3,2,1,0:T(8,128)(2,1)S(1)} %pad_maximum_fusion.own_ref), channel_id=1, source_target_pairs={{32,0},{64,32},{96,64},{128,96},{160,128},{192,160},{224,192},{256... | collective-permute-start | bytes 2359304 | tf_op jit(solution)/shard_map/ppermute | solution.py:327
  29.8 2.4 %collective-permute-start.2 = (bf16[2,8,32,768]{3,2,1,0:T(8,128)(2,1)S(1)}, bf16[2,8,32,768]{3,2,1,0:T(8,128)(2,1)}, u32[]{:S(2)}, u32[]{:S(2)}) collective-permute-start(bf16[2,8,32,768]{3,2,1,0:T(8,128)(2,1)S(1)} %pad_maximum_fusion.own_ref), channel_id=1, source_target_pairs={{0,32},{32,64},{64,96},{96,128},{128,160},{160,192},{192,224},{224... | collective-permute-start | bytes 2359304 | tf_op jit(solution)/shard_map/ppermute | solution.py:326
  32.2 7.9 %all-to-all-done.x_ref = bf16[32,32,128]{2,1,0:T(8,128)(2,1)S(1)} async-done(((bf16[32,32,128]{2,1,0:T(8,128)(2,1)}), bf16[32,32,128]{2,1,0:T(8,128)(2,1)S(1)}, u32[]{:S(2)}, u32[]{:S(2)}) %all-to-all-start) | async-done | bytes 262176 | tf_op jit(solution)/shard_map/all_to_all | solution.py:320
  40.1 0.0 copy-done.11
  40.1 0.0 copy-start.6
  40.1 0.0 copy-start.8
  40.1 3.1 %dilated.1 = bf16[32,16,256]{2,1,0:T(8,128)(2,1)} custom-call(s32[1]{0:T(128)S(6)} %select_n.7.pos_ref, s32[16]{0:T(128)S(1)} %copy-done.11, bf16[32,32,128]{2,1,0:T(8,128)(2,1)S(1)} %all-to-all-done.x_ref, s32[8,256]{1,0:T(8,128)S(1)} %get-tuple-element.16.keyseg_ref), custom_call_target="tpu_custom_call" | custom-call | flops 2147483648 | bytes 1048576 | tf_op jit(solution)/shard_map/dilated/pallas_call | solution.py:328
  43.2 3.9 %all-to-all-start.1 = ((bf16[32,16,256]{2,1,0:T(8,128)(2,1)}), bf16[32,16,256]{2,1,0:T(8,128)(2,1)S(1)}, u32[]{:S(2)}, u32[]{:S(2)}) async-start(bf16[32,16,256]{2,1,0:T(8,128)(2,1)} %dilated.1), calls=%async_computation.1 | async-start | bytes 524288 | tf_op jit(solution)/shard_map/all_to_all | solution.py:336
  47.1 0.0 copy-start
  47.1 0.0 collective-permute-done.3.down_ref
  47.2 0.0 copy-start.12
  47.2 0.9 %copy-done.12 = bf16[2,8,32,768]{3,2,1,0:T(8,128)(2,1)} copy-done((bf16[2,8,32,768]{3,2,1,0:T(8,128)(2,1)}, bf16[2,8,32,768]{3,2,1,0:T(8,128)(2,1)S(1)}, u32[]{:S(2)}) %copy-start.12) | copy-done | bytes 786456
  48.1 0.0 collective-permute-done.2.up_ref
  48.1 0.0 copy-done.6
  48.1 0.0 copy-done.8
  48.1 0.0 copy-start.13
  48.1 1.1 %copy-done.13 = bf16[2,8,32,768]{3,2,1,0:T(8,128)(2,1)S(1)} copy-done((bf16[2,8,32,768]{3,2,1,0:T(8,128)(2,1)S(1)}, bf16[2,8,32,768]{3,2,1,0:T(8,128)(2,1)}, u32[]{:S(2)}) %copy-start.13) | copy-done | bytes 786456
  49.2 5.0 %window.1 = (f32[128,768]{1,0:T(8,128)S(1)}, f32[128,768]{1,0:T(8,128)S(1)}) custom-call(bf16[8,16,768]{2,1,0:T(8,128)(2,1)S(1)} %copy-done.8, bf16[2,8,32,768]{3,2,1,0:T(8,128)(2,1)} %collective-permute-done.2.up_ref, bf16[2,8,32,768]{3,2,1,0:T(8,128)(2,1)S(1)} %pad_maximum_fusion.own_ref, bf16[2,8,32,768]{3,2,1,0:T(8,128)(2,1)S(1)} %copy-done.13, ...), custom_call_target="tpu_custom_call" | custom-call | flops 4294967296 | bytes 1048576 | tf_op jit(solution)/shard_map/window/pallas_call | solution.py:340
  54.2 6.6 %all-to-all-done.1.back_ref = bf16[32,16,256]{2,1,0:T(8,128)(2,1)S(1)} async-done(((bf16[32,16,256]{2,1,0:T(8,128)(2,1)}), bf16[32,16,256]{2,1,0:T(8,128)(2,1)S(1)}, u32[]{:S(2)}, u32[]{:S(2)}) %all-to-all-start.1) | async-done | bytes 262176 | tf_op jit(solution)/shard_map/all_to_all | solution.py:336
  60.8 0.0 copy-done
  60.8 1.3 %merge.1 = bf16[8,16,768]{2,1,0:T(8,128)(2,1)} custom-call(f32[128,768]{1,0:T(8,128)S(1)} %get-tuple-element.13.win_ref, f32[128,768]{1,0:T(8,128)S(1)} %get-tuple-element.14.lse_ref, bf16[32,16,256]{2,1,0:T(8,128)(2,1)S(1)} %all-to-all-done.1.back_ref, bf16[768,768]{1,0:T(8,128)(2,1)S(1)} %copy-done), custom_call_target="tpu_custom_call" | custom-call | flops 268435456 | bytes 1048576 | tf_op jit(solution)/shard_map/merge/pallas_call | solution.py:348
Async XLA Ops:
  0.0 0.9 %copy-start.1 = (bf16[8,16,768]{2,1,0:T(8,128)(2,1)S(1)}, bf16[8,16,768]{2,1,0:T(8,128)(2,1)}, u32[]{:S(2)}) copy-start(bf16[8,16,768]{2,1,0:T(8,128)(2,1)} %k_hbm.1) | copy-start | bytes 589828
  0.9 0.9 %copy-start.3 = (bf16[8,16,768]{2,1,0:T(8,128)(2,1)S(1)}, bf16[8,16,768]{2,1,0:T(8,128)(2,1)}, u32[]{:S(2)}) copy-start(bf16[8,16,768]{2,1,0:T(8,128)(2,1)} %v_hbm.1) | copy-start | bytes 589828
  1.9 0.9 %copy-start.5 = (s32[128,512]{1,0:T(8,128)S(1)}, s32[128,512]{1,0:T(8,128)}, u32[]{:S(2)}) copy-start(s32[128,512]{1,0:T(8,128)} %tissue_ref.1) | copy-start | bytes 786436
  2.8 0.9 %copy-start.7 = (bf16[8,16,768]{2,1,0:T(8,128)(2,1)S(1)}, bf16[8,16,768]{2,1,0:T(8,128)(2,1)}, u32[]{:S(2)}) copy-start(bf16[8,16,768]{2,1,0:T(8,128)(2,1)} %q_ref.1) | copy-start | bytes 589828
  3.7 0.7 %copy-start.9 = (s32[16]{0:T(128)S(1)}, s32[16]{0:T(128)}, u32[]{:S(2)}) copy-start(s32[16]{0:T(128)} %dil_ref.1) | copy-start | bytes 196
  4.4 0.7 %copy-start.10 = (s32[16]{0:T(128)S(1)}, s32[16]{0:T(128)}, u32[]{:S(2)}) copy-start(s32[16]{0:T(128)} %seg_ref.3) | copy-start | bytes 196
  5.0 22.7 %copy-start.2 = (bf16[8,16,768]{2,1,0:T(8,128)(2,1)S(1)}, bf16[8,16,768]{2,1,0:T(8,128)(2,1)}, u32[]{:S(2)}) copy-start(bf16[8,16,768]{2,1,0:T(8,128)(2,1)} %k_hbm.1) | copy-start | bytes 589828
  5.0 22.7 %copy-start.4 = (bf16[8,16,768]{2,1,0:T(8,128)(2,1)S(1)}, bf16[8,16,768]{2,1,0:T(8,128)(2,1)}, u32[]{:S(2)}) copy-start(bf16[8,16,768]{2,1,0:T(8,128)(2,1)} %v_hbm.1) | copy-start | bytes 589828
  7.9 32.2 %copy-start.11 = (s32[16]{0:T(128)S(1)}, s32[16]{0:T(128)}, u32[]{:S(2)}) copy-start(s32[16]{0:T(128)} %seg_ref.3) | copy-start | bytes 196
  7.9 19.9 %collective-permute-start = (bf16[2,8,8,768]{3,2,1,0:T(8,128)(2,1)S(1)}, bf16[2,8,8,768]{3,2,1,0:T(8,128)(2,1)S(1)}, u32[]{:S(2)}, u32[]{:S(2)}) collective-permute-start(bf16[2,8,8,768]{3,2,1,0:T(8,128)(2,1)S(1)} %get-tuple-element.11), channel_id=1, source_target_pairs={{0,1},{1,2},{2,3},{3,4},{4,5},{5,6},{6,7},{7,8},{8,9},{9,10},{10,1... | collective-permute-start | bytes 589832 | tf_op jit(solution)/shard_map/ppermute | solution.py:323
  11.3 16.5 %collective-permute-start.1 = (bf16[2,8,8,768]{3,2,1,0:T(8,128)(2,1)S(1)}, bf16[2,8,8,768]{3,2,1,0:T(8,128)(2,1)S(1)}, u32[]{:S(2)}, u32[]{:S(2)}) collective-permute-start(bf16[2,8,8,768]{3,2,1,0:T(8,128)(2,1)S(1)} %get-tuple-element.12), channel_id=1, source_target_pairs={{1,0},{2,1},{3,2},{4,3},{5,4},{6,5},{7,6},{8,7},{9,8},{10,9},{11,1... | collective-permute-start | bytes 589832 | tf_op jit(solution)/shard_map/ppermute | solution.py:324
  12.6 27.5 %all-to-all-start = ((bf16[32,32,128]{2,1,0:T(8,128)(2,1)}), bf16[32,32,128]{2,1,0:T(8,128)(2,1)S(1)}, u32[]{:S(2)}, u32[]{:S(2)}) async-start(bf16[32,32,128]{2,1,0:T(8,128)(2,1)} %get-tuple-element.15), calls=%async_computation | async-start | bytes 524288 | tf_op jit(solution)/shard_map/all_to_all | solution.py:320
  27.9 19.3 %collective-permute-start.3 = (bf16[2,8,32,768]{3,2,1,0:T(8,128)(2,1)S(1)}, bf16[2,8,32,768]{3,2,1,0:T(8,128)(2,1)S(1)}, u32[]{:S(2)}, u32[]{:S(2)}) collective-permute-start(bf16[2,8,32,768]{3,2,1,0:T(8,128)(2,1)S(1)} %pad_maximum_fusion.own_ref), channel_id=1, source_target_pairs={{32,0},{64,32},{96,64},{128,96},{160,128},{192,160},{224,192},{256... | collective-permute-start | bytes 2359304 | tf_op jit(solution)/shard_map/ppermute | solution.py:327
  29.8 18.3 %collective-permute-start.2 = (bf16[2,8,32,768]{3,2,1,0:T(8,128)(2,1)S(1)}, bf16[2,8,32,768]{3,2,1,0:T(8,128)(2,1)}, u32[]{:S(2)}, u32[]{:S(2)}) collective-permute-start(bf16[2,8,32,768]{3,2,1,0:T(8,128)(2,1)S(1)} %pad_maximum_fusion.own_ref), channel_id=1, source_target_pairs={{0,32},{32,64},{64,96},{96,128},{128,160},{160,192},{192,224},{224... | collective-permute-start | bytes 2359304 | tf_op jit(solution)/shard_map/ppermute | solution.py:326
  40.1 8.0 %copy-start.6 = (s32[128,512]{1,0:T(8,128)S(1)}, s32[128,512]{1,0:T(8,128)}, u32[]{:S(2)}) copy-start(s32[128,512]{1,0:T(8,128)} %tissue_ref.1) | copy-start | bytes 786436
  40.1 8.0 %copy-start.8 = (bf16[8,16,768]{2,1,0:T(8,128)(2,1)S(1)}, bf16[8,16,768]{2,1,0:T(8,128)(2,1)}, u32[]{:S(2)}) copy-start(bf16[8,16,768]{2,1,0:T(8,128)(2,1)} %q_ref.1) | copy-start | bytes 589828
  43.2 17.6 %all-to-all-start.1 = ((bf16[32,16,256]{2,1,0:T(8,128)(2,1)}), bf16[32,16,256]{2,1,0:T(8,128)(2,1)S(1)}, u32[]{:S(2)}, u32[]{:S(2)}) async-start(bf16[32,16,256]{2,1,0:T(8,128)(2,1)} %dilated.1), calls=%async_computation.1 | async-start | bytes 524288 | tf_op jit(solution)/shard_map/all_to_all | solution.py:336
  47.1 13.7 %copy-start = (bf16[768,768]{1,0:T(8,128)(2,1)S(1)}, bf16[768,768]{1,0:T(8,128)(2,1)}, u32[]{:S(2)}) copy-start(bf16[768,768]{1,0:T(8,128)(2,1)} %weight_ref.1) | copy-start | bytes 3538948
  47.2 0.9 %copy-start.12 = (bf16[2,8,32,768]{3,2,1,0:T(8,128)(2,1)}, bf16[2,8,32,768]{3,2,1,0:T(8,128)(2,1)S(1)}, u32[]{:S(2)}) copy-start(bf16[2,8,32,768]{3,2,1,0:T(8,128)(2,1)S(1)} %collective-permute-done.3.down_ref) | copy-start | bytes 2359300
  48.1 1.1 %copy-start.13 = (bf16[2,8,32,768]{3,2,1,0:T(8,128)(2,1)S(1)}, bf16[2,8,32,768]{3,2,1,0:T(8,128)(2,1)}, u32[]{:S(2)}) copy-start(bf16[2,8,32,768]{3,2,1,0:T(8,128)(2,1)} %copy-done.12) | copy-start | bytes 2359300

commit v3 on v2

--- a/solution.py
+++ b/solution.py
@@ -16,6 +16,7 @@
 WIN = 256
 WIN_START = (0, 128, 384, 512)
 LOG2E = 1.4426950408889634
+CHUNK = 128
 STATS = 3
 
 
@@ -30,8 +31,8 @@
 
 
 def pack_kernel(
-    dil_ref, seg_ref, q_hbm, k_hbm, v_hbm, t_hbm, send_ref, right_ref, left_ref, keyseg_ref,
-    q_ref, k_ref, v_ref, t_ref, sem,
+    dil_hbm, seg_hbm, q_hbm, k_hbm, v_hbm, t_hbm, send_ref, right_ref, left_ref, bias_ref,
+    q_ref, k_ref, v_ref, t_ref, dil_ref, seg_ref, sem,
 ):
     rows, cols, width = q_ref.shape
     total_cols = t_ref.shape[1]
@@ -44,6 +45,8 @@
         pltpu.make_async_copy(k_hbm, k_ref, sem.at[1]),
         pltpu.make_async_copy(v_hbm, v_ref, sem.at[2]),
         pltpu.make_async_copy(q_hbm, q_ref, sem.at[3]),
+        pltpu.make_async_copy(dil_hbm, dil_ref, sem.at[4]),
+        pltpu.make_async_copy(seg_hbm, seg_ref, sem.at[5]),
     ]
     for copy in copies:
         copy.start()
@@ -62,6 +65,8 @@
         tissue = jnp.where(((group * GROUP_HEADS + sub) >> bit) & 1 == 1, shifted, tissue)
     slot_tissue = jnp.dot(tissue.astype(jnp.bfloat16), pick, preferred_element_type=jnp.float32)
     key_slot = iota((1, keys), 1)
+    copies[4].wait()
+    copies[5].wait()
     for hh in range(GROUP_HEADS):
         head = group * GROUP_HEADS + hh
         key_col = (key_slot // STEP) * cols + (key_slot % STEP) * STEP + head % STEP
@@ -69,7 +74,11 @@
         ok = (key_slot % STEP < 2) & ((key_col & period) == (head & period))
         ok = ok & (slot_tissue[hh : hh + 1] > 0.5)
         shift = total_cols.bit_length() - 1 - seg_ref[head]
-        keyseg_ref[hh : hh + 1, :] = jnp.where(ok, jnp.right_shift(key_col, shift), -1)
+        key_seg = jnp.where(ok, jnp.right_shift(key_col, shift), -1)
+        for c in range(total_cols // CHUNK):
+            near = key_seg == jnp.right_shift(c * CHUNK, shift)
+            at = hh * (total_cols // CHUNK) + c
+            bias_ref[at : at + 1, :] = jnp.where(near, 0.0, NEG)
     phase = (iota((STEP, width), 1) // dh) % STEP == iota((STEP, width), 0)
     sub = iota((STEP, width), 0)
     copies[1].wait()
@@ -106,15 +115,13 @@
             send_ref[d, 2 * STEP : 3 * STEP, :] = jnp.where(low, first, second).astype(jnp.bfloat16)
 
 
-def dilated_kernel(pos_ref, seg_ref, x_ref, keyseg_ref, out_ref, s_ref, p_ref):
+def dilated_kernel(x_ref, bias_ref, out_ref, s_ref, p_ref):
     peers = x_ref.shape[0]
     cols = out_ref.shape[1]
     total_cols = peers * cols
     dh = 48
-    group = pos_ref[0]
-    odd = group % 2
+    odd = lax.axis_index("col") % 2
     keys = peers * STEP
-    log_cols = total_cols.bit_length() - 1
     low = iota((1, 128), 1) < 64
     zero = jnp.zeros((), jnp.bfloat16)
     q_full = x_ref[:, : 2 * STEP, :].reshape(total_cols, 128)
@@ -130,7 +137,6 @@
     v_all = jnp.concatenate([kv2, kv6], axis=1).astype(jnp.bfloat16)
     lane = iota((1, WIN), 1)
     place = jnp.where(odd == 1, jnp.where(lane < 128, lane + 64, lane - 128), lane)
-    chunk = 128
     out = jnp.zeros((total_cols, WIN), jnp.float32)
     stat = jnp.zeros((total_cols, 128), jnp.float32)
     stat_lane = iota((1, 128), 1)
@@ -141,18 +147,17 @@
         )
     for hh in range(GROUP_HEADS):
         mine = (place >= hh * dh) & (place < (hh + 1) * dh) & (lane < 192)
-        shift = log_cols - seg_ref[group * GROUP_HEADS + hh]
-        keyseg = keyseg_ref[hh : hh + 1, :]
         tops, totals = [], []
-        for c0 in range(0, total_cols, chunk):
-            bias = jnp.where(keyseg == jnp.right_shift(c0, shift), 0.0, NEG)
-            at = slice(hh * total_cols + c0, hh * total_cols + c0 + chunk)
+        for c0 in range(0, total_cols, CHUNK):
+            row = (hh * total_cols + c0) // CHUNK
+            bias = bias_ref[row : row + 1, :]
+            at = slice(hh * total_cols + c0, hh * total_cols + c0 + CHUNK)
             s = s_ref[at, :] * (LOG2E / math.sqrt(dh)) + bias
             top = jnp.maximum(jnp.max(s, axis=1, keepdims=True), 0.5 * NEG)
             p = jnp.exp2(s - top)
             tops.append(top)
             totals.append(jnp.sum(p, axis=1, keepdims=True))
-            p_ref[c0 : c0 + chunk, :] = p.astype(jnp.bfloat16)
+            p_ref[c0 : c0 + CHUNK, :] = p.astype(jnp.bfloat16)
         numer = jnp.dot(p_ref[...], v_all, preferred_element_type=jnp.float32)
         total = jnp.concatenate(totals, axis=0)
         safe = jnp.maximum(total, 0.5)
@@ -169,7 +174,15 @@
     out_ref[...] = out.astype(jnp.bfloat16).reshape(out_ref.shape)
 
 
-def window_kernel(q_ref, up_ref, own_ref, down_ref, tissue_ref, out_ref, lse_ref, bias_ref, s_ref, p_ref):
+def window_kernel(
+    q_ref, up_hbm, own_ref, down_hbm, tissue_ref, out_ref, lse_ref, bias_ref, s_ref, p_ref, up_ref, down_ref, sem
+):
+    copies = [
+        pltpu.make_async_copy(up_hbm, up_ref, sem.at[0]),
+        pltpu.make_async_copy(down_hbm, down_ref, sem.at[1]),
+    ]
+    for copy in copies:
+        copy.start()
     rows, cols, width = q_ref.shape
     queries = rows * cols
     dh = width // HEAD_COUNT
@@ -199,6 +212,8 @@
         bias_ref[:, b * keys : (b + 1) * keys] = jnp.where(ok, 0.0, NEG)
     lane = iota((1, WIN), 1)
     chunk = 64
+    for copy in copies:
+        copy.wait()
     for g in range(GROUPS):
         w0 = WIN_START[g]
         off = g * GROUP_HEADS * dh - w0
@@ -286,7 +301,7 @@
 
 
 def call(kernel, out_shape, ins, scratch=(), flops=0, name=None):
-    spaces = dict(s=pltpu.SMEM, v=pltpu.VMEM, a=pl.ANY)
+    spaces = dict(v=pltpu.VMEM, h=pltpu.HBM)
     vmem = pl.BlockSpec(memory_space=pltpu.VMEM)
     many = isinstance(out_shape, (tuple, list))
     return pl.pallas_call(
@@ -309,14 +324,17 @@
     shape, vmem = jax.ShapeDtypeStruct, pltpu.VMEM
     keys_d = peers * STEP
     half = shape((2, rows, R, width), bf16)
-    send, right, left, keyseg = call(
+    hbm = [pltpu.with_memory_space_constraint(x, pltpu.HBM) for x in (dilation_levels, segment_levels, q, k, v, tissue)]
+    send, right, left, bias = call(
         pack_kernel,
-        [shape((peers, 4 * STEP, 128), bf16), half, half, shape((STEP, keys_d), jnp.int32)],
-        ins="ssaaaa",
+        [shape((peers, 4 * STEP, 128), bf16), half, half, shape((16, keys_d), f32)],
+        ins="hhhhhh",
         scratch=[vmem((rows, cols, width), bf16)] * 3
-        + [vmem((rows, tissue.shape[1]), jnp.int32), pltpu.SemaphoreType.DMA((4,))],
+        + [vmem((rows, tissue.shape[1]), jnp.int32)]
+        + [pltpu.SMEM((HEAD_COUNT,), jnp.int32)] * 2
+        + [pltpu.SemaphoreType.DMA((6,))],
         name="pack",
-    )(dilation_levels, segment_levels, q, k, v, tissue)
+    )(*hbm)
     got = lax.all_to_all(send, "col", 0, 0, tiled=True)
     up_c = [(i, i + 1) for i in range(peers - 1)]
     up_r = [(i, i + 1) for i in range(n_row - 1)]
@@ -328,11 +346,11 @@
     back = call(
         dilated_kernel,
         shape((peers, cols, WIN), bf16),
-        ins="ssvv",
+        ins="vv",
         scratch=[vmem((GROUP_HEADS * peers * cols, keys_d), f32), vmem((peers * cols, keys_d), bf16)],
         flops=1 << 31,
         name="dilated",
-    )(lax.axis_index("col").reshape(1) % GROUPS, segment_levels, got, keyseg)
+    )(got, bias)
     back = lax.all_to_all(back, "col", 0, 0, tiled=True)
     keys = rows * (cols + 2 * R)
     queries = rows * cols
@@ -340,11 +358,13 @@
     win, lse = call(
         window_kernel,
         [shape((queries, width), f32)] * 2,
-        ins="vvvvv",
-        scratch=[vmem((queries, 3 * keys), f32), vmem((stack, 3 * keys), f32), vmem((stack, 3 * keys), bf16)],
+        ins="vhvhv",
+        scratch=[vmem((queries, 3 * keys), f32), vmem((stack, 3 * keys), f32), vmem((stack, 3 * keys), bf16)]
+        + [vmem(own.shape, bf16)] * 2
+        + [pltpu.SemaphoreType.DMA((2,))],
         flops=1 << 32,
         name="window",
-    )(q, above, own, below, tissue)
+    )(q, pltpu.with_memory_space_constraint(above, pltpu.HBM), own, pltpu.with_memory_space_constraint(below, pltpu.HBM), tissue)
     return call(merge_kernel, shape((rows, cols, width), bf16), ins="vvvv", flops=1 << 28, name="merge")(
         win, lse, back, weight
     )

time: 62.6 us -> 56.4 us (0.901)
  local copies, waits for them, and re-layouts: 7.11 us -> 0.94 us
  waiting for transfers between devices: 14.5 us -> 15.4 us
  Pallas kernels: 12.2 us -> 11.3 us
    unnamed x28 -> x12, local copies, waits for them, and re-layouts: 7.11 us -> 0.94 us
    all_to_all x1, waiting for transfers between devices: 6.58 us -> 7.55 us  [per_device(): back = lax.all_to_all(back, 'col', 0, 0, tiled=True)]
  transfers between devices with their start and end apart: 6 -> 6, of which waited for: 2 -> 2; matrix products, arithmetic and copies ran while one was open for 0% -> 0% of each run, Pallas kernels for 13% -> 14%
where the time goes in v3:
time: 56.4 us; the launch traced here: 56 us
  starting transfers between devices  28.1 us (50%)
  waiting for transfers between devices  15.4 us (27%)
  Pallas kernels  11.3 us (20%)
  local copies, waits for them, and re-layouts  0.94 us (2%)
    all_to_all x1, starting transfers between devices, per_device(): got = lax.all_to_all(send, 'col', 0, 0, tiled=True)  15.2 us
    all_to_all x1, waiting for transfers between devices, per_device(): got = lax.all_to_all(send, 'col', 0, 0, tiled=True)  7.87 us
    all_to_all x1, waiting for transfers between devices, per_device(): back = lax.all_to_all(back, 'col', 0, 0, tiled=True)  7.55 us
    pallas_call x1, Pallas kernels, per_device(): call(window_kernel, [shape((queries, width), f32)] * 2, ins='vhvhv', scra...  5.14 us
    all_to_all x1, starting transfers between devices, per_device(): back = lax.all_to_all(back, 'col', 0, 0, tiled=True)  3.87 us
    ppermute x1, starting transfers between devices, per_device(): from_left = lax.ppermute(right, 'col', up_c)  3.41 us
    pallas_call x1, Pallas kernels, per_device(): call(dilated_kernel, shape((peers, cols, WIN), bf16), ins='vv', scratch=[...  2.61 us
    ppermute x1, starting transfers between devices, per_device(): above = lax.ppermute(own, 'row', up_r)  2.41 us
  transfers between devices with their start and end apart: 6, of which 2 were waited for; matrix products, arithmetic and copies ran while one was open for 0% of the time, Pallas kernels for 14%

profile of v3, /device:TPU:24, one launch (start us, length us, event | category | flops | bytes accessed | tf_op | source)
XLA Modules:
  0.0 56.0 jit_solution(3343828396875445046)
XLA Ops:
  0.0 0.0 copy-start.4
  0.0 0.0 copy-start.3
  0.0 2.3 %pack.1 = (bf16[32,32,128]{2,1,0:T(8,128)(2,1)}, bf16[2,8,8,768]{3,2,1,0:T(8,128)(2,1)S(1)}, bf16[2,8,8,768]{3,2,1,0:T(8,128)(2,1)S(1)}, f32[16,256]{1,0:T(8,128)S(1)}) custom-call(s32[16]{0:T(128)} %dil_hbm.1, s32[16]{0:T(128)} %seg_hbm.1, bf16[8,16,768]{2,1,0:T(8,128)(2,1)} %q_ref.1, bf16[8,16,768]{2,1,0:T(8,128)(2,1)} %k_hbm.1, ...), custom_call_target="tpu_custom_call" | custom-call | bytes 1048576 | tf_op jit(solution)/shard_map/pack/pallas_call | solution.py:328
  2.3 3.4 %collective-permute-start = (bf16[2,8,8,768]{3,2,1,0:T(8,128)(2,1)S(1)}, bf16[2,8,8,768]{3,2,1,0:T(8,128)(2,1)S(1)}, u32[]{:S(2)}, u32[]{:S(2)}) collective-permute-start(bf16[2,8,8,768]{3,2,1,0:T(8,128)(2,1)S(1)} %get-tuple-element.11), channel_id=1, source_target_pairs={{0,1},{1,2},{2,3},{3,4},{4,5},{5,6},{6,7},{7,8},{8,9},{9,10},{10,1... | collective-permute-start | bytes 589832 | tf_op jit(solution)/shard_map/ppermute | solution.py:341
  5.7 1.3 %collective-permute-start.1 = (bf16[2,8,8,768]{3,2,1,0:T(8,128)(2,1)S(1)}, bf16[2,8,8,768]{3,2,1,0:T(8,128)(2,1)S(1)}, u32[]{:S(2)}, u32[]{:S(2)}) collective-permute-start(bf16[2,8,8,768]{3,2,1,0:T(8,128)(2,1)S(1)} %get-tuple-element.12), channel_id=1, source_target_pairs={{1,0},{2,1},{3,2},{4,3},{5,4},{6,5},{7,6},{8,7},{9,8},{10,9},{11,1... | collective-permute-start | bytes 589832 | tf_op jit(solution)/shard_map/ppermute | solution.py:342
  7.0 15.2 %all-to-all-start = ((bf16[32,32,128]{2,1,0:T(8,128)(2,1)}), bf16[32,32,128]{2,1,0:T(8,128)(2,1)S(1)}, u32[]{:S(2)}, u32[]{:S(2)}) async-start(bf16[32,32,128]{2,1,0:T(8,128)(2,1)} %get-tuple-element.15), calls=%async_computation | async-start | bytes 524288 | tf_op jit(solution)/shard_map/all_to_all | solution.py:338
  22.2 0.0 collective-permute-done
  22.2 0.0 collective-permute-done.1
  22.2 0.0 copy-done.4
  22.2 0.0 copy-done.3
  22.2 0.1 pad_maximum_fusion.own_ref
  22.3 1.9 %collective-permute-start.3 = (bf16[2,8,32,768]{3,2,1,0:T(8,128)(2,1)S(1)}, bf16[2,8,32,768]{3,2,1,0:T(8,128)(2,1)S(1)}, u32[]{:S(2)}, u32[]{:S(2)}) collective-permute-start(bf16[2,8,32,768]{3,2,1,0:T(8,128)(2,1)S(1)} %pad_maximum_fusion.own_ref), channel_id=1, source_target_pairs={{32,0},{64,32},{96,64},{128,96},{160,128},{192,160},{224,192},{256... | collective-permute-start | bytes 2359304 | tf_op jit(solution)/shard_map/ppermute | solution.py:345
  24.2 2.4 %collective-permute-start.2 = (bf16[2,8,32,768]{3,2,1,0:T(8,128)(2,1)S(1)}, bf16[2,8,32,768]{3,2,1,0:T(8,128)(2,1)}, u32[]{:S(2)}, u32[]{:S(2)}) collective-permute-start(bf16[2,8,32,768]{3,2,1,0:T(8,128)(2,1)S(1)} %pad_maximum_fusion.own_ref), channel_id=1, source_target_pairs={{0,32},{32,64},{64,96},{96,128},{128,160},{160,192},{192,224},{224... | collective-permute-start | bytes 2359304 | tf_op jit(solution)/shard_map/ppermute | solution.py:344
  26.6 7.9 %all-to-all-done.x_ref = bf16[32,32,128]{2,1,0:T(8,128)(2,1)S(1)} async-done(((bf16[32,32,128]{2,1,0:T(8,128)(2,1)}), bf16[32,32,128]{2,1,0:T(8,128)(2,1)S(1)}, u32[]{:S(2)}, u32[]{:S(2)}) %all-to-all-start) | async-done | bytes 262176 | tf_op jit(solution)/shard_map/all_to_all | solution.py:338
  34.5 0.0 copy-start.1
  34.5 0.0 copy-start.2
  34.5 2.6 %dilated.1 = bf16[32,16,256]{2,1,0:T(8,128)(2,1)} custom-call(bf16[32,32,128]{2,1,0:T(8,128)(2,1)S(1)} %all-to-all-done.x_ref, f32[16,256]{1,0:T(8,128)S(1)} %get-tuple-element.16.bias_ref), custom_call_target="tpu_custom_call" | custom-call | flops 2147483648 | bytes 1048576 | tf_op jit(solution)/shard_map/dilated/pallas_call | solution.py:346
  37.1 3.9 %all-to-all-start.1 = ((bf16[32,16,256]{2,1,0:T(8,128)(2,1)}), bf16[32,16,256]{2,1,0:T(8,128)(2,1)S(1)}, u32[]{:S(2)}, u32[]{:S(2)}) async-start(bf16[32,16,256]{2,1,0:T(8,128)(2,1)} %dilated.1), calls=%async_computation.1 | async-start | bytes 524288 | tf_op jit(solution)/shard_map/all_to_all | solution.py:354
  41.0 0.0 copy-start
  41.0 0.0 collective-permute-done.3.down_hbm
  41.0 0.0 copy-start.5
  41.0 0.9 %copy-done.5 = bf16[2,8,32,768]{3,2,1,0:T(8,128)(2,1)} copy-done((bf16[2,8,32,768]{3,2,1,0:T(8,128)(2,1)}, bf16[2,8,32,768]{3,2,1,0:T(8,128)(2,1)S(1)}, u32[]{:S(2)}) %copy-start.5) | copy-done | bytes 786456
  42.0 0.0 collective-permute-done.2.up_hbm
  42.0 0.0 copy-done.1
  42.0 0.0 copy-done.2
  42.0 5.1 %window.1 = (f32[128,768]{1,0:T(8,128)S(1)}, f32[128,768]{1,0:T(8,128)S(1)}) custom-call(bf16[8,16,768]{2,1,0:T(8,128)(2,1)S(1)} %copy-done.2, bf16[2,8,32,768]{3,2,1,0:T(8,128)(2,1)} %collective-permute-done.2.up_hbm, bf16[2,8,32,768]{3,2,1,0:T(8,128)(2,1)S(1)} %pad_maximum_fusion.own_ref, bf16[2,8,32,768]{3,2,1,0:T(8,128)(2,1)} %copy-done.5, ...), custom_call_target="tpu_custom_call" | custom-call | flops 4294967296 | bytes 1048576 | tf_op jit(solution)/shard_map/window/pallas_call | solution.py:358
  47.1 7.5 %all-to-all-done.1.back_ref = bf16[32,16,256]{2,1,0:T(8,128)(2,1)S(1)} async-done(((bf16[32,16,256]{2,1,0:T(8,128)(2,1)}), bf16[32,16,256]{2,1,0:T(8,128)(2,1)S(1)}, u32[]{:S(2)}, u32[]{:S(2)}) %all-to-all-start.1) | async-done | bytes 262176 | tf_op jit(solution)/shard_map/all_to_all | solution.py:354
  54.7 0.0 copy-done
  54.7 1.3 %merge.1 = bf16[8,16,768]{2,1,0:T(8,128)(2,1)} custom-call(f32[128,768]{1,0:T(8,128)S(1)} %get-tuple-element.13.win_ref, f32[128,768]{1,0:T(8,128)S(1)} %get-tuple-element.14.lse_ref, bf16[32,16,256]{2,1,0:T(8,128)(2,1)S(1)} %all-to-all-done.1.back_ref, bf16[768,768]{1,0:T(8,128)(2,1)S(1)} %copy-done), custom_call_target="tpu_custom_call" | custom-call | flops 268435456 | bytes 1048576 | tf_op jit(solution)/shard_map/merge/pallas_call | solution.py:368
Async XLA Ops:
  0.0 22.2 %copy-start.4 = (bf16[8,16,768]{2,1,0:T(8,128)(2,1)S(1)}, bf16[8,16,768]{2,1,0:T(8,128)(2,1)}, u32[]{:S(2)}) copy-start(bf16[8,16,768]{2,1,0:T(8,128)(2,1)} %v_hbm.1) | copy-start | bytes 589828
  0.0 22.2 %copy-start.3 = (bf16[8,16,768]{2,1,0:T(8,128)(2,1)S(1)}, bf16[8,16,768]{2,1,0:T(8,128)(2,1)}, u32[]{:S(2)}) copy-start(bf16[8,16,768]{2,1,0:T(8,128)(2,1)} %k_hbm.1) | copy-start | bytes 589828
  2.3 19.9 %collective-permute-start = (bf16[2,8,8,768]{3,2,1,0:T(8,128)(2,1)S(1)}, bf16[2,8,8,768]{3,2,1,0:T(8,128)(2,1)S(1)}, u32[]{:S(2)}, u32[]{:S(2)}) collective-permute-start(bf16[2,8,8,768]{3,2,1,0:T(8,128)(2,1)S(1)} %get-tuple-element.11), channel_id=1, source_target_pairs={{0,1},{1,2},{2,3},{3,4},{4,5},{5,6},{6,7},{7,8},{8,9},{9,10},{10,1... | collective-permute-start | bytes 589832 | tf_op jit(solution)/shard_map/ppermute | solution.py:341
  5.7 16.5 %collective-permute-start.1 = (bf16[2,8,8,768]{3,2,1,0:T(8,128)(2,1)S(1)}, bf16[2,8,8,768]{3,2,1,0:T(8,128)(2,1)S(1)}, u32[]{:S(2)}, u32[]{:S(2)}) collective-permute-start(bf16[2,8,8,768]{3,2,1,0:T(8,128)(2,1)S(1)} %get-tuple-element.12), channel_id=1, source_target_pairs={{1,0},{2,1},{3,2},{4,3},{5,4},{6,5},{7,6},{8,7},{9,8},{10,9},{11,1... | collective-permute-start | bytes 589832 | tf_op jit(solution)/shard_map/ppermute | solution.py:342
  7.0 27.5 %all-to-all-start = ((bf16[32,32,128]{2,1,0:T(8,128)(2,1)}), bf16[32,32,128]{2,1,0:T(8,128)(2,1)S(1)}, u32[]{:S(2)}, u32[]{:S(2)}) async-start(bf16[32,32,128]{2,1,0:T(8,128)(2,1)} %get-tuple-element.15), calls=%async_computation | async-start | bytes 524288 | tf_op jit(solution)/shard_map/all_to_all | solution.py:338
  22.3 18.7 %collective-permute-start.3 = (bf16[2,8,32,768]{3,2,1,0:T(8,128)(2,1)S(1)}, bf16[2,8,32,768]{3,2,1,0:T(8,128)(2,1)S(1)}, u32[]{:S(2)}, u32[]{:S(2)}) collective-permute-start(bf16[2,8,32,768]{3,2,1,0:T(8,128)(2,1)S(1)} %pad_maximum_fusion.own_ref), channel_id=1, source_target_pairs={{32,0},{64,32},{96,64},{128,96},{160,128},{192,160},{224,192},{256... | collective-permute-start | bytes 2359304 | tf_op jit(solution)/shard_map/ppermute | solution.py:345
  24.2 17.7 %collective-permute-start.2 = (bf16[2,8,32,768]{3,2,1,0:T(8,128)(2,1)S(1)}, bf16[2,8,32,768]{3,2,1,0:T(8,128)(2,1)}, u32[]{:S(2)}, u32[]{:S(2)}) collective-permute-start(bf16[2,8,32,768]{3,2,1,0:T(8,128)(2,1)S(1)} %pad_maximum_fusion.own_ref), channel_id=1, source_target_pairs={{0,32},{32,64},{64,96},{96,128},{128,160},{160,192},{192,224},{224... | collective-permute-start | bytes 2359304 | tf_op jit(solution)/shard_map/ppermute | solution.py:344
  34.5 7.4 %copy-start.1 = (s32[128,512]{1,0:T(8,128)S(1)}, s32[128,512]{1,0:T(8,128)}, u32[]{:S(2)}) copy-start(s32[128,512]{1,0:T(8,128)} %tissue_ref.1) | copy-start | bytes 786436
  34.5 7.5 %copy-start.2 = (bf16[8,16,768]{2,1,0:T(8,128)(2,1)S(1)}, bf16[8,16,768]{2,1,0:T(8,128)(2,1)}, u32[]{:S(2)}) copy-start(bf16[8,16,768]{2,1,0:T(8,128)(2,1)} %q_ref.1) | copy-start | bytes 589828
  37.1 17.5 %all-to-all-start.1 = ((bf16[32,16,256]{2,1,0:T(8,128)(2,1)}), bf16[32,16,256]{2,1,0:T(8,128)(2,1)S(1)}, u32[]{:S(2)}, u32[]{:S(2)}) async-start(bf16[32,16,256]{2,1,0:T(8,128)(2,1)} %dilated.1), calls=%async_computation.1 | async-start | bytes 524288 | tf_op jit(solution)/shard_map/all_to_all | solution.py:354
  41.0 13.7 %copy-start = (bf16[768,768]{1,0:T(8,128)(2,1)S(1)}, bf16[768,768]{1,0:T(8,128)(2,1)}, u32[]{:S(2)}) copy-start(bf16[768,768]{1,0:T(8,128)(2,1)} %weight_ref.1) | copy-start | bytes 3538948
  41.0 0.9 %copy-start.5 = (bf16[2,8,32,768]{3,2,1,0:T(8,128)(2,1)}, bf16[2,8,32,768]{3,2,1,0:T(8,128)(2,1)S(1)}, u32[]{:S(2)}) copy-start(bf16[2,8,32,768]{3,2,1,0:T(8,128)(2,1)S(1)} %collective-permute-done.3.down_hbm) | copy-start | bytes 2359300

commit v4 on v1

v4 whole, which is shorter than its diff:
```python
import math

import jax
import jax.numpy as jnp
from jax import lax
from jax.experimental import pallas as pl
from jax.experimental.pallas import tpu as pltpu
from jax.sharding import PartitionSpec as P


HEAD_COUNT = 16
R = 8
STEP = 8
NEG = -1e30
GROUPS = 4
GROUP_HEADS = HEAD_COUNT // GROUPS
WIN = 256
WIN_START = (0, 128, 384, 512)
LOG2E = 1.4426950408889634
X = 4
KEYS = 4
SLOTS = 8
STATS = 3


def iota(shape, dim):
    return lax.broadcasted_iota(jnp.int32, shape, dim)


def pack_kernel(
    dil_hbm, seg_hbm, k_hbm, v_hbm, t_hbm, send_ref, right_ref, left_ref, ok_ref,
    k_ref, v_ref, t_ref, dil_ref, seg_ref, sem,
):
    rows, cols, width = k_ref.shape
    total_cols = t_ref.shape[1]
    dh = width // HEAD_COUNT
    slots = total_cols // cols * KEYS
    row0 = pl.multiple_of(lax.axis_index("row") * rows, rows)
    me_col = lax.axis_index("col")
    copies = [
        pltpu.make_async_copy(t_hbm.at[pl.ds(row0, rows), :], t_ref, sem.at[0]),
        pltpu.make_async_copy(k_hbm, k_ref, sem.at[1]),
        pltpu.make_async_copy(v_hbm, v_ref, sem.at[2]),
        pltpu.make_async_copy(dil_hbm, dil_ref, sem.at[3]),
        pltpu.make_async_copy(seg_hbm, seg_ref, sem.at[4]),
    ]
    for copy in copies:
        copy.start()
    slot = iota((total_cols, slots), 1)
    pick = iota((total_cols, slots), 0) == (slot // KEYS) * cols + (slot % 2) * STEP
    pick = jnp.where(pick, 1.0, 0.0).astype(jnp.bfloat16)
    sub = iota((STEP, total_cols), 0)
    copies[0].wait()
    live = []
    for rr in range(2):
        own = jnp.where(sub == me_col % X * 2 + rr, t_ref[...].astype(jnp.float32), 0.0)
        own = jnp.broadcast_to(jnp.sum(own, axis=0, keepdims=True), (STEP, total_cols))
        for bit in range(3):
            own = jnp.where((sub >> bit) & 1 == 1, pltpu.roll(own, total_cols - (1 << bit), 1), own)
        live.append(own)
    live = jnp.concatenate(live, axis=0).astype(jnp.bfloat16)
    live = jnp.dot(live, pick, preferred_element_type=jnp.float32)
    key_slot = iota((STEP, slots), 1)
    key_col = (key_slot // KEYS) * cols + (key_slot % 2) * STEP + iota((STEP, slots), 0)
    phase_id = iota((STEP, slots), 0)
    copies[3].wait()
    copies[4].wait()
    for half in range(HEAD_COUNT // STEP):
        dil = jnp.zeros((STEP, slots), jnp.int32)
        seg = jnp.zeros((STEP, slots), jnp.int32)
        for p in range(STEP):
            dil = jnp.where(phase_id == p, dil_ref[half * STEP + p], dil)
            seg = jnp.where(phase_id == p, seg_ref[half * STEP + p], seg)
        period = jnp.left_shift(STEP, dil) - 1
        shift = total_cols.bit_length() - 1 - seg
        head = phase_id + half * STEP
        ok = (key_col & period) == (head & period)
        ok = ok & (jnp.right_shift(key_col, shift) == jnp.right_shift(me_col // X * (X * cols), shift))
        for rr in range(2):
            good = ok & (key_slot % KEYS // 2 == rr) & (live[rr * STEP : (rr + 1) * STEP] > 0.5)
            at = (half * 2 + rr) * STEP
            ok_ref[at : at + STEP, :] = jnp.where(good, 1.0, 0.0)
    phase = (iota((STEP, width), 1) // dh) % STEP == iota((STEP, width), 0)
    sub = iota((STEP, width), 0)
    copies[1].wait()
    copies[2].wait()
    for i, ref in enumerate((k_ref, v_ref)):
        right_ref[i] = ref[:, cols - R :, :]
        left_ref[i] = ref[:, :R, :]
    for x in range(X):
        tile = jnp.zeros((SLOTS, width), jnp.float32)
        for i, ref in enumerate((k_ref, v_ref)):
            for rr in range(2):
                for j in range(2):
                    block = ref[2 * x + rr, j * STEP : (j + 1) * STEP, :].astype(jnp.float32)
                    picked = jnp.sum(jnp.where(phase, block, 0.0), axis=0, keepdims=True)
                    tile = jnp.where(sub == 4 * i + 2 * rr + j, picked, tile)
        tile = tile.astype(jnp.bfloat16)
        for z in range(send_ref.shape[0] // X):
            send_ref[z * X + x] = tile


NT = (((1,), (1,)), ((), ()))
TN = (((0,), (0,)), ((), ()))


def stacked_queries(q_ref, g):
    rows, cols, width = q_ref.shape
    dh = width // HEAD_COUNT
    w0 = WIN_START[g]
    off = g * GROUP_HEADS * dh - w0
    lane = iota((1, WIN), 1)
    q_win = q_ref[:, :, w0 : w0 + WIN].reshape(rows * cols, WIN)
    zero = jnp.zeros((), jnp.bfloat16)
    first = [off + hh * dh for hh in range(GROUP_HEADS)]
    return jnp.concatenate([jnp.where((lane >= f) & (lane < f + dh), q_win, zero) for f in first], axis=0)


def put_transposed(dst_ref, col, x):
    for tile in range(x.shape[1] // 128):
        part = x[:, tile * 128 : (tile + 1) * 128].astype(jnp.float32)
        dst_ref[tile * 128 : (tile + 1) * 128, col : col + x.shape[0]] = part.T.astype(dst_ref.dtype)


def dilated_kernel(q_ref, kv_ref, ok_ref, out_ref, s_ref, k_ref, vt_ref, ot_ref):
    two_x, cols, width = q_ref.shape
    queries = two_x * cols
    stacked = GROUP_HEADS * queries
    dh = width // HEAD_COUNT
    peers = kv_ref.shape[0]
    upper = iota((SLOTS, width), 0) >= KEYS
    values = []
    for pair in range(peers // 2):
        even = kv_ref[2 * pair].astype(jnp.float32)
        odd = kv_ref[2 * pair + 1].astype(jnp.float32)
        k_ref[pair * SLOTS : (pair + 1) * SLOTS, :] = jnp.where(upper, pltpu.roll(odd, KEYS, 0), even)
        values.append(jnp.where(upper, odd, pltpu.roll(even, KEYS, 0)))
    put_transposed(vt_ref, 0, jnp.concatenate(values, axis=0))
    for g in range(GROUPS):
        w0 = WIN_START[g]
        s_ref[:, g * stacked : (g + 1) * stacked] = lax.dot_general(
            k_ref[:, w0 : w0 + WIN].astype(jnp.bfloat16),
            stacked_queries(q_ref, g),
            NT,
            preferred_element_type=jnp.float32,
        )
    ok = ok_ref[...].astype(jnp.bfloat16)
    part = iota((ok.shape[0], queries), 0)
    odd_row = iota((ok.shape[0], queries), 1) // cols % 2
    lses = []
    for h in range(HEAD_COUNT):
        row = (h // STEP * 2 + odd_row) * STEP + h % STEP
        mine = jnp.where(part == row, 1.0, 0.0).astype(jnp.bfloat16)
        live = lax.dot_general(ok, mine, TN, preferred_element_type=jnp.float32)
        s = s_ref[:, h * queries : (h + 1) * queries] * (LOG2E / math.sqrt(dh))
        s = jnp.where(live > 0.5, s, NEG)
        top = jnp.maximum(jnp.max(s, axis=0, keepdims=True), 0.5 * NEG)
        p = jnp.exp2(s - top)
        total = jnp.sum(p, axis=0, keepdims=True)
        safe = jnp.maximum(total, 0.5)
        numer = jnp.dot(
            vt_ref[h * dh : (h + 1) * dh, :], p.astype(jnp.bfloat16), preferred_element_type=jnp.float32
        )
        ot_ref[h * dh : (h + 1) * dh, :] = numer * (1.0 / safe)
        lses.append(jnp.where(total > 0.0, top + jnp.log2(safe), NEG))
    lse = jnp.concatenate(lses, axis=0)
    first = lse.astype(jnp.bfloat16).astype(jnp.float32)
    second = (lse - first).astype(jnp.bfloat16).astype(jnp.float32)
    for i, piece in enumerate((first, second, lse - first - second)):
        ot_ref[width + i * HEAD_COUNT : width + (i + 1) * HEAD_COUNT, :] = piece
    ot_ref[width + STATS * HEAD_COUNT :, :] = jnp.zeros((128 - STATS * HEAD_COUNT, queries), jnp.float32)
    for tile in range(width // 128 + 1):
        at = slice(tile * 128, (tile + 1) * 128)
        out_ref[:, :, at] = ot_ref[at, :].T.astype(jnp.bfloat16).reshape(two_x, cols, 128)


def window_kernel(
    q_ref, up_hbm, own_ref, down_hbm, tissue_ref, out_ref, top_ref, total_ref,
    bias_ref, s_ref, vt_ref, up_ref, down_ref, sem,
):
    copies = [
        pltpu.make_async_copy(up_hbm, up_ref, sem.at[0]),
        pltpu.make_async_copy(down_hbm, down_ref, sem.at[1]),
    ]
    for copy in copies:
        copy.start()
    rows, cols, width = q_ref.shape
    queries = rows * cols
    stacked = GROUP_HEADS * queries
    dh = width // HEAD_COUNT
    wide = cols + 2 * R
    keys = rows * wide
    grid_rows, grid_cols = tissue_ref.shape
    row0, col0 = lax.axis_index("row") * rows, lax.axis_index("col") * cols
    k_id = iota((keys, queries), 0)
    q_id = iota((keys, queries), 1)
    q_row, q_col = q_id // cols, q_id % cols
    k_row, k_col = k_id // wide, k_id % wide - R
    near_cols = jnp.abs(k_col - q_col) <= R
    lane = iota((grid_cols, 128), 1)
    spread = (iota((grid_cols, 128), 0) == col0 - R + lane) & (lane < wide)
    spread = jnp.where(spread, 1.0, 0.0).astype(jnp.bfloat16)
    by_row = jnp.where(iota((keys, rows), 0) // wide == iota((keys, rows), 1), 1.0, 0.0).astype(jnp.bfloat16)
    own_lane = iota((keys, 128), 1) == iota((keys, 128), 0) % wide
    ones = jnp.ones((128, queries), jnp.bfloat16)
    stacks = [stacked_queries(q_ref, g) for g in range(GROUPS)]
    for b, ref in ((1, own_ref), (0, up_ref), (2, down_ref)):
        at_b = slice(b * keys, (b + 1) * keys)
        first = row0 + (b - 1) * rows
        inside = (first >= 0) & (first < grid_rows)
        at = pl.multiple_of(jnp.clip(first, 0, grid_rows - rows), rows)
        tiles = tissue_ref[pl.ds(at, rows), :].astype(jnp.float32).astype(jnp.bfloat16)
        tiles = jnp.dot(tiles, spread, preferred_element_type=jnp.float32).astype(jnp.bfloat16)
        live = jnp.dot(by_row, tiles, preferred_element_type=jnp.float32)
        live = jnp.where(own_lane, live, 0.0).astype(jnp.bfloat16)
        live = jnp.dot(live, ones, preferred_element_type=jnp.float32)
        ok = near_cols & (jnp.abs(k_row + (b - 1) * rows - q_row) <= R) & (live > 0.5) & inside
        if b == 1:
            ok = ok | ((k_row == q_row) & (k_col == q_col))
        bias_ref[at_b, :] = jnp.where(ok, 0.0, NEG)
        if b == 0:
            for copy in copies:
                copy.wait()
        for g in range(GROUPS):
            w0 = WIN_START[g]
            k_win = ref[0, :, :, w0 : w0 + WIN].reshape(keys, WIN)
            s_ref[at_b, g * stacked : (g + 1) * stacked] = lax.dot_general(
                k_win, stacks[g], NT, preferred_element_type=jnp.float32
            )
        put_transposed(vt_ref, b * keys, ref[1].reshape(keys, width))
    for h in range(HEAD_COUNT):
        s = s_ref[:, h * queries : (h + 1) * queries] * (LOG2E / math.sqrt(dh)) + bias_ref[...]
        top = jnp.max(s, axis=0, keepdims=True)
        p = jnp.exp2(s - top)
        top_ref[h : h + 1, :] = top
        total_ref[h : h + 1, :] = jnp.sum(p, axis=0, keepdims=True)
        out_ref[h * dh : (h + 1) * dh, :] = jnp.dot(
            vt_ref[h * dh : (h + 1) * dh, :], p.astype(jnp.bfloat16), preferred_element_type=jnp.float32
        )


def merge_kernel(win_ref, top_ref, total_ref, back_ref, weight_ref, out_ref, bt_ref, at_ref):
    rows, cols, width = out_ref.shape
    queries = rows * cols
    dh = width // HEAD_COUNT
    put_transposed(bt_ref, 0, back_ref[...].reshape(queries, width + 128))
    lse = bt_ref[width : width + HEAD_COUNT, :]
    for part in range(1, STATS):
        lse = lse + bt_ref[width + part * HEAD_COUNT : width + (part + 1) * HEAD_COUNT, :]
    top = top_ref[...]
    big = jnp.maximum(top, lse)
    a = jnp.exp2(top - big)
    b = jnp.exp2(lse - big)
    inverse = 1.0 / (a * total_ref[...] + b)
    a, b = a * inverse, b * inverse
    for h in range(HEAD_COUNT):
        at = slice(h * dh, (h + 1) * dh)
        mixed = a[h : h + 1] * win_ref[at, :] + b[h : h + 1] * bt_ref[at, :]
        at_ref[at, :] = mixed
    att = jnp.concatenate(
        [at_ref[t * 128 : (t + 1) * 128, :].T.astype(jnp.bfloat16) for t in range(width // 128)], axis=1
    )
    enc = jnp.dot(att, weight_ref[...], preferred_element_type=jnp.float32)
    out_ref[...] = enc.astype(jnp.bfloat16).reshape(out_ref.shape)


def call(kernel, out_shape, ins, scratch=(), flops=0):
    spaces = dict(v=pltpu.VMEM, h=pltpu.HBM)
    vmem = pl.BlockSpec(memory_space=pltpu.VMEM)
    many = isinstance(out_shape, (tuple, list))
    return pl.pallas_call(
        kernel,
        out_shape=out_shape,
        in_specs=[pl.BlockSpec(memory_space=spaces[c]) for c in ins],
        out_specs=[vmem] * len(out_shape) if many else vmem,
        scratch_shapes=list(scratch),
        cost_estimate=pl.CostEstimate(flops=flops, transcendentals=0, bytes_accessed=1 << 20),
        compiler_params=pltpu.CompilerParams(vmem_limit_bytes=24 << 20),
    )


def per_device(q, k, v, tissue, dilation_levels, segment_levels, weight):
    rows, cols, width = q.shape
    peers = lax.axis_size("col")
    n_row = lax.axis_size("row")
    bf16, f32 = jnp.bfloat16, jnp.float32
    shape, vmem = jax.ShapeDtypeStruct, pltpu.VMEM
    slots = peers * KEYS
    x_groups = [[z * X + x for x in range(X)] for z in range(peers // X)]
    half = shape((2, rows, R, width), bf16)
    hbm = [pltpu.with_memory_space_constraint(x, pltpu.HBM) for x in (dilation_levels, segment_levels, k, v, tissue)]
    q_x = lax.all_to_all(q, "col", 0, 0, tiled=True, axis_index_groups=x_groups)
    send, right, left, ok = call(
        pack_kernel,
        [shape((peers, SLOTS, width), bf16), half, half, shape((2 * HEAD_COUNT, slots), f32)],
        ins="hhhhh",
        scratch=[vmem((rows, cols, width), bf16)] * 2
        + [vmem((rows, tissue.shape[1]), jnp.int32)]
        + [pltpu.SMEM((HEAD_COUNT,), jnp.int32)] * 2
        + [pltpu.SemaphoreType.DMA((5,))],
    )(*hbm)
    got = lax.all_to_all(send, "col", 0, 0, tiled=True)
    up_c = [(i, i + 1) for i in range(peers - 1)]
    up_r = [(i, i + 1) for i in range(n_row - 1)]
    from_left = lax.ppermute(right, "col", up_c)
    from_right = lax.ppermute(left, "col", [(b, a) for a, b in up_c])
    own = jnp.concatenate([from_left, jnp.stack([k, v]), from_right], axis=2)
    above = lax.ppermute(own, "row", up_r)
    below = lax.ppermute(own, "row", [(b, a) for a, b in up_r])
    queries = rows * cols
    stack = HEAD_COUNT * queries
    back = call(
        dilated_kernel,
        shape((rows, cols, width + 128), bf16),
        ins="vvv",
        scratch=[
            vmem((slots, stack), f32),
            vmem((slots, width), f32),
            vmem((width, slots), bf16),
            vmem((width + 128, queries), f32),
        ],
        flops=1 << 31,
    )(q_x, got, ok)
    back = lax.all_to_all(back, "col", 0, 0, tiled=True, axis_index_groups=x_groups)
    keys = 3 * rows * (cols + 2 * R)
    above, below = (pltpu.with_memory_space_constraint(x, pltpu.HBM) for x in (above, below))
    per_head = shape((HEAD_COUNT, queries), f32)
    win, top, total = call(
        window_kernel,
        [shape((width, queries), f32), per_head, per_head],
        ins="vhvhv",
        scratch=[vmem((keys, queries), f32), vmem((keys, stack), f32), vmem((width, keys), bf16)]
        + [vmem(own.shape, bf16)] * 2
        + [pltpu.SemaphoreType.DMA((2,))],
        flops=1 << 32,
    )(q, above, own, below, tissue)
    return call(
        merge_kernel,
        shape((rows, cols, width), bf16),
        ins="v" * 5,
        scratch=[vmem((width + 128, queries), f32), vmem((width, queries), f32)],
        flops=1 << 28,
    )(win, top, total, back, weight)


def solution(mesh):
    spec = P("row", "col", None)
    return jax.shard_map(
        per_device,
        mesh=mesh,
        in_specs=(spec, spec, spec, P(), P(), P(), P()),
        out_specs=spec,
        check_vma=False,
    )
```

time: 60.3 us -> 61.7 us (1.023)
  the two profiles are of different devices: /device:TPU:8 before, /device:TPU:40 now
where the time goes in v4:
time: 61.7 us; the launch traced here: 61.2 us
  starting transfers between devices  26 us (42%)
  Pallas kernels  12.3 us (20%)
  blocking collectives  11.8 us (19%)
  waiting for transfers between devices  10.8 us (18%)
    all_to_all x1, starting transfers between devices, per_device(): got = lax.all_to_all(send, 'col', 0, 0, tiled=True)  13.6 us
    all_to_all x1, blocking collectives, per_device(): q_x = lax.all_to_all(q, 'col', 0, 0, tiled=True, axis_index_groups=x_groups)  11.8 us
    all_to_all x1, waiting for transfers between devices, per_device(): got = lax.all_to_all(send, 'col', 0, 0, tiled=True)  9.24 us
    pallas_call x1, Pallas kernels, per_device(): call(window_kernel, [shape((width, queries), f32), per_head, per_head], i...  4.83 us
    pallas_call x1, Pallas kernels, per_device(): call(dilated_kernel, shape((rows, cols, width + 128), bf16), ins='vvv', s...  4.08 us
    ppermute x1, starting transfers between devices, per_device(): from_left = lax.ppermute(right, 'col', up_c)  3.41 us
    all_to_all x1, starting transfers between devices, per_device(): lax.all_to_all(back, 'col', 0, 0, tiled=True, axis_index_groups=x_groups)  3.38 us
    ppermute x1, starting transfers between devices, per_device(): above = lax.ppermute(own, 'row', up_r)  2.41 us
  transfers between devices with their start and end apart: 6, of which 2 were waited for; matrix products, arithmetic and copies ran while one was open for 0% of the time, Pallas kernels for 15%

profile of v4, /device:TPU:40, one launch (start us, length us, event | category | flops | bytes accessed | tf_op | source)
XLA Modules:
  0.0 61.2 jit_solution(1495414911966836363)
XLA Ops:
  0.0 0.0 copy-start.4
  0.0 0.0 copy-start.3
  0.0 2.2 %shard_map.73 = (bf16[32,8,768]{2,1,0:T(8,128)(2,1)}, bf16[2,8,8,768]{3,2,1,0:T(8,128)(2,1)S(1)}, bf16[2,8,8,768]{3,2,1,0:T(8,128)(2,1)S(1)}, f32[32,128]{1,0:T(8,128)S(1)}) custom-call(s32[16]{0:T(128)} %dil_hbm.1, s32[16]{0:T(128)} %seg_hbm.1, bf16[8,16,768]{2,1,0:T(8,128)(2,1)} %k_hbm.1, bf16[8,16,768]{2,1,0:T(8,128)(2,1)} %v_hbm.1, s32[128,512]{1,0:T(8,128)} %tissue_ref.1), custom_call_target="tpu_custom_call" | custom-call | bytes 1048576 | tf_op jit(solution)/shard_map/pallas_call | solution.py:293
  2.2 3.4 %collective-permute-start = (bf16[2,8,8,768]{3,2,1,0:T(8,128)(2,1)S(1)}, bf16[2,8,8,768]{3,2,1,0:T(8,128)(2,1)S(1)}, u32[]{:S(2)}, u32[]{:S(2)}) collective-permute-start(bf16[2,8,8,768]{3,2,1,0:T(8,128)(2,1)S(1)} %get-tuple-element.12), channel_id=1, source_target_pairs={{0,1},{1,2},{2,3},{3,4},{4,5},{5,6},{6,7},{7,8},{8,9},{9,10},{10,1... | collective-permute-start | bytes 589832 | tf_op jit(solution)/shard_map/ppermute | solution.py:305
  5.6 1.3 %collective-permute-start.1 = (bf16[2,8,8,768]{3,2,1,0:T(8,128)(2,1)S(1)}, bf16[2,8,8,768]{3,2,1,0:T(8,128)(2,1)S(1)}, u32[]{:S(2)}, u32[]{:S(2)}) collective-permute-start(bf16[2,8,8,768]{3,2,1,0:T(8,128)(2,1)S(1)} %get-tuple-element.13), channel_id=1, source_target_pairs={{1,0},{2,1},{3,2},{4,3},{5,4},{6,5},{7,6},{8,7},{9,8},{10,9},{11,1... | collective-permute-start | bytes 589832 | tf_op jit(solution)/shard_map/ppermute | solution.py:306
  6.9 11.8 %all_to_all.15.q_ref = bf16[8,16,768]{2,1,0:T(8,128)(2,1)S(1)} all-to-all(bf16[8,16,768]{2,1,0:T(8,128)(2,1)} %q_ref.1), channel_id=1, replica_groups={{0,1,2,3},{4,5,6,7},{8,9,10,11},{12,13,14,15},{16,17,18,19},{20,21,22,2..., dimensions={0} | all-to-all | bytes 393216 | tf_op jit(solution)/shard_map/all_to_all | solution.py:292
  18.7 13.6 %all-to-all-start.1 = ((bf16[32,8,768]{2,1,0:T(8,128)(2,1)}), bf16[32,8,768]{2,1,0:T(8,128)(2,1)S(1)}, u32[]{:S(2)}, u32[]{:S(2)}) async-start(bf16[32,8,768]{2,1,0:T(8,128)(2,1)} %get-tuple-element.17), calls=%async_computation.1 | async-start | bytes 786432 | tf_op jit(solution)/shard_map/all_to_all | solution.py:302
  32.4 0.0 collective-permute-done
  32.4 0.0 collective-permute-done.1
  32.4 0.0 copy-done.4
  32.4 0.0 copy-done.3
  32.4 0.1 pad_maximum_fusion.own_ref
  32.5 1.9 %collective-permute-start.3 = (bf16[2,8,32,768]{3,2,1,0:T(8,128)(2,1)S(1)}, bf16[2,8,32,768]{3,2,1,0:T(8,128)(2,1)}, u32[]{:S(2)}, u32[]{:S(2)}) collective-permute-start(bf16[2,8,32,768]{3,2,1,0:T(8,128)(2,1)S(1)} %pad_maximum_fusion.own_ref), channel_id=1, source_target_pairs={{32,0},{64,32},{96,64},{128,96},{160,128},{192,160},{224,192},{256... | collective-permute-start | bytes 2359304 | tf_op jit(solution)/shard_map/ppermute | solution.py:309
  34.4 2.4 %collective-permute-start.2 = (bf16[2,8,32,768]{3,2,1,0:T(8,128)(2,1)S(1)}, bf16[2,8,32,768]{3,2,1,0:T(8,128)(2,1)}, u32[]{:S(2)}, u32[]{:S(2)}) collective-permute-start(bf16[2,8,32,768]{3,2,1,0:T(8,128)(2,1)S(1)} %pad_maximum_fusion.own_ref), channel_id=1, source_target_pairs={{0,32},{32,64},{64,96},{96,128},{128,160},{160,192},{192,224},{224... | collective-permute-start | bytes 2359304 | tf_op jit(solution)/shard_map/ppermute | solution.py:308
  36.8 9.2 %all-to-all-done.1.kv_ref = bf16[32,8,768]{2,1,0:T(8,128)(2,1)S(1)} async-done(((bf16[32,8,768]{2,1,0:T(8,128)(2,1)}), bf16[32,8,768]{2,1,0:T(8,128)(2,1)S(1)}, u32[]{:S(2)}, u32[]{:S(2)}) %all-to-all-start.1) | async-done | bytes 393248 | tf_op jit(solution)/shard_map/all_to_all | solution.py:302
  46.1 0.0 copy-start.1
  46.1 0.0 copy-start.2
  46.1 4.1 %shard_map.75 = bf16[8,16,896]{2,1,0:T(8,128)(2,1)} custom-call(bf16[8,16,768]{2,1,0:T(8,128)(2,1)S(1)} %all_to_all.15.q_ref, bf16[32,8,768]{2,1,0:T(8,128)(2,1)S(1)} %all-to-all-done.1.kv_ref, f32[32,128]{1,0:T(8,128)S(1)} %get-tuple-element.18.ok_ref), custom_call_target="tpu_custom_call" | custom-call | flops 2147483648 | bytes 1048576 | tf_op jit(solution)/shard_map/pallas_call | solution.py:312
  50.2 3.4 %all-to-all-start.2 = ((bf16[8,16,896]{2,1,0:T(8,128)(2,1)}), bf16[8,16,896]{2,1,0:T(8,128)(2,1)S(1)}, u32[]{:S(2)}, u32[]{:S(2)}) async-start(bf16[8,16,896]{2,1,0:T(8,128)(2,1)} %shard_map.75), calls=%async_computation.2 | async-start | bytes 458752 | tf_op jit(solution)/shard_map/all_to_all | solution.py:324
  53.6 0.0 copy-start
  53.6 0.0 collective-permute-done.3.down_hbm
  53.6 0.0 collective-permute-done.2.up_hbm
  53.6 0.0 copy-done.1
  53.6 0.0 copy-done.2
  53.6 4.8 %shard_map.74 = (f32[768,128]{1,0:T(8,128)S(1)}, f32[16,128]{1,0:T(8,128)S(1)}, f32[16,128]{1,0:T(8,128)S(1)}) custom-call(bf16[8,16,768]{2,1,0:T(8,128)(2,1)S(1)} %copy-done.2, bf16[2,8,32,768]{3,2,1,0:T(8,128)(2,1)} %collective-permute-done.2.up_hbm, bf16[2,8,32,768]{3,2,1,0:T(8,128)(2,1)S(1)} %pad_maximum_fusion.own_ref, ...), custom_call_target="tpu_custom_call" | custom-call | flops 4294967296 | bytes 1048576 | tf_op jit(solution)/shard_map/pallas_call | solution.py:328
  58.4 1.6 %all-to-all-done.2.back_ref = bf16[8,16,896]{2,1,0:T(8,128)(2,1)S(1)} async-done(((bf16[8,16,896]{2,1,0:T(8,128)(2,1)}), bf16[8,16,896]{2,1,0:T(8,128)(2,1)S(1)}, u32[]{:S(2)}, u32[]{:S(2)}) %all-to-all-start.2) | async-done | bytes 229408 | tf_op jit(solution)/shard_map/all_to_all | solution.py:324
  60.0 0.0 copy-done
  60.0 1.2 %shard_map.76 = bf16[8,16,768]{2,1,0:T(8,128)(2,1)} custom-call(f32[768,128]{1,0:T(8,128)S(1)} %get-tuple-element.14.win_ref, f32[16,128]{1,0:T(8,128)S(1)} %get-tuple-element.15.top_ref, f32[16,128]{1,0:T(8,128)S(1)} %get-tuple-element.16.total_ref, bf16[8,16,896]{2,1,0:T(8,128)(2,1)S(1)} %all-to-all-done.2.back_ref, bf16[768,768]{1,0:T(8,128)(2,1)S(1)} %copy-done), custom_call_target="tpu_custom_call" | custom-call | flops 268435456 | bytes 1048576 | tf_op jit(solution)/shard_map/pallas_call | solution.py:337
Async XLA Ops:
  0.0 32.4 %copy-start.4 = (bf16[8,16,768]{2,1,0:T(8,128)(2,1)S(1)}, bf16[8,16,768]{2,1,0:T(8,128)(2,1)}, u32[]{:S(2)}) copy-start(bf16[8,16,768]{2,1,0:T(8,128)(2,1)} %v_hbm.1) | copy-start | bytes 589828
  0.0 32.4 %copy-start.3 = (bf16[8,16,768]{2,1,0:T(8,128)(2,1)S(1)}, bf16[8,16,768]{2,1,0:T(8,128)(2,1)}, u32[]{:S(2)}) copy-start(bf16[8,16,768]{2,1,0:T(8,128)(2,1)} %k_hbm.1) | copy-start | bytes 589828
  2.2 30.1 %collective-permute-start = (bf16[2,8,8,768]{3,2,1,0:T(8,128)(2,1)S(1)}, bf16[2,8,8,768]{3,2,1,0:T(8,128)(2,1)S(1)}, u32[]{:S(2)}, u32[]{:S(2)}) collective-permute-start(bf16[2,8,8,768]{3,2,1,0:T(8,128)(2,1)S(1)} %get-tuple-element.12), channel_id=1, source_target_pairs={{0,1},{1,2},{2,3},{3,4},{4,5},{5,6},{6,7},{7,8},{8,9},{9,10},{10,1... | collective-permute-start | bytes 589832 | tf_op jit(solution)/shard_map/ppermute | solution.py:305
  5.6 26.7 %collective-permute-start.1 = (bf16[2,8,8,768]{3,2,1,0:T(8,128)(2,1)S(1)}, bf16[2,8,8,768]{3,2,1,0:T(8,128)(2,1)S(1)}, u32[]{:S(2)}, u32[]{:S(2)}) collective-permute-start(bf16[2,8,8,768]{3,2,1,0:T(8,128)(2,1)S(1)} %get-tuple-element.13), channel_id=1, source_target_pairs={{1,0},{2,1},{3,2},{4,3},{5,4},{6,5},{7,6},{8,7},{9,8},{10,9},{11,1... | collective-permute-start | bytes 589832 | tf_op jit(solution)/shard_map/ppermute | solution.py:306
  18.7 27.4 %all-to-all-start.1 = ((bf16[32,8,768]{2,1,0:T(8,128)(2,1)}), bf16[32,8,768]{2,1,0:T(8,128)(2,1)S(1)}, u32[]{:S(2)}, u32[]{:S(2)}) async-start(bf16[32,8,768]{2,1,0:T(8,128)(2,1)} %get-tuple-element.17), calls=%async_computation.1 | async-start | bytes 786432 | tf_op jit(solution)/shard_map/all_to_all | solution.py:302
  32.5 21.1 %collective-permute-start.3 = (bf16[2,8,32,768]{3,2,1,0:T(8,128)(2,1)S(1)}, bf16[2,8,32,768]{3,2,1,0:T(8,128)(2,1)}, u32[]{:S(2)}, u32[]{:S(2)}) collective-permute-start(bf16[2,8,32,768]{3,2,1,0:T(8,128)(2,1)S(1)} %pad_maximum_fusion.own_ref), channel_id=1, source_target_pairs={{32,0},{64,32},{96,64},{128,96},{160,128},{192,160},{224,192},{256... | collective-permute-start | bytes 2359304 | tf_op jit(solution)/shard_map/ppermute | solution.py:309
  34.4 19.2 %collective-permute-start.2 = (bf16[2,8,32,768]{3,2,1,0:T(8,128)(2,1)S(1)}, bf16[2,8,32,768]{3,2,1,0:T(8,128)(2,1)}, u32[]{:S(2)}, u32[]{:S(2)}) collective-permute-start(bf16[2,8,32,768]{3,2,1,0:T(8,128)(2,1)S(1)} %pad_maximum_fusion.own_ref), channel_id=1, source_target_pairs={{0,32},{32,64},{64,96},{96,128},{128,160},{160,192},{192,224},{224... | collective-permute-start | bytes 2359304 | tf_op jit(solution)/shard_map/ppermute | solution.py:308
  46.1 7.5 %copy-start.1 = (s32[128,512]{1,0:T(8,128)S(1)}, s32[128,512]{1,0:T(8,128)}, u32[]{:S(2)}) copy-start(s32[128,512]{1,0:T(8,128)} %tissue_ref.1) | copy-start | bytes 786436
  46.1 7.5 %copy-start.2 = (bf16[8,16,768]{2,1,0:T(8,128)(2,1)S(1)}, bf16[8,16,768]{2,1,0:T(8,128)(2,1)}, u32[]{:S(2)}) copy-start(bf16[8,16,768]{2,1,0:T(8,128)(2,1)} %q_ref.1) | copy-start | bytes 589828
  50.2 9.9 %all-to-all-start.2 = ((bf16[8,16,896]{2,1,0:T(8,128)(2,1)}), bf16[8,16,896]{2,1,0:T(8,128)(2,1)S(1)}, u32[]{:S(2)}, u32[]{:S(2)}) async-start(bf16[8,16,896]{2,1,0:T(8,128)(2,1)} %shard_map.75), calls=%async_computation.2 | async-start | bytes 458752 | tf_op jit(solution)/shard_map/all_to_all | solution.py:324
  53.6 6.5 %copy-start = (bf16[768,768]{1,0:T(8,128)(2,1)S(1)}, bf16[768,768]{1,0:T(8,128)(2,1)}, u32[]{:S(2)}) copy-start(bf16[768,768]{1,0:T(8,128)(2,1)} %weight_ref.1) | copy-start | bytes 3538948

commit v5 on v4

--- a/solution.py
+++ b/solution.py
@@ -1,3 +1,4 @@
+import functools
 import math
 
 import jax
@@ -60,6 +61,7 @@
         live.append(own)
     live = jnp.concatenate(live, axis=0).astype(jnp.bfloat16)
     live = jnp.dot(live, pick, preferred_element_type=jnp.float32)
+    ok_ref[...] = jnp.zeros(ok_ref.shape, jnp.float32)
     key_slot = iota((STEP, slots), 1)
     key_col = (key_slot // KEYS) * cols + (key_slot % 2) * STEP + iota((STEP, slots), 0)
     phase_id = iota((STEP, slots), 0)
@@ -79,7 +81,8 @@
         for rr in range(2):
             good = ok & (key_slot % KEYS // 2 == rr) & (live[rr * STEP : (rr + 1) * STEP] > 0.5)
             at = (half * 2 + rr) * STEP
-            ok_ref[at : at + STEP, :] = jnp.where(good, 1.0, 0.0)
+            for copy_at in (at, at + 64):
+                ok_ref[copy_at : copy_at + STEP, :] = jnp.where(good, 0.0, NEG)
     phase = (iota((STEP, width), 1) // dh) % STEP == iota((STEP, width), 0)
     sub = iota((STEP, width), 0)
     copies[1].wait()
@@ -101,7 +104,6 @@
 
 
 NT = (((1,), (1,)), ((), ()))
-TN = (((0,), (0,)), ((), ()))
 
 
 def stacked_queries(q_ref, g):
@@ -136,33 +138,41 @@
         k_ref[pair * SLOTS : (pair + 1) * SLOTS, :] = jnp.where(upper, pltpu.roll(odd, KEYS, 0), even)
         values.append(jnp.where(upper, odd, pltpu.roll(even, KEYS, 0)))
     put_transposed(vt_ref, 0, jnp.concatenate(values, axis=0))
+    penalty = ok_ref[...].T.astype(jnp.bfloat16)
+    lane = iota((1, 128), 1)
+    q_id = iota((stacked, 128), 0)
     for g in range(GROUPS):
         w0 = WIN_START[g]
+        head = g * GROUP_HEADS + q_id // queries
+        row = (head // STEP * 2 + q_id // cols % 2) * STEP + head % STEP
+        choose = jnp.where(lane % 64 == row, 1.0, 0.0).astype(jnp.bfloat16)
+        stack = stacked_queries(q_ref, g)
+        k_win = k_ref[:, w0 : w0 + WIN].astype(jnp.bfloat16)
+        if g % 2:
+            stack = jnp.concatenate([jnp.where(lane < 64, choose, stack[:, :128]), stack[:, 128:]], axis=1)
+            k_win = jnp.concatenate([jnp.where(lane < 64, penalty, k_win[:, :128]), k_win[:, 128:]], axis=1)
+        else:
+            stack = jnp.concatenate([stack[:, :128], jnp.where(lane < 64, stack[:, 128:], choose)], axis=1)
+            k_win = jnp.concatenate([k_win[:, :128], jnp.where(lane < 64, k_win[:, 128:], penalty)], axis=1)
         s_ref[:, g * stacked : (g + 1) * stacked] = lax.dot_general(
-            k_ref[:, w0 : w0 + WIN].astype(jnp.bfloat16),
-            stacked_queries(q_ref, g),
-            NT,
-            preferred_element_type=jnp.float32,
+            k_win, stack, NT, preferred_element_type=jnp.float32
         )
-    ok = ok_ref[...].astype(jnp.bfloat16)
-    part = iota((ok.shape[0], queries), 0)
-    odd_row = iota((ok.shape[0], queries), 1) // cols % 2
     lses = []
-    for h in range(HEAD_COUNT):
-        row = (h // STEP * 2 + odd_row) * STEP + h % STEP
-        mine = jnp.where(part == row, 1.0, 0.0).astype(jnp.bfloat16)
-        live = lax.dot_general(ok, mine, TN, preferred_element_type=jnp.float32)
-        s = s_ref[:, h * queries : (h + 1) * queries] * (LOG2E / math.sqrt(dh))
-        s = jnp.where(live > 0.5, s, NEG)
-        top = jnp.maximum(jnp.max(s, axis=0, keepdims=True), 0.5 * NEG)
+    for g in range(GROUPS):
+        s = s_ref[:, g * stacked : (g + 1) * stacked] * (LOG2E / math.sqrt(dh))
+        top = jnp.maximum(jnp.max(s, axis=0, keepdims=True), 0.1 * NEG)
         p = jnp.exp2(s - top)
         total = jnp.sum(p, axis=0, keepdims=True)
+        p = p.astype(jnp.bfloat16)
         safe = jnp.maximum(total, 0.5)
-        numer = jnp.dot(
-            vt_ref[h * dh : (h + 1) * dh, :], p.astype(jnp.bfloat16), preferred_element_type=jnp.float32
-        )
-        ot_ref[h * dh : (h + 1) * dh, :] = numer * (1.0 / safe)
-        lses.append(jnp.where(total > 0.0, top + jnp.log2(safe), NEG))
+        lse = jnp.where(total > 0.0, top + jnp.log2(safe), NEG)
+        inverse = 1.0 / safe
+        for hh in range(GROUP_HEADS):
+            h = g * GROUP_HEADS + hh
+            at = slice(hh * queries, (hh + 1) * queries)
+            numer = jnp.dot(vt_ref[h * dh : (h + 1) * dh, :], p[:, at], preferred_element_type=jnp.float32)
+            ot_ref[h * dh : (h + 1) * dh, :] = numer * inverse[:, at]
+            lses.append(lse[:, at])
     lse = jnp.concatenate(lses, axis=0)
     first = lse.astype(jnp.bfloat16).astype(jnp.float32)
     second = (lse - first).astype(jnp.bfloat16).astype(jnp.float32)
@@ -174,14 +184,16 @@
         out_ref[:, :, at] = ot_ref[at, :].T.astype(jnp.bfloat16).reshape(two_x, cols, 128)
 
 
-def window_kernel(
-    q_ref, up_hbm, own_ref, down_hbm, tissue_ref, out_ref, top_ref, total_ref,
-    bias_ref, s_ref, vt_ref, up_ref, down_ref, sem,
-):
-    copies = [
-        pltpu.make_async_copy(up_hbm, up_ref, sem.at[0]),
-        pltpu.make_async_copy(down_hbm, down_ref, sem.at[1]),
-    ]
+def window_kernel(*refs, blocks):
+    n = len(blocks)
+    q_ref, tissue_ref = refs[:2]
+    sources = refs[2 : 2 + n]
+    out_ref, top_ref, total_ref, bias_ref, s_ref, vt_ref = refs[2 + n : 8 + n]
+    copies = []
+    if len(refs) > 8 + n:
+        held = refs[8 + n : -1]
+        copies = [pltpu.make_async_copy(sources[i], held[i], refs[-1].at[i]) for i in range(n)]
+        sources = held
     for copy in copies:
         copy.start()
     rows, cols, width = q_ref.shape
@@ -204,9 +216,9 @@
     own_lane = iota((keys, 128), 1) == iota((keys, 128), 0) % wide
     ones = jnp.ones((128, queries), jnp.bfloat16)
     stacks = [stacked_queries(q_ref, g) for g in range(GROUPS)]
-    for b, ref in ((1, own_ref), (0, up_ref), (2, down_ref)):
-        at_b = slice(b * keys, (b + 1) * keys)
-        first = row0 + (b - 1) * rows
+    for i, (b, ref) in enumerate(zip(blocks, sources, strict=True)):
+        at_b = slice(i * keys, (i + 1) * keys)
+        first = row0 + b * rows
         inside = (first >= 0) & (first < grid_rows)
         at = pl.multiple_of(jnp.clip(first, 0, grid_rows - rows), rows)
         tiles = tissue_ref[pl.ds(at, rows), :].astype(jnp.float32).astype(jnp.bfloat16)
@@ -214,23 +226,22 @@
         live = jnp.dot(by_row, tiles, preferred_element_type=jnp.float32)
         live = jnp.where(own_lane, live, 0.0).astype(jnp.bfloat16)
         live = jnp.dot(live, ones, preferred_element_type=jnp.float32)
-        ok = near_cols & (jnp.abs(k_row + (b - 1) * rows - q_row) <= R) & (live > 0.5) & inside
-        if b == 1:
+        ok = near_cols & (jnp.abs(k_row + b * rows - q_row) <= R) & (live > 0.5) & inside
+        if b == 0:
             ok = ok | ((k_row == q_row) & (k_col == q_col))
         bias_ref[at_b, :] = jnp.where(ok, 0.0, NEG)
-        if b == 0:
-            for copy in copies:
-                copy.wait()
+        if copies:
+            copies[i].wait()
         for g in range(GROUPS):
             w0 = WIN_START[g]
             k_win = ref[0, :, :, w0 : w0 + WIN].reshape(keys, WIN)
             s_ref[at_b, g * stacked : (g + 1) * stacked] = lax.dot_general(
                 k_win, stacks[g], NT, preferred_element_type=jnp.float32
             )
-        put_transposed(vt_ref, b * keys, ref[1].reshape(keys, width))
+        put_transposed(vt_ref, i * keys, ref[1].reshape(keys, width))
     for h in range(HEAD_COUNT):
         s = s_ref[:, h * queries : (h + 1) * queries] * (LOG2E / math.sqrt(dh)) + bias_ref[...]
-        top = jnp.max(s, axis=0, keepdims=True)
+        top = jnp.maximum(jnp.max(s, axis=0, keepdims=True), 0.1 * NEG)
         p = jnp.exp2(s - top)
         top_ref[h : h + 1, :] = top
         total_ref[h : h + 1, :] = jnp.sum(p, axis=0, keepdims=True)
@@ -239,7 +250,10 @@
         )
 
 
-def merge_kernel(win_ref, top_ref, total_ref, back_ref, weight_ref, out_ref, bt_ref, at_ref):
+def merge_kernel(
+    own_ref, own_top_ref, own_total_ref, far_ref, far_top_ref, far_total_ref, back_ref, weight_ref, out_ref,
+    bt_ref, at_ref,
+):
     rows, cols, width = out_ref.shape
     queries = rows * cols
     dh = width // HEAD_COUNT
@@ -247,16 +261,16 @@
     lse = bt_ref[width : width + HEAD_COUNT, :]
     for part in range(1, STATS):
         lse = lse + bt_ref[width + part * HEAD_COUNT : width + (part + 1) * HEAD_COUNT, :]
-    top = top_ref[...]
-    big = jnp.maximum(top, lse)
-    a = jnp.exp2(top - big)
-    b = jnp.exp2(lse - big)
-    inverse = 1.0 / (a * total_ref[...] + b)
-    a, b = a * inverse, b * inverse
+    big = jnp.maximum(jnp.maximum(own_top_ref[...], far_top_ref[...]), lse)
+    a = jnp.exp2(own_top_ref[...] - big)
+    b = jnp.exp2(far_top_ref[...] - big)
+    c = jnp.exp2(lse - big)
+    inverse = 1.0 / (a * own_total_ref[...] + b * far_total_ref[...] + c)
+    a, b, c = a * inverse, b * inverse, c * inverse
     for h in range(HEAD_COUNT):
         at = slice(h * dh, (h + 1) * dh)
-        mixed = a[h : h + 1] * win_ref[at, :] + b[h : h + 1] * bt_ref[at, :]
-        at_ref[at, :] = mixed
+        one = slice(h, h + 1)
+        at_ref[at, :] = a[one] * own_ref[at, :] + b[one] * far_ref[at, :] + c[one] * bt_ref[at, :]
     att = jnp.concatenate(
         [at_ref[t * 128 : (t + 1) * 128, :].T.astype(jnp.bfloat16) for t in range(width // 128)], axis=1
     )
@@ -292,7 +306,7 @@
     q_x = lax.all_to_all(q, "col", 0, 0, tiled=True, axis_index_groups=x_groups)
     send, right, left, ok = call(
         pack_kernel,
-        [shape((peers, SLOTS, width), bf16), half, half, shape((2 * HEAD_COUNT, slots), f32)],
+        [shape((peers, SLOTS, width), bf16), half, half, shape((128, slots), f32)],
         ins="hhhhh",
         scratch=[vmem((rows, cols, width), bf16)] * 2
         + [vmem((rows, tissue.shape[1]), jnp.int32)]
@@ -322,25 +336,30 @@
         flops=1 << 31,
     )(q_x, got, ok)
     back = lax.all_to_all(back, "col", 0, 0, tiled=True, axis_index_groups=x_groups)
-    keys = 3 * rows * (cols + 2 * R)
+    keys = rows * (cols + 2 * R)
+    per_head = shape((HEAD_COUNT, queries), f32)
+
+    def window(blocks, sources, ins, extra=()):
+        n = len(blocks) * keys
+        return call(
+            functools.partial(window_kernel, blocks=blocks),
+            [shape((width, queries), f32), per_head, per_head],
+            ins="vv" + ins,
+            scratch=[vmem((n, queries), f32), vmem((n, stack), f32), vmem((width, n), bf16), *extra],
+            flops=len(blocks) << 31,
+        )(q, tissue, *sources)
+
+    own_parts = window((0,), (own,), "v")
     above, below = (pltpu.with_memory_space_constraint(x, pltpu.HBM) for x in (above, below))
-    per_head = shape((HEAD_COUNT, queries), f32)
-    win, top, total = call(
-        window_kernel,
-        [shape((width, queries), f32), per_head, per_head],
-        ins="vhvhv",
-        scratch=[vmem((keys, queries), f32), vmem((keys, stack), f32), vmem((width, keys), bf16)]
-        + [vmem(own.shape, bf16)] * 2
-        + [pltpu.SemaphoreType.DMA((2,))],
-        flops=1 << 32,
-    )(q, above, own, below, tissue)
+    extra = [vmem(own.shape, bf16)] * 2 + [pltpu.SemaphoreType.DMA((2,))]
+    far_parts = window((-1, 1), (above, below), "hh", extra)
     return call(
         merge_kernel,
         shape((rows, cols, width), bf16),
-        ins="v" * 5,
+        ins="v" * 8,
         scratch=[vmem((width + 128, queries), f32), vmem((width, queries), f32)],
         flops=1 << 28,
-    )(win, top, total, back, weight)
+    )(*own_parts, *far_parts, back, weight)
 
 
 def solution(mesh):

time: 61.7 us -> 59.7 us (0.968)
  the two profiles are of different devices: /device:TPU:40 before, /device:TPU:16 now
where the time goes in v5:
time: 59.7 us; the launch traced here: 59.2 us
  starting transfers between devices  26.2 us (44%)
  blocking collectives  11.8 us (20%)
  waiting for transfers between devices  10.9 us (18%)
  Pallas kernels  10.1 us (17%)
    all_to_all x1, starting transfers between devices, per_device(): got = lax.all_to_all(send, 'col', 0, 0, tiled=True)  13.8 us
    all_to_all x1, blocking collectives, per_device(): q_x = lax.all_to_all(q, 'col', 0, 0, tiled=True, axis_index_groups=x_groups)  11.8 us
    all_to_all x1, waiting for transfers between devices, per_device(): got = lax.all_to_all(send, 'col', 0, 0, tiled=True)  8.01 us
    pallas_call x2, Pallas kernels, window(): call(functools.partial(window_kernel, blocks=blocks), [shape((width, quer...  4.79 us
    ppermute x1, starting transfers between devices, per_device(): from_left = lax.ppermute(right, 'col', up_c)  3.41 us
    all_to_all x1, starting transfers between devices, per_device(): lax.all_to_all(back, 'col', 0, 0, tiled=True, axis_index_groups=x_groups)  3.38 us
    all_to_all x1, waiting for transfers between devices, per_device(): lax.all_to_all(back, 'col', 0, 0, tiled=True, axis_index_groups=x_groups)  2.85 us
    ppermute x1, starting transfers between devices, per_device(): above = lax.ppermute(own, 'row', up_r)  2.41 us
  transfers between devices with their start and end apart: 6, of which 2 were waited for; matrix products, arithmetic and copies ran while one was open for 0% of the time, Pallas kernels for 11%

profile of v5, /device:TPU:16, one launch (start us, length us, event | category | flops | bytes accessed | tf_op | source)
XLA Modules:
  0.0 59.2 jit_solution(4806351416293070013)
XLA Ops:
  0.0 0.0 copy-start.4
  0.0 0.0 copy-start.3
  0.0 2.2 %shard_map.73 = (bf16[32,8,768]{2,1,0:T(8,128)(2,1)}, bf16[2,8,8,768]{3,2,1,0:T(8,128)(2,1)S(1)}, bf16[2,8,8,768]{3,2,1,0:T(8,128)(2,1)S(1)}, f32[128,128]{1,0:T(8,128)S(1)}) custom-call(s32[16]{0:T(128)} %dil_hbm.1, s32[16]{0:T(128)} %seg_hbm.1, bf16[8,16,768]{2,1,0:T(8,128)(2,1)} %k_hbm.1, bf16[8,16,768]{2,1,0:T(8,128)(2,1)} %v_hbm.1, s32[128,512]{1,0:T(8,128)} %refs_1_.3), custom_call_target="tpu_custom_call" | custom-call | bytes 1048576 | tf_op jit(solution)/shard_map/pallas_call | solution.py:307
  2.2 3.4 %collective-permute-start = (bf16[2,8,8,768]{3,2,1,0:T(8,128)(2,1)S(1)}, bf16[2,8,8,768]{3,2,1,0:T(8,128)(2,1)S(1)}, u32[]{:S(2)}, u32[]{:S(2)}) collective-permute-start(bf16[2,8,8,768]{3,2,1,0:T(8,128)(2,1)S(1)} %get-tuple-element.15), channel_id=1, source_target_pairs={{0,1},{1,2},{2,3},{3,4},{4,5},{5,6},{6,7},{7,8},{8,9},{9,10},{10,1... | collective-permute-start | bytes 589832 | tf_op jit(solution)/shard_map/ppermute | solution.py:319
  5.6 1.3 %collective-permute-start.1 = (bf16[2,8,8,768]{3,2,1,0:T(8,128)(2,1)S(1)}, bf16[2,8,8,768]{3,2,1,0:T(8,128)(2,1)S(1)}, u32[]{:S(2)}, u32[]{:S(2)}) collective-permute-start(bf16[2,8,8,768]{3,2,1,0:T(8,128)(2,1)S(1)} %get-tuple-element.16), channel_id=1, source_target_pairs={{1,0},{2,1},{3,2},{4,3},{5,4},{6,5},{7,6},{8,7},{9,8},{10,9},{11,1... | collective-permute-start | bytes 589832 | tf_op jit(solution)/shard_map/ppermute | solution.py:320
  6.9 11.8 %all_to_all.15.q_ref = bf16[8,16,768]{2,1,0:T(8,128)(2,1)S(1)} all-to-all(bf16[8,16,768]{2,1,0:T(8,128)(2,1)} %refs_0_.3), channel_id=1, replica_groups={{0,1,2,3},{4,5,6,7},{8,9,10,11},{12,13,14,15},{16,17,18,19},{20,21,22,2..., dimensions={0} | all-to-all | bytes 393216 | tf_op jit(solution)/shard_map/all_to_all | solution.py:306
  18.7 0.0 copy-start.1
  18.7 0.0 copy-start.2
  18.7 13.8 %all-to-all-start.1 = ((bf16[32,8,768]{2,1,0:T(8,128)(2,1)}), bf16[32,8,768]{2,1,0:T(8,128)(2,1)S(1)}, u32[]{:S(2)}, u32[]{:S(2)}) async-start(bf16[32,8,768]{2,1,0:T(8,128)(2,1)} %get-tuple-element.23), calls=%async_computation.1 | async-start | bytes 786432 | tf_op jit(solution)/shard_map/all_to_all | solution.py:316
  32.5 0.0 collective-permute-done
  32.5 0.0 collective-permute-done.1
  32.5 0.0 copy-done.4
  32.5 0.0 copy-done.3
  32.5 0.1 pad_maximum_fusion.refs_2_
  32.6 1.9 %collective-permute-start.3 = (bf16[2,8,32,768]{3,2,1,0:T(8,128)(2,1)S(1)}, bf16[2,8,32,768]{3,2,1,0:T(8,128)(2,1)}, u32[]{:S(2)}, u32[]{:S(2)}) collective-permute-start(bf16[2,8,32,768]{3,2,1,0:T(8,128)(2,1)S(1)} %pad_maximum_fusion.refs_2_), channel_id=1, source_target_pairs={{32,0},{64,32},{96,64},{128,96},{160,128},{192,160},{224,192},{256... | collective-permute-start | bytes 2359304 | tf_op jit(solution)/shard_map/ppermute | solution.py:323
  34.6 2.4 %collective-permute-start.2 = (bf16[2,8,32,768]{3,2,1,0:T(8,128)(2,1)S(1)}, bf16[2,8,32,768]{3,2,1,0:T(8,128)(2,1)}, u32[]{:S(2)}, u32[]{:S(2)}) collective-permute-start(bf16[2,8,32,768]{3,2,1,0:T(8,128)(2,1)S(1)} %pad_maximum_fusion.refs_2_), channel_id=1, source_target_pairs={{0,32},{32,64},{64,96},{96,128},{128,160},{160,192},{192,224},{224... | collective-permute-start | bytes 2359304 | tf_op jit(solution)/shard_map/ppermute | solution.py:322
  37.0 0.0 copy-done.1
  37.0 0.0 copy-done.2
  37.0 1.2 %shard_map.74 = (f32[768,128]{1,0:T(8,128)S(1)}, f32[16,128]{1,0:T(8,128)S(1)}, f32[16,128]{1,0:T(8,128)S(1)}) custom-call(bf16[8,16,768]{2,1,0:T(8,128)(2,1)S(1)} %copy-done.2, s32[128,512]{1,0:T(8,128)S(1)} %copy-done.1, bf16[2,8,32,768]{3,2,1,0:T(8,128)(2,1)S(1)} %pad_maximum_fusion.refs_2_), custom_call_target="tpu_custom_call" | custom-call | flops 2147483648 | bytes 1048576 | tf_op jit(solution)/shard_map/pallas_call | solution.py:344
  38.2 8.0 %all-to-all-done.1.kv_ref = bf16[32,8,768]{2,1,0:T(8,128)(2,1)S(1)} async-done(((bf16[32,8,768]{2,1,0:T(8,128)(2,1)}), bf16[32,8,768]{2,1,0:T(8,128)(2,1)S(1)}, u32[]{:S(2)}, u32[]{:S(2)}) %all-to-all-start.1) | async-done | bytes 393248 | tf_op jit(solution)/shard_map/all_to_all | solution.py:316
  46.2 1.9 %shard_map.76 = bf16[8,16,896]{2,1,0:T(8,128)(2,1)} custom-call(bf16[8,16,768]{2,1,0:T(8,128)(2,1)S(1)} %all_to_all.15.q_ref, bf16[32,8,768]{2,1,0:T(8,128)(2,1)S(1)} %all-to-all-done.1.kv_ref, f32[128,128]{1,0:T(8,128)S(1)} %get-tuple-element.24.ok_ref), custom_call_target="tpu_custom_call" | custom-call | flops 2147483648 | bytes 1048576 | tf_op jit(solution)/shard_map/pallas_call | solution.py:326
  48.2 3.4 %all-to-all-start.2 = ((bf16[8,16,896]{2,1,0:T(8,128)(2,1)}), bf16[8,16,896]{2,1,0:T(8,128)(2,1)S(1)}, u32[]{:S(2)}, u32[]{:S(2)}) async-start(bf16[8,16,896]{2,1,0:T(8,128)(2,1)} %shard_map.76), calls=%async_computation.2 | async-start | bytes 458752 | tf_op jit(solution)/shard_map/all_to_all | solution.py:338
  51.5 0.0 copy-start
  51.6 0.0 collective-permute-done.3.refs_3_
  51.6 0.0 collective-permute-done.2.refs_2_
  51.6 3.6 %shard_map.75 = (f32[768,128]{1,0:T(8,128)S(1)}, f32[16,128]{1,0:T(8,128)S(1)}, f32[16,128]{1,0:T(8,128)S(1)}) custom-call(bf16[8,16,768]{2,1,0:T(8,128)(2,1)S(1)} %copy-done.2, s32[128,512]{1,0:T(8,128)S(1)} %copy-done.1, bf16[2,8,32,768]{3,2,1,0:T(8,128)(2,1)} %collective-permute-done.2.refs_2_, bf16[2,8,32,768]{3,2,1,0:T(8,128)(2,1)} %collective-permute-done.3.refs_3_), custom_call_target="tpu_custom_call" | custom-call | flops 4294967296 | bytes 1048576 | tf_op jit(solution)/shard_map/pallas_call | solution.py:344
  55.2 2.8 %all-to-all-done.2.back_ref = bf16[8,16,896]{2,1,0:T(8,128)(2,1)S(1)} async-done(((bf16[8,16,896]{2,1,0:T(8,128)(2,1)}), bf16[8,16,896]{2,1,0:T(8,128)(2,1)S(1)}, u32[]{:S(2)}, u32[]{:S(2)}) %all-to-all-start.2) | async-done | bytes 229408 | tf_op jit(solution)/shard_map/all_to_all | solution.py:338
  58.0 0.0 copy-done
  58.0 1.2 %shard_map.77 = bf16[8,16,768]{2,1,0:T(8,128)(2,1)} custom-call(f32[768,128]{1,0:T(8,128)S(1)} %get-tuple-element.17.own_ref, f32[16,128]{1,0:T(8,128)S(1)} %get-tuple-element.18.own_top_ref, f32[16,128]{1,0:T(8,128)S(1)} %get-tuple-element.19.own_total_ref, f32[768,128]{1,0:T(8,128)S(1)} %get-tuple-element.20.far_ref, ...), custom_call_target="tpu_custom_call" | custom-call | flops 268435456 | bytes 1048576 | tf_op jit(solution)/shard_map/pallas_call | solution.py:356
Async XLA Ops:
  0.0 32.5 %copy-start.4 = (bf16[8,16,768]{2,1,0:T(8,128)(2,1)S(1)}, bf16[8,16,768]{2,1,0:T(8,128)(2,1)}, u32[]{:S(2)}) copy-start(bf16[8,16,768]{2,1,0:T(8,128)(2,1)} %v_hbm.1) | copy-start | bytes 589828
  0.0 32.5 %copy-start.3 = (bf16[8,16,768]{2,1,0:T(8,128)(2,1)S(1)}, bf16[8,16,768]{2,1,0:T(8,128)(2,1)}, u32[]{:S(2)}) copy-start(bf16[8,16,768]{2,1,0:T(8,128)(2,1)} %k_hbm.1) | copy-start | bytes 589828
  2.2 30.3 %collective-permute-start = (bf16[2,8,8,768]{3,2,1,0:T(8,128)(2,1)S(1)}, bf16[2,8,8,768]{3,2,1,0:T(8,128)(2,1)S(1)}, u32[]{:S(2)}, u32[]{:S(2)}) collective-permute-start(bf16[2,8,8,768]{3,2,1,0:T(8,128)(2,1)S(1)} %get-tuple-element.15), channel_id=1, source_target_pairs={{0,1},{1,2},{2,3},{3,4},{4,5},{5,6},{6,7},{7,8},{8,9},{9,10},{10,1... | collective-permute-start | bytes 589832 | tf_op jit(solution)/shard_map/ppermute | solution.py:319
  5.6 26.9 %collective-permute-start.1 = (bf16[2,8,8,768]{3,2,1,0:T(8,128)(2,1)S(1)}, bf16[2,8,8,768]{3,2,1,0:T(8,128)(2,1)S(1)}, u32[]{:S(2)}, u32[]{:S(2)}) collective-permute-start(bf16[2,8,8,768]{3,2,1,0:T(8,128)(2,1)S(1)} %get-tuple-element.16), channel_id=1, source_target_pairs={{1,0},{2,1},{3,2},{4,3},{5,4},{6,5},{7,6},{8,7},{9,8},{10,9},{11,1... | collective-permute-start | bytes 589832 | tf_op jit(solution)/shard_map/ppermute | solution.py:320
  18.7 18.2 %copy-start.1 = (s32[128,512]{1,0:T(8,128)S(1)}, s32[128,512]{1,0:T(8,128)}, u32[]{:S(2)}) copy-start(s32[128,512]{1,0:T(8,128)} %refs_1_.3) | copy-start | bytes 786436
  18.7 18.3 %copy-start.2 = (bf16[8,16,768]{2,1,0:T(8,128)(2,1)S(1)}, bf16[8,16,768]{2,1,0:T(8,128)(2,1)}, u32[]{:S(2)}) copy-start(bf16[8,16,768]{2,1,0:T(8,128)(2,1)} %refs_0_.3) | copy-start | bytes 589828
  18.7 27.5 %all-to-all-start.1 = ((bf16[32,8,768]{2,1,0:T(8,128)(2,1)}), bf16[32,8,768]{2,1,0:T(8,128)(2,1)S(1)}, u32[]{:S(2)}, u32[]{:S(2)}) async-start(bf16[32,8,768]{2,1,0:T(8,128)(2,1)} %get-tuple-element.23), calls=%async_computation.1 | async-start | bytes 786432 | tf_op jit(solution)/shard_map/all_to_all | solution.py:316
  32.6 18.9 %collective-permute-start.3 = (bf16[2,8,32,768]{3,2,1,0:T(8,128)(2,1)S(1)}, bf16[2,8,32,768]{3,2,1,0:T(8,128)(2,1)}, u32[]{:S(2)}, u32[]{:S(2)}) collective-permute-start(bf16[2,8,32,768]{3,2,1,0:T(8,128)(2,1)S(1)} %pad_maximum_fusion.refs_2_), channel_id=1, source_target_pairs={{32,0},{64,32},{96,64},{128,96},{160,128},{192,160},{224,192},{256... | collective-permute-start | bytes 2359304 | tf_op jit(solution)/shard_map/ppermute | solution.py:323
  34.6 17.0 %collective-permute-start.2 = (bf16[2,8,32,768]{3,2,1,0:T(8,128)(2,1)S(1)}, bf16[2,8,32,768]{3,2,1,0:T(8,128)(2,1)}, u32[]{:S(2)}, u32[]{:S(2)}) collective-permute-start(bf16[2,8,32,768]{3,2,1,0:T(8,128)(2,1)S(1)} %pad_maximum_fusion.refs_2_), channel_id=1, source_target_pairs={{0,32},{32,64},{64,96},{96,128},{128,160},{160,192},{192,224},{224... | collective-permute-start | bytes 2359304 | tf_op jit(solution)/shard_map/ppermute | solution.py:322
  48.2 9.9 %all-to-all-start.2 = ((bf16[8,16,896]{2,1,0:T(8,128)(2,1)}), bf16[8,16,896]{2,1,0:T(8,128)(2,1)S(1)}, u32[]{:S(2)}, u32[]{:S(2)}) async-start(bf16[8,16,896]{2,1,0:T(8,128)(2,1)} %shard_map.76), calls=%async_computation.2 | async-start | bytes 458752 | tf_op jit(solution)/shard_map/all_to_all | solution.py:338
  51.5 6.5 %copy-start = (bf16[768,768]{1,0:T(8,128)(2,1)S(1)}, bf16[768,768]{1,0:T(8,128)(2,1)}, u32[]{:S(2)}) copy-start(bf16[768,768]{1,0:T(8,128)(2,1)} %weight_ref.1) | copy-start | bytes 3538948

commit v6 on v5

--- a/solution.py
+++ b/solution.py
@@ -29,8 +29,8 @@
 
 
 def pack_kernel(
-    dil_hbm, seg_hbm, k_hbm, v_hbm, t_hbm, send_ref, right_ref, left_ref, ok_ref,
-    k_ref, v_ref, t_ref, dil_ref, seg_ref, sem,
+    dil_hbm, seg_hbm, k_hbm, v_hbm, t_hbm, q_hbm, send_ref, right_ref, left_ref, ok_ref,
+    k_ref, v_ref, t_ref, dil_ref, seg_ref, q_ref, tile_ref, sem,
 ):
     rows, cols, width = k_ref.shape
     total_cols = t_ref.shape[1]
@@ -44,6 +44,10 @@
         pltpu.make_async_copy(v_hbm, v_ref, sem.at[2]),
         pltpu.make_async_copy(dil_hbm, dil_ref, sem.at[3]),
         pltpu.make_async_copy(seg_hbm, seg_ref, sem.at[4]),
+    ]
+    queries = q_hbm.shape[1]
+    copies += [
+        pltpu.make_async_copy(q_hbm, q_ref, sem.at[5]),
     ]
     for copy in copies:
         copy.start()
@@ -98,21 +102,27 @@
                     block = ref[2 * x + rr, j * STEP : (j + 1) * STEP, :].astype(jnp.float32)
                     picked = jnp.sum(jnp.where(phase, block, 0.0), axis=0, keepdims=True)
                     tile = jnp.where(sub == 4 * i + 2 * rr + j, picked, tile)
-        tile = tile.astype(jnp.bfloat16)
-        for z in range(send_ref.shape[0] // X):
-            send_ref[z * X + x] = tile
+        tile_ref[x] = tile.astype(jnp.bfloat16)
+        if x == 0:
+            copies[5].wait()
+            sends = [pltpu.make_async_copy(q_ref, send_ref.at[:, pl.ds(0, queries), :], sem.at[6])]
+            sends[0].start()
+    sends.append(pltpu.make_async_copy(tile_ref, send_ref.at[:, pl.ds(queries, SLOTS), :], sem.at[7]))
+    sends[1].start()
+    for copy in sends:
+        copy.wait()
 
 
 NT = (((1,), (1,)), ((), ()))
 
 
-def stacked_queries(q_ref, g):
-    rows, cols, width = q_ref.shape
+def stacked_queries(q_ref, g, take):
+    rows, cols, width = q_ref.shape[0], take, q_ref.shape[2]
     dh = width // HEAD_COUNT
     w0 = WIN_START[g]
     off = g * GROUP_HEADS * dh - w0
     lane = iota((1, WIN), 1)
-    q_win = q_ref[:, :, w0 : w0 + WIN].reshape(rows * cols, WIN)
+    q_win = q_ref[:, :take, w0 : w0 + WIN].reshape(rows * cols, WIN)
     zero = jnp.zeros((), jnp.bfloat16)
     first = [off + hh * dh for hh in range(GROUP_HEADS)]
     return jnp.concatenate([jnp.where((lane >= f) & (lane < f + dh), q_win, zero) for f in first], axis=0)
@@ -125,7 +135,7 @@
 
 
 def dilated_kernel(q_ref, kv_ref, ok_ref, out_ref, s_ref, k_ref, vt_ref, ot_ref):
-    two_x, cols, width = q_ref.shape
+    two_x, cols, width = out_ref.shape[0], out_ref.shape[1], q_ref.shape[2]
     queries = two_x * cols
     stacked = GROUP_HEADS * queries
     dh = width // HEAD_COUNT
@@ -140,13 +150,17 @@
     put_transposed(vt_ref, 0, jnp.concatenate(values, axis=0))
     penalty = ok_ref[...].T.astype(jnp.bfloat16)
     lane = iota((1, 128), 1)
-    q_id = iota((stacked, 128), 0)
+    second = iota((queries, 128), 0) // cols % 2 == 1
     for g in range(GROUPS):
         w0 = WIN_START[g]
-        head = g * GROUP_HEADS + q_id // queries
-        row = (head // STEP * 2 + q_id // cols % 2) * STEP + head % STEP
-        choose = jnp.where(lane % 64 == row, 1.0, 0.0).astype(jnp.bfloat16)
-        stack = stacked_queries(q_ref, g)
+        choose = []
+        for head in range(g * GROUP_HEADS, (g + 1) * GROUP_HEADS):
+            row = head // STEP * 2 * STEP + head % STEP
+            one = (jnp.where(lane % 64 == row + rr * STEP, 1.0, 0.0) for rr in range(2))
+            zero, one = (jnp.broadcast_to(x, (queries, 128)) for x in one)
+            choose.append(jnp.where(second, one, zero).astype(jnp.bfloat16))
+        choose = jnp.concatenate(choose, axis=0)
+        stack = stacked_queries(q_ref, g, 2 * cols)
         k_win = k_ref[:, w0 : w0 + WIN].astype(jnp.bfloat16)
         if g % 2:
             stack = jnp.concatenate([jnp.where(lane < 64, choose, stack[:, :128]), stack[:, 128:]], axis=1)
@@ -215,7 +229,7 @@
     by_row = jnp.where(iota((keys, rows), 0) // wide == iota((keys, rows), 1), 1.0, 0.0).astype(jnp.bfloat16)
     own_lane = iota((keys, 128), 1) == iota((keys, 128), 0) % wide
     ones = jnp.ones((128, queries), jnp.bfloat16)
-    stacks = [stacked_queries(q_ref, g) for g in range(GROUPS)]
+    stacks = [stacked_queries(q_ref, g, cols) for g in range(GROUPS)]
     for i, (b, ref) in enumerate(zip(blocks, sources, strict=True)):
         at_b = slice(i * keys, (i + 1) * keys)
         first = row0 + b * rows
@@ -278,15 +292,16 @@
     out_ref[...] = enc.astype(jnp.bfloat16).reshape(out_ref.shape)
 
 
-def call(kernel, out_shape, ins, scratch=(), flops=0):
+def call(kernel, out_shape, ins, scratch=(), flops=0, outs=None):
     spaces = dict(v=pltpu.VMEM, h=pltpu.HBM)
-    vmem = pl.BlockSpec(memory_space=pltpu.VMEM)
     many = isinstance(out_shape, (tuple, list))
     return pl.pallas_call(
         kernel,
         out_shape=out_shape,
         in_specs=[pl.BlockSpec(memory_space=spaces[c]) for c in ins],
-        out_specs=[vmem] * len(out_shape) if many else vmem,
+        out_specs=[pl.BlockSpec(memory_space=spaces[c]) for c in outs or "v" * len(out_shape)]
+        if many
+        else pl.BlockSpec(memory_space=pltpu.VMEM),
         scratch_shapes=list(scratch),
         cost_estimate=pl.CostEstimate(flops=flops, transcendentals=0, bytes_accessed=1 << 20),
         compiler_params=pltpu.CompilerParams(vmem_limit_bytes=24 << 20),
@@ -303,17 +318,21 @@
     x_groups = [[z * X + x for x in range(X)] for z in range(peers // X)]
     half = shape((2, rows, R, width), bf16)
     hbm = [pltpu.with_memory_space_constraint(x, pltpu.HBM) for x in (dilation_levels, segment_levels, k, v, tissue)]
-    q_x = lax.all_to_all(q, "col", 0, 0, tiled=True, axis_index_groups=x_groups)
+    hbm.append(pltpu.with_memory_space_constraint(q.reshape(X, 2 * cols, width), pltpu.HBM))
     send, right, left, ok = call(
         pack_kernel,
-        [shape((peers, SLOTS, width), bf16), half, half, shape((128, slots), f32)],
-        ins="hhhhh",
+        [shape((X, 2 * cols + SLOTS, width), bf16), half, half, shape((128, slots), f32)],
+        ins="hhhhhh",
+        outs="hvvv",
         scratch=[vmem((rows, cols, width), bf16)] * 2
         + [vmem((rows, tissue.shape[1]), jnp.int32)]
         + [pltpu.SMEM((HEAD_COUNT,), jnp.int32)] * 2
-        + [pltpu.SemaphoreType.DMA((5,))],
+        + [vmem((X, 2 * cols, width), bf16), vmem((X, SLOTS, width), bf16), pltpu.SemaphoreType.DMA((8,))],
     )(*hbm)
-    got = lax.all_to_all(send, "col", 0, 0, tiled=True)
+    stripe = lax.all_to_all(send, "col", 0, 0, tiled=True, axis_index_groups=x_groups)
+    z_groups = [[z * X + x for z in range(peers // X)] for x in range(X)]
+    got = jnp.broadcast_to(stripe[None, :, 2 * cols :], (peers // X, X, SLOTS, width))
+    got = lax.all_to_all(got.reshape(peers, SLOTS, width), "col", 0, 0, tiled=True, axis_index_groups=z_groups)
     up_c = [(i, i + 1) for i in range(peers - 1)]
     up_r = [(i, i + 1) for i in range(n_row - 1)]
     from_left = lax.ppermute(right, "col", up_c)
@@ -334,7 +353,7 @@
             vmem((width + 128, queries), f32),
         ],
         flops=1 << 31,
-    )(q_x, got, ok)
+    )(stripe, got, ok)
     back = lax.all_to_all(back, "col", 0, 0, tiled=True, axis_index_groups=x_groups)
     keys = rows * (cols + 2 * R)
     per_head = shape((HEAD_COUNT, queries), f32)

time: 59.7 us -> 57.7 us (0.966)
  the two profiles are of different devices: /device:TPU:16 before, /device:TPU:40 now
where the time goes in v6:
time: 57.7 us; the launch traced here: 57.3 us
  starting transfers between devices  25.1 us (44%)
  blocking collectives  11.8 us (20%)
  waiting for transfers between devices  10.2 us (18%)
  Pallas kernels  9.16 us (16%)
  local copies, waits for them, and re-layouts  0.8 us (1%)
    all_to_all x1, starting transfers between devices, per_device(): lax.all_to_all(got.reshape(peers, SLOTS, width), 'col', 0, 0, tiled=True,...  12 us
    all_to_all x1, blocking collectives, per_device(): lax.all_to_all(send, 'col', 0, 0, tiled=True, axis_index_groups=x_groups)  11.8 us
    all_to_all x1, waiting for transfers between devices, per_device(): lax.all_to_all(got.reshape(peers, SLOTS, width), 'col', 0, 0, tiled=True,...  7.27 us
    pallas_call x2, Pallas kernels, window(): call(functools.partial(window_kernel, blocks=blocks), [shape((width, quer...  4.79 us
    all_to_all x1, starting transfers between devices, per_device(): lax.all_to_all(back, 'col', 0, 0, tiled=True, axis_index_groups=x_groups)  4.09 us
    ppermute x1, starting transfers between devices, per_device(): from_left = lax.ppermute(right, 'col', up_c)  3.41 us
    all_to_all x1, waiting for transfers between devices, per_device(): lax.all_to_all(back, 'col', 0, 0, tiled=True, axis_index_groups=x_groups)  2.9 us
    ppermute x1, starting transfers between devices, per_device(): above = lax.ppermute(own, 'row', up_r)  2.41 us
  transfers between devices with their start and end apart: 6, of which 2 were waited for; matrix products, arithmetic and copies ran while one was open for 1% of the time, Pallas kernels for 11%

profile of v6, /device:TPU:40, one launch (start us, length us, event | category | flops | bytes accessed | tf_op | source)
XLA Modules:
  0.0 57.3 jit_solution(17521408060737762479)
XLA Ops:
  0.0 0.0 copy-start.3
  0.0 0.0 copy-start.4
  0.0 1.6 %shard_map.73 = (bf16[4,40,768]{2,1,0:T(8,128)(2,1)S(1)}, bf16[2,8,8,768]{3,2,1,0:T(8,128)(2,1)S(1)}, bf16[2,8,8,768]{3,2,1,0:T(8,128)(2,1)S(1)}, f32[128,128]{1,0:T(8,128)S(1)}) custom-call(s32[16]{0:T(128)} %dil_hbm.1, s32[16]{0:T(128)} %seg_hbm.1, bf16[8,16,768]{2,1,0:T(8,128)(2,1)} %k_hbm.1, bf16[8,16,768]{2,1,0:T(8,128)(2,1)} %v_hbm.1, ...), custom_call_target="tpu_custom_call" | custom-call | bytes 1048576 | tf_op jit(solution)/shard_map/pallas_call | solution.py:322
  1.6 3.4 %collective-permute-start = (bf16[2,8,8,768]{3,2,1,0:T(8,128)(2,1)S(1)}, bf16[2,8,8,768]{3,2,1,0:T(8,128)(2,1)S(1)}, u32[]{:S(2)}, u32[]{:S(2)}) collective-permute-start(bf16[2,8,8,768]{3,2,1,0:T(8,128)(2,1)S(1)} %get-tuple-element.15), channel_id=1, source_target_pairs={{0,1},{1,2},{2,3},{3,4},{4,5},{5,6},{6,7},{7,8},{8,9},{9,10},{10,1... | collective-permute-start | bytes 589832 | tf_op jit(solution)/shard_map/ppermute | solution.py:338
  5.0 1.3 %collective-permute-start.1 = (bf16[2,8,8,768]{3,2,1,0:T(8,128)(2,1)S(1)}, bf16[2,8,8,768]{3,2,1,0:T(8,128)(2,1)S(1)}, u32[]{:S(2)}, u32[]{:S(2)}) collective-permute-start(bf16[2,8,8,768]{3,2,1,0:T(8,128)(2,1)S(1)} %get-tuple-element.16), channel_id=1, source_target_pairs={{1,0},{2,1},{3,2},{4,3},{5,4},{6,5},{7,6},{8,7},{9,8},{10,9},{11,1... | collective-permute-start | bytes 589832 | tf_op jit(solution)/shard_map/ppermute | solution.py:339
  6.3 11.8 %all_to_all.15.q_ref = bf16[4,40,768]{2,1,0:T(8,128)(2,1)S(1)} all-to-all(bf16[4,40,768]{2,1,0:T(8,128)(2,1)S(1)} %get-tuple-element.23), channel_id=1, replica_groups={{0,1,2,3},{4,5,6,7},{8,9,10,11},{12,13,14,15},{16,17,18,19},{20,21,22,2..., dimensions={0} | all-to-all | bytes 491520 | tf_op jit(solution)/shard_map/all_to_all | solution.py:332
  18.2 0.8 %broadcast_in_dim.2 = bf16[8,4,8,768]{3,2,1,0:T(8,128)(2,1)} broadcast(bf16[4,8,768]{2,1,0:T(8,128)(2,1)S(1)} %slice.4), dimensions={1,2,3} | broadcast | bytes 442368 | tf_op jit(solution)/shard_map/broadcast_in_dim | solution.py:334
  18.9 0.0 copy-start.1
  18.9 0.0 copy-start.2
  18.9 12.0 %all-to-all-start.1 = ((bf16[32,8,768]{2,1,0:T(8,128)(2,1)}), bf16[32,8,768]{2,1,0:T(8,128)(2,1)S(1)}, u32[]{:S(2)}, u32[]{:S(2)}) async-start(bf16[32,8,768]{2,1,0:T(8,128)(2,1)} %bitcast.3), calls=%async_computation.1 | async-start | bytes 786432 | tf_op jit(solution)/shard_map/all_to_all | solution.py:335
  30.9 0.0 collective-permute-done
  31.0 0.0 collective-permute-done.1
  31.0 0.0 copy-done.3
  31.0 0.0 copy-done.4
  31.0 0.1 pad_maximum_fusion.refs_2_
  31.1 1.9 %collective-permute-start.3 = (bf16[2,8,32,768]{3,2,1,0:T(8,128)(2,1)S(1)}, bf16[2,8,32,768]{3,2,1,0:T(8,128)(2,1)}, u32[]{:S(2)}, u32[]{:S(2)}) collective-permute-start(bf16[2,8,32,768]{3,2,1,0:T(8,128)(2,1)S(1)} %pad_maximum_fusion.refs_2_), channel_id=1, source_target_pairs={{32,0},{64,32},{96,64},{128,96},{160,128},{192,160},{224,192},{256... | collective-permute-start | bytes 2359304 | tf_op jit(solution)/shard_map/ppermute | solution.py:342
  33.0 2.4 %collective-permute-start.2 = (bf16[2,8,32,768]{3,2,1,0:T(8,128)(2,1)S(1)}, bf16[2,8,32,768]{3,2,1,0:T(8,128)(2,1)}, u32[]{:S(2)}, u32[]{:S(2)}) collective-permute-start(bf16[2,8,32,768]{3,2,1,0:T(8,128)(2,1)S(1)} %pad_maximum_fusion.refs_2_), channel_id=1, source_target_pairs={{0,32},{32,64},{64,96},{96,128},{128,160},{160,192},{192,224},{224... | collective-permute-start | bytes 2359304 | tf_op jit(solution)/shard_map/ppermute | solution.py:341
  35.4 0.0 copy-done.1
  35.4 0.0 copy-done.2
  35.4 1.2 %shard_map.74 = (f32[768,128]{1,0:T(8,128)S(1)}, f32[16,128]{1,0:T(8,128)S(1)}, f32[16,128]{1,0:T(8,128)S(1)}) custom-call(bf16[8,16,768]{2,1,0:T(8,128)(2,1)S(1)} %copy-done.2, s32[128,512]{1,0:T(8,128)S(1)} %copy-done.1, bf16[2,8,32,768]{3,2,1,0:T(8,128)(2,1)S(1)} %pad_maximum_fusion.refs_2_), custom_call_target="tpu_custom_call" | custom-call | flops 2147483648 | bytes 1048576 | tf_op jit(solution)/shard_map/pallas_call | solution.py:363
  36.7 7.3 %all-to-all-done.1.kv_ref = bf16[32,8,768]{2,1,0:T(8,128)(2,1)S(1)} async-done(((bf16[32,8,768]{2,1,0:T(8,128)(2,1)}), bf16[32,8,768]{2,1,0:T(8,128)(2,1)S(1)}, u32[]{:S(2)}, u32[]{:S(2)}) %all-to-all-start.1) | async-done | bytes 393248 | tf_op jit(solution)/shard_map/all_to_all | solution.py:335
  43.9 1.6 %shard_map.76 = bf16[8,16,896]{2,1,0:T(8,128)(2,1)} custom-call(bf16[4,40,768]{2,1,0:T(8,128)(2,1)S(1)} %all_to_all.15.q_ref, bf16[32,8,768]{2,1,0:T(8,128)(2,1)S(1)} %all-to-all-done.1.kv_ref, f32[128,128]{1,0:T(8,128)S(1)} %get-tuple-element.24.ok_ref), custom_call_target="tpu_custom_call" | custom-call | flops 2147483648 | bytes 1048576 | tf_op jit(solution)/shard_map/pallas_call | solution.py:345
  45.5 4.1 %all-to-all-start.2 = ((bf16[8,16,896]{2,1,0:T(8,128)(2,1)}), bf16[8,16,896]{2,1,0:T(8,128)(2,1)S(1)}, u32[]{:S(2)}, u32[]{:S(2)}) async-start(bf16[8,16,896]{2,1,0:T(8,128)(2,1)} %shard_map.76), calls=%async_computation.2 | async-start | bytes 458752 | tf_op jit(solution)/shard_map/all_to_all | solution.py:357
  49.6 0.0 copy-start
  49.6 0.0 collective-permute-done.3.refs_3_
  49.6 0.0 collective-permute-done.2.refs_2_
  49.6 3.6 %shard_map.75 = (f32[768,128]{1,0:T(8,128)S(1)}, f32[16,128]{1,0:T(8,128)S(1)}, f32[16,128]{1,0:T(8,128)S(1)}) custom-call(bf16[8,16,768]{2,1,0:T(8,128)(2,1)S(1)} %copy-done.2, s32[128,512]{1,0:T(8,128)S(1)} %copy-done.1, bf16[2,8,32,768]{3,2,1,0:T(8,128)(2,1)} %collective-permute-done.2.refs_2_, bf16[2,8,32,768]{3,2,1,0:T(8,128)(2,1)} %collective-permute-done.3.refs_3_), custom_call_target="tpu_custom_call" | custom-call | flops 4294967296 | bytes 1048576 | tf_op jit(solution)/shard_map/pallas_call | solution.py:363
  53.2 2.9 %all-to-all-done.2.back_ref = bf16[8,16,896]{2,1,0:T(8,128)(2,1)S(1)} async-done(((bf16[8,16,896]{2,1,0:T(8,128)(2,1)}), bf16[8,16,896]{2,1,0:T(8,128)(2,1)S(1)}, u32[]{:S(2)}, u32[]{:S(2)}) %all-to-all-start.2) | async-done | bytes 229408 | tf_op jit(solution)/shard_map/all_to_all | solution.py:357
  56.1 0.0 copy-done
  56.1 1.2 %shard_map.77 = bf16[8,16,768]{2,1,0:T(8,128)(2,1)} custom-call(f32[768,128]{1,0:T(8,128)S(1)} %get-tuple-element.17.own_ref, f32[16,128]{1,0:T(8,128)S(1)} %get-tuple-element.18.own_top_ref, f32[16,128]{1,0:T(8,128)S(1)} %get-tuple-element.19.own_total_ref, f32[768,128]{1,0:T(8,128)S(1)} %get-tuple-element.20.far_ref, ...), custom_call_target="tpu_custom_call" | custom-call | flops 268435456 | bytes 1048576 | tf_op jit(solution)/shard_map/pallas_call | solution.py:375
  (1 shorter events, 0.0 us)
Async XLA Ops:
  0.0 31.0 %copy-start.3 = (bf16[8,16,768]{2,1,0:T(8,128)(2,1)S(1)}, bf16[8,16,768]{2,1,0:T(8,128)(2,1)}, u32[]{:S(2)}) copy-start(bf16[8,16,768]{2,1,0:T(8,128)(2,1)} %k_hbm.1) | copy-start | bytes 589828
  0.0 31.0 %copy-start.4 = (bf16[8,16,768]{2,1,0:T(8,128)(2,1)S(1)}, bf16[8,16,768]{2,1,0:T(8,128)(2,1)}, u32[]{:S(2)}) copy-start(bf16[8,16,768]{2,1,0:T(8,128)(2,1)} %v_hbm.1) | copy-start | bytes 589828
  1.6 29.4 %collective-permute-start = (bf16[2,8,8,768]{3,2,1,0:T(8,128)(2,1)S(1)}, bf16[2,8,8,768]{3,2,1,0:T(8,128)(2,1)S(1)}, u32[]{:S(2)}, u32[]{:S(2)}) collective-permute-start(bf16[2,8,8,768]{3,2,1,0:T(8,128)(2,1)S(1)} %get-tuple-element.15), channel_id=1, source_target_pairs={{0,1},{1,2},{2,3},{3,4},{4,5},{5,6},{6,7},{7,8},{8,9},{9,10},{10,1... | collective-permute-start | bytes 589832 | tf_op jit(solution)/shard_map/ppermute | solution.py:338
  5.0 25.9 %collective-permute-start.1 = (bf16[2,8,8,768]{3,2,1,0:T(8,128)(2,1)S(1)}, bf16[2,8,8,768]{3,2,1,0:T(8,128)(2,1)S(1)}, u32[]{:S(2)}, u32[]{:S(2)}) collective-permute-start(bf16[2,8,8,768]{3,2,1,0:T(8,128)(2,1)S(1)} %get-tuple-element.16), channel_id=1, source_target_pairs={{1,0},{2,1},{3,2},{4,3},{5,4},{6,5},{7,6},{8,7},{9,8},{10,9},{11,1... | collective-permute-start | bytes 589832 | tf_op jit(solution)/shard_map/ppermute | solution.py:339
  18.9 16.5 %copy-start.1 = (s32[128,512]{1,0:T(8,128)S(1)}, s32[128,512]{1,0:T(8,128)}, u32[]{:S(2)}) copy-start(s32[128,512]{1,0:T(8,128)} %refs_1_.3) | copy-start | bytes 786436
  18.9 16.5 %copy-start.2 = (bf16[8,16,768]{2,1,0:T(8,128)(2,1)S(1)}, bf16[8,16,768]{2,1,0:T(8,128)(2,1)}, u32[]{:S(2)}) copy-start(bf16[8,16,768]{2,1,0:T(8,128)(2,1)} %refs_0_.3) | copy-start | bytes 589828
  18.9 25.0 %all-to-all-start.1 = ((bf16[32,8,768]{2,1,0:T(8,128)(2,1)}), bf16[32,8,768]{2,1,0:T(8,128)(2,1)S(1)}, u32[]{:S(2)}, u32[]{:S(2)}) async-start(bf16[32,8,768]{2,1,0:T(8,128)(2,1)} %bitcast.3), calls=%async_computation.1 | async-start | bytes 786432 | tf_op jit(solution)/shard_map/all_to_all | solution.py:335
  31.1 18.6 %collective-permute-start.3 = (bf16[2,8,32,768]{3,2,1,0:T(8,128)(2,1)S(1)}, bf16[2,8,32,768]{3,2,1,0:T(8,128)(2,1)}, u32[]{:S(2)}, u32[]{:S(2)}) collective-permute-start(bf16[2,8,32,768]{3,2,1,0:T(8,128)(2,1)S(1)} %pad_maximum_fusion.refs_2_), channel_id=1, source_target_pairs={{32,0},{64,32},{96,64},{128,96},{160,128},{192,160},{224,192},{256... | collective-permute-start | bytes 2359304 | tf_op jit(solution)/shard_map/ppermute | solution.py:342
  33.0 16.6 %collective-permute-start.2 = (bf16[2,8,32,768]{3,2,1,0:T(8,128)(2,1)S(1)}, bf16[2,8,32,768]{3,2,1,0:T(8,128)(2,1)}, u32[]{:S(2)}, u32[]{:S(2)}) collective-permute-start(bf16[2,8,32,768]{3,2,1,0:T(8,128)(2,1)S(1)} %pad_maximum_fusion.refs_2_), channel_id=1, source_target_pairs={{0,32},{32,64},{64,96},{96,128},{128,160},{160,192},{192,224},{224... | collective-permute-start | bytes 2359304 | tf_op jit(solution)/shard_map/ppermute | solution.py:341
  45.5 10.6 %all-to-all-start.2 = ((bf16[8,16,896]{2,1,0:T(8,128)(2,1)}), bf16[8,16,896]{2,1,0:T(8,128)(2,1)S(1)}, u32[]{:S(2)}, u32[]{:S(2)}) async-start(bf16[8,16,896]{2,1,0:T(8,128)(2,1)} %shard_map.76), calls=%async_computation.2 | async-start | bytes 458752 | tf_op jit(solution)/shard_map/all_to_all | solution.py:357
  49.6 6.5 %copy-start = (bf16[768,768]{1,0:T(8,128)(2,1)S(1)}, bf16[768,768]{1,0:T(8,128)(2,1)}, u32[]{:S(2)}) copy-start(bf16[768,768]{1,0:T(8,128)(2,1)} %weight_ref.1) | copy-start | bytes 3538948

commit v7 on v6

--- a/solution.py
+++ b/solution.py
@@ -29,7 +29,7 @@
 
 
 def pack_kernel(
-    dil_hbm, seg_hbm, k_hbm, v_hbm, t_hbm, q_hbm, send_ref, right_ref, left_ref, ok_ref,
+    dil_hbm, seg_hbm, k_hbm, v_hbm, t_hbm, q_hbm, send_ref, first_ref, second_ref, ok_ref,
     k_ref, v_ref, t_ref, dil_ref, seg_ref, q_ref, tile_ref, sem,
 ):
     rows, cols, width = k_ref.shape
@@ -91,9 +91,6 @@
     sub = iota((STEP, width), 0)
     copies[1].wait()
     copies[2].wait()
-    for i, ref in enumerate((k_ref, v_ref)):
-        right_ref[i] = ref[:, cols - R :, :]
-        left_ref[i] = ref[:, :R, :]
     for x in range(X):
         tile = jnp.zeros((SLOTS, width), jnp.float32)
         for i, ref in enumerate((k_ref, v_ref)):
@@ -109,6 +106,10 @@
             sends[0].start()
     sends.append(pltpu.make_async_copy(tile_ref, send_ref.at[:, pl.ds(queries, SLOTS), :], sem.at[7]))
     sends[1].start()
+    for i, ref in enumerate((k_ref, v_ref)):
+        right, left = ref[:, cols - R :, :], ref[:, :R, :]
+        first_ref[i] = jnp.where(me_col % 2 == 0, right, left)
+        second_ref[i] = jnp.where(me_col % 2 == 0, left, right)
     for copy in sends:
         copy.wait()
 
@@ -221,10 +222,16 @@
     k_id = iota((keys, queries), 0)
     q_id = iota((keys, queries), 1)
     q_row, q_col = q_id // cols, q_id % cols
-    k_row, k_col = k_id // wide, k_id % wide - R
+    turn = lax.axis_index("col") % 2 * (wide - R)
+
+    def column(at):
+        return at - R + jnp.where(at < R, turn, 0) - jnp.where(at >= wide - R, turn, 0)
+
+    side = 1 - lax.axis_index("row") % 2 * 2
+    k_row, k_col = k_id // wide, column(k_id % wide)
     near_cols = jnp.abs(k_col - q_col) <= R
     lane = iota((grid_cols, 128), 1)
-    spread = (iota((grid_cols, 128), 0) == col0 - R + lane) & (lane < wide)
+    spread = (iota((grid_cols, 128), 0) == col0 + column(lane)) & (lane < wide)
     spread = jnp.where(spread, 1.0, 0.0).astype(jnp.bfloat16)
     by_row = jnp.where(iota((keys, rows), 0) // wide == iota((keys, rows), 1), 1.0, 0.0).astype(jnp.bfloat16)
     own_lane = iota((keys, 128), 1) == iota((keys, 128), 0) % wide
@@ -232,6 +239,7 @@
     stacks = [stacked_queries(q_ref, g, cols) for g in range(GROUPS)]
     for i, (b, ref) in enumerate(zip(blocks, sources, strict=True)):
         at_b = slice(i * keys, (i + 1) * keys)
+        b = b * side
         first = row0 + b * rows
         inside = (first >= 0) & (first < grid_rows)
         at = pl.multiple_of(jnp.clip(first, 0, grid_rows - rows), rows)
@@ -241,7 +249,7 @@
         live = jnp.where(own_lane, live, 0.0).astype(jnp.bfloat16)
         live = jnp.dot(live, ones, preferred_element_type=jnp.float32)
         ok = near_cols & (jnp.abs(k_row + b * rows - q_row) <= R) & (live > 0.5) & inside
-        if b == 0:
+        if blocks[i] == 0:
             ok = ok | ((k_row == q_row) & (k_col == q_col))
         bias_ref[at_b, :] = jnp.where(ok, 0.0, NEG)
         if copies:
@@ -308,6 +316,11 @@
     )
 
 
+def partners(count, first):
+    low = range(first, count - 1, 2)
+    return [(i, i + 1) for i in low] + [(i + 1, i) for i in low]
+
+
 def per_device(q, k, v, tissue, dilation_levels, segment_levels, weight):
     rows, cols, width = q.shape
     peers = lax.axis_size("col")
@@ -319,7 +332,7 @@
     half = shape((2, rows, R, width), bf16)
     hbm = [pltpu.with_memory_space_constraint(x, pltpu.HBM) for x in (dilation_levels, segment_levels, k, v, tissue)]
     hbm.append(pltpu.with_memory_space_constraint(q.reshape(X, 2 * cols, width), pltpu.HBM))
-    send, right, left, ok = call(
+    send, first, second, ok = call(
         pack_kernel,
         [shape((X, 2 * cols + SLOTS, width), bf16), half, half, shape((128, slots), f32)],
         ins="hhhhhh",
@@ -333,13 +346,11 @@
     z_groups = [[z * X + x for z in range(peers // X)] for x in range(X)]
     got = jnp.broadcast_to(stripe[None, :, 2 * cols :], (peers // X, X, SLOTS, width))
     got = lax.all_to_all(got.reshape(peers, SLOTS, width), "col", 0, 0, tiled=True, axis_index_groups=z_groups)
-    up_c = [(i, i + 1) for i in range(peers - 1)]
-    up_r = [(i, i + 1) for i in range(n_row - 1)]
-    from_left = lax.ppermute(right, "col", up_c)
-    from_right = lax.ppermute(left, "col", [(b, a) for a, b in up_c])
-    own = jnp.concatenate([from_left, jnp.stack([k, v]), from_right], axis=2)
-    above = lax.ppermute(own, "row", up_r)
-    below = lax.ppermute(own, "row", [(b, a) for a, b in up_r])
+    from_first = lax.ppermute(first, "col", partners(peers, 0))
+    from_second = lax.ppermute(second, "col", partners(peers, 1))
+    own = jnp.concatenate([from_second, jnp.stack([k, v]), from_first], axis=2)
+    above = lax.ppermute(own, "row", partners(n_row, 0))
+    below = lax.ppermute(own, "row", partners(n_row, 1))
     queries = rows * cols
     stack = HEAD_COUNT * queries
     back = call(
@@ -371,7 +382,7 @@
     own_parts = window((0,), (own,), "v")
     above, below = (pltpu.with_memory_space_constraint(x, pltpu.HBM) for x in (above, below))
     extra = [vmem(own.shape, bf16)] * 2 + [pltpu.SemaphoreType.DMA((2,))]
-    far_parts = window((-1, 1), (above, below), "hh", extra)
+    far_parts = window((1, -1), (above, below), "hh", extra)
     return call(
         merge_kernel,
         shape((rows, cols, width), bf16),

time: 57.7 us -> 55.7 us (0.965)
  the two profiles are of different devices: /device:TPU:40 before, /device:TPU:48 now
where the time goes in v7:
time: 55.7 us; the launch traced here: 55.3 us
  starting transfers between devices  24.3 us (44%)
  blocking collectives  11.2 us (20%)
  waiting for transfers between devices  9.54 us (17%)
  Pallas kernels  9.21 us (17%)
  local copies, waits for them, and re-layouts  0.8 us (1%)
    all_to_all x1, blocking collectives, per_device(): lax.all_to_all(send, 'col', 0, 0, tiled=True, axis_index_groups=x_groups)  11.2 us
    all_to_all x1, starting transfers between devices, per_device(): lax.all_to_all(got.reshape(peers, SLOTS, width), 'col', 0, 0, tiled=True,...  9.54 us
    all_to_all x1, waiting for transfers between devices, per_device(): lax.all_to_all(got.reshape(peers, SLOTS, width), 'col', 0, 0, tiled=True,...  6.68 us
    ppermute x1, starting transfers between devices, per_device(): from_first = lax.ppermute(first, 'col', partners(peers, 0))  6.13 us
    pallas_call x2, Pallas kernels, window(): call(functools.partial(window_kernel, blocks=blocks), [shape((width, quer...  4.81 us
    all_to_all x1, starting transfers between devices, per_device(): lax.all_to_all(back, 'col', 0, 0, tiled=True, axis_index_groups=x_groups)  3.38 us
    all_to_all x1, waiting for transfers between devices, per_device(): lax.all_to_all(back, 'col', 0, 0, tiled=True, axis_index_groups=x_groups)  2.85 us
    ppermute x1, starting transfers between devices, per_device(): above = lax.ppermute(own, 'row', partners(n_row, 0))  2.69 us
  transfers between devices with their start and end apart: 6, of which 2 were waited for; matrix products, arithmetic and copies ran while one was open for 2% of the time, Pallas kernels for 12%

profile of v7, /device:TPU:48, one launch (start us, length us, event | category | flops | bytes accessed | tf_op | source)
XLA Modules:
  0.0 55.3 jit_solution(13369619825982722242)
XLA Ops:
  0.0 0.0 copy-start.3
  0.0 0.0 copy-start.4
  0.0 1.6 %shard_map.73 = (bf16[4,40,768]{2,1,0:T(8,128)(2,1)S(1)}, bf16[2,8,8,768]{3,2,1,0:T(8,128)(2,1)S(1)}, bf16[2,8,8,768]{3,2,1,0:T(8,128)(2,1)S(1)}, f32[128,128]{1,0:T(8,128)S(1)}) custom-call(s32[16]{0:T(128)} %dil_hbm.1, s32[16]{0:T(128)} %seg_hbm.1, bf16[8,16,768]{2,1,0:T(8,128)(2,1)} %k_hbm.1, bf16[8,16,768]{2,1,0:T(8,128)(2,1)} %v_hbm.1, ...), custom_call_target="tpu_custom_call" | custom-call | bytes 1048576 | tf_op jit(solution)/shard_map/pallas_call | solution.py:335
  1.6 0.7 %collective-permute-start = (bf16[2,8,8,768]{3,2,1,0:T(8,128)(2,1)S(1)}, bf16[2,8,8,768]{3,2,1,0:T(8,128)(2,1)S(1)}, u32[]{:S(2)}, u32[]{:S(2)}) collective-permute-start(bf16[2,8,8,768]{3,2,1,0:T(8,128)(2,1)S(1)} %get-tuple-element.15), channel_id=1, source_target_pairs={{1,2},{3,4},{5,6},{7,8},{9,10},{11,12},{13,14},{15,16},{17,18},{19... | collective-permute-start | bytes 589832 | tf_op jit(solution)/shard_map/ppermute | solution.py:350
  2.3 6.1 %collective-permute-start.1 = (bf16[2,8,8,768]{3,2,1,0:T(8,128)(2,1)S(1)}, bf16[2,8,8,768]{3,2,1,0:T(8,128)(2,1)S(1)}, u32[]{:S(2)}, u32[]{:S(2)}) collective-permute-start(bf16[2,8,8,768]{3,2,1,0:T(8,128)(2,1)S(1)} %get-tuple-element.16), channel_id=1, source_target_pairs={{0,1},{2,3},{4,5},{6,7},{8,9},{10,11},{12,13},{14,15},{16,17},{18,... | collective-permute-start | bytes 589832 | tf_op jit(solution)/shard_map/ppermute | solution.py:349
  8.4 11.2 %all_to_all.15.q_ref = bf16[4,40,768]{2,1,0:T(8,128)(2,1)S(1)} all-to-all(bf16[4,40,768]{2,1,0:T(8,128)(2,1)S(1)} %get-tuple-element.23), channel_id=1, replica_groups={{0,1,2,3},{4,5,6,7},{8,9,10,11},{12,13,14,15},{16,17,18,19},{20,21,22,2..., dimensions={0} | all-to-all | bytes 491520 | tf_op jit(solution)/shard_map/all_to_all | solution.py:345
  19.6 0.8 %broadcast_in_dim.2 = bf16[8,4,8,768]{3,2,1,0:T(8,128)(2,1)} broadcast(bf16[4,8,768]{2,1,0:T(8,128)(2,1)S(1)} %slice.4), dimensions={1,2,3} | broadcast | bytes 442368 | tf_op jit(solution)/shard_map/broadcast_in_dim | solution.py:347
  20.4 0.0 copy-start.1
  20.4 0.0 copy-start.2
  20.4 9.5 %all-to-all-start.1 = ((bf16[32,8,768]{2,1,0:T(8,128)(2,1)}), bf16[32,8,768]{2,1,0:T(8,128)(2,1)S(1)}, u32[]{:S(2)}, u32[]{:S(2)}) async-start(bf16[32,8,768]{2,1,0:T(8,128)(2,1)} %bitcast.3), calls=%async_computation.1 | async-start | bytes 786432 | tf_op jit(solution)/shard_map/all_to_all | solution.py:348
  29.9 0.0 collective-permute-done
  30.0 0.0 collective-permute-done.1
  30.0 0.0 copy-done.3
  30.0 0.0 copy-done.4
  30.0 0.1 pad_maximum_fusion.refs_2_
  30.1 1.9 %collective-permute-start.3 = (bf16[2,8,32,768]{3,2,1,0:T(8,128)(2,1)S(1)}, bf16[2,8,32,768]{3,2,1,0:T(8,128)(2,1)}, u32[]{:S(2)}, u32[]{:S(2)}) collective-permute-start(bf16[2,8,32,768]{3,2,1,0:T(8,128)(2,1)S(1)} %pad_maximum_fusion.refs_2_), channel_id=1, source_target_pairs={{32,64},{96,128},{160,192},{224,256},{288,320},{352,384},{416,448}... | collective-permute-start | bytes 2359304 | tf_op jit(solution)/shard_map/ppermute | solution.py:353
  32.0 2.7 %collective-permute-start.2 = (bf16[2,8,32,768]{3,2,1,0:T(8,128)(2,1)S(1)}, bf16[2,8,32,768]{3,2,1,0:T(8,128)(2,1)}, u32[]{:S(2)}, u32[]{:S(2)}) collective-permute-start(bf16[2,8,32,768]{3,2,1,0:T(8,128)(2,1)S(1)} %pad_maximum_fusion.refs_2_), channel_id=1, source_target_pairs={{0,32},{64,96},{128,160},{192,224},{256,288},{320,352},{384,416},{... | collective-permute-start | bytes 2359304 | tf_op jit(solution)/shard_map/ppermute | solution.py:352
  34.7 0.0 copy-done.1
  34.7 0.0 copy-done.2
  34.7 1.2 %shard_map.74 = (f32[768,128]{1,0:T(8,128)S(1)}, f32[16,128]{1,0:T(8,128)S(1)}, f32[16,128]{1,0:T(8,128)S(1)}) custom-call(bf16[8,16,768]{2,1,0:T(8,128)(2,1)S(1)} %copy-done.2, s32[128,512]{1,0:T(8,128)S(1)} %copy-done.1, bf16[2,8,32,768]{3,2,1,0:T(8,128)(2,1)S(1)} %pad_maximum_fusion.refs_2_), custom_call_target="tpu_custom_call" | custom-call | flops 2147483648 | bytes 1048576 | tf_op jit(solution)/shard_map/pallas_call | solution.py:374
  36.0 6.7 %all-to-all-done.1.kv_ref = bf16[32,8,768]{2,1,0:T(8,128)(2,1)S(1)} async-done(((bf16[32,8,768]{2,1,0:T(8,128)(2,1)}), bf16[32,8,768]{2,1,0:T(8,128)(2,1)S(1)}, u32[]{:S(2)}, u32[]{:S(2)}) %all-to-all-start.1) | async-done | bytes 393248 | tf_op jit(solution)/shard_map/all_to_all | solution.py:348
  42.6 1.6 %shard_map.76 = bf16[8,16,896]{2,1,0:T(8,128)(2,1)} custom-call(bf16[4,40,768]{2,1,0:T(8,128)(2,1)S(1)} %all_to_all.15.q_ref, bf16[32,8,768]{2,1,0:T(8,128)(2,1)S(1)} %all-to-all-done.1.kv_ref, f32[128,128]{1,0:T(8,128)S(1)} %get-tuple-element.24.ok_ref), custom_call_target="tpu_custom_call" | custom-call | flops 2147483648 | bytes 1048576 | tf_op jit(solution)/shard_map/pallas_call | solution.py:356
  44.3 3.4 %all-to-all-start.2 = ((bf16[8,16,896]{2,1,0:T(8,128)(2,1)}), bf16[8,16,896]{2,1,0:T(8,128)(2,1)S(1)}, u32[]{:S(2)}, u32[]{:S(2)}) async-start(bf16[8,16,896]{2,1,0:T(8,128)(2,1)} %shard_map.76), calls=%async_computation.2 | async-start | bytes 458752 | tf_op jit(solution)/shard_map/all_to_all | solution.py:368
  47.6 0.0 copy-start
  47.7 0.0 collective-permute-done.3.refs_3_
  47.7 0.0 collective-permute-done.2.refs_2_
  47.7 3.6 %shard_map.75 = (f32[768,128]{1,0:T(8,128)S(1)}, f32[16,128]{1,0:T(8,128)S(1)}, f32[16,128]{1,0:T(8,128)S(1)}) custom-call(bf16[8,16,768]{2,1,0:T(8,128)(2,1)S(1)} %copy-done.2, s32[128,512]{1,0:T(8,128)S(1)} %copy-done.1, bf16[2,8,32,768]{3,2,1,0:T(8,128)(2,1)} %collective-permute-done.2.refs_2_, bf16[2,8,32,768]{3,2,1,0:T(8,128)(2,1)} %collective-permute-done.3.refs_3_), custom_call_target="tpu_custom_call" | custom-call | flops 4294967296 | bytes 1048576 | tf_op jit(solution)/shard_map/pallas_call | solution.py:374
  51.3 2.9 %all-to-all-done.2.back_ref = bf16[8,16,896]{2,1,0:T(8,128)(2,1)S(1)} async-done(((bf16[8,16,896]{2,1,0:T(8,128)(2,1)}), bf16[8,16,896]{2,1,0:T(8,128)(2,1)S(1)}, u32[]{:S(2)}, u32[]{:S(2)}) %all-to-all-start.2) | async-done | bytes 229408 | tf_op jit(solution)/shard_map/all_to_all | solution.py:368
  54.1 0.0 copy-done
  54.1 1.2 %shard_map.77 = bf16[8,16,768]{2,1,0:T(8,128)(2,1)} custom-call(f32[768,128]{1,0:T(8,128)S(1)} %get-tuple-element.17.own_ref, f32[16,128]{1,0:T(8,128)S(1)} %get-tuple-element.18.own_top_ref, f32[16,128]{1,0:T(8,128)S(1)} %get-tuple-element.19.own_total_ref, f32[768,128]{1,0:T(8,128)S(1)} %get-tuple-element.20.far_ref, ...), custom_call_target="tpu_custom_call" | custom-call | flops 268435456 | bytes 1048576 | tf_op jit(solution)/shard_map/pallas_call | solution.py:386
  (1 shorter events, 0.0 us)
Async XLA Ops:
  0.0 30.0 %copy-start.3 = (bf16[8,16,768]{2,1,0:T(8,128)(2,1)S(1)}, bf16[8,16,768]{2,1,0:T(8,128)(2,1)}, u32[]{:S(2)}) copy-start(bf16[8,16,768]{2,1,0:T(8,128)(2,1)} %k_hbm.1) | copy-start | bytes 589828
  0.0 30.0 %copy-start.4 = (bf16[8,16,768]{2,1,0:T(8,128)(2,1)S(1)}, bf16[8,16,768]{2,1,0:T(8,128)(2,1)}, u32[]{:S(2)}) copy-start(bf16[8,16,768]{2,1,0:T(8,128)(2,1)} %v_hbm.1) | copy-start | bytes 589828
  1.6 28.3 %collective-permute-start = (bf16[2,8,8,768]{3,2,1,0:T(8,128)(2,1)S(1)}, bf16[2,8,8,768]{3,2,1,0:T(8,128)(2,1)S(1)}, u32[]{:S(2)}, u32[]{:S(2)}) collective-permute-start(bf16[2,8,8,768]{3,2,1,0:T(8,128)(2,1)S(1)} %get-tuple-element.15), channel_id=1, source_target_pairs={{1,2},{3,4},{5,6},{7,8},{9,10},{11,12},{13,14},{15,16},{17,18},{19... | collective-permute-start | bytes 589832 | tf_op jit(solution)/shard_map/ppermute | solution.py:350
  2.3 27.7 %collective-permute-start.1 = (bf16[2,8,8,768]{3,2,1,0:T(8,128)(2,1)S(1)}, bf16[2,8,8,768]{3,2,1,0:T(8,128)(2,1)S(1)}, u32[]{:S(2)}, u32[]{:S(2)}) collective-permute-start(bf16[2,8,8,768]{3,2,1,0:T(8,128)(2,1)S(1)} %get-tuple-element.16), channel_id=1, source_target_pairs={{0,1},{2,3},{4,5},{6,7},{8,9},{10,11},{12,13},{14,15},{16,17},{18,... | collective-permute-start | bytes 589832 | tf_op jit(solution)/shard_map/ppermute | solution.py:349
  20.4 14.3 %copy-start.1 = (s32[128,512]{1,0:T(8,128)S(1)}, s32[128,512]{1,0:T(8,128)}, u32[]{:S(2)}) copy-start(s32[128,512]{1,0:T(8,128)} %refs_1_.3) | copy-start | bytes 786436
  20.4 14.3 %copy-start.2 = (bf16[8,16,768]{2,1,0:T(8,128)(2,1)S(1)}, bf16[8,16,768]{2,1,0:T(8,128)(2,1)}, u32[]{:S(2)}) copy-start(bf16[8,16,768]{2,1,0:T(8,128)(2,1)} %refs_0_.3) | copy-start | bytes 589828
  20.4 22.2 %all-to-all-start.1 = ((bf16[32,8,768]{2,1,0:T(8,128)(2,1)}), bf16[32,8,768]{2,1,0:T(8,128)(2,1)S(1)}, u32[]{:S(2)}, u32[]{:S(2)}) async-start(bf16[32,8,768]{2,1,0:T(8,128)(2,1)} %bitcast.3), calls=%async_computation.1 | async-start | bytes 786432 | tf_op jit(solution)/shard_map/all_to_all | solution.py:348
  30.1 17.6 %collective-permute-start.3 = (bf16[2,8,32,768]{3,2,1,0:T(8,128)(2,1)S(1)}, bf16[2,8,32,768]{3,2,1,0:T(8,128)(2,1)}, u32[]{:S(2)}, u32[]{:S(2)}) collective-permute-start(bf16[2,8,32,768]{3,2,1,0:T(8,128)(2,1)S(1)} %pad_maximum_fusion.refs_2_), channel_id=1, source_target_pairs={{32,64},{96,128},{160,192},{224,256},{288,320},{352,384},{416,448}... | collective-permute-start | bytes 2359304 | tf_op jit(solution)/shard_map/ppermute | solution.py:353
  32.0 15.7 %collective-permute-start.2 = (bf16[2,8,32,768]{3,2,1,0:T(8,128)(2,1)S(1)}, bf16[2,8,32,768]{3,2,1,0:T(8,128)(2,1)}, u32[]{:S(2)}, u32[]{:S(2)}) collective-permute-start(bf16[2,8,32,768]{3,2,1,0:T(8,128)(2,1)S(1)} %pad_maximum_fusion.refs_2_), channel_id=1, source_target_pairs={{0,32},{64,96},{128,160},{192,224},{256,288},{320,352},{384,416},{... | collective-permute-start | bytes 2359304 | tf_op jit(solution)/shard_map/ppermute | solution.py:352
  44.3 9.9 %all-to-all-start.2 = ((bf16[8,16,896]{2,1,0:T(8,128)(2,1)}), bf16[8,16,896]{2,1,0:T(8,128)(2,1)S(1)}, u32[]{:S(2)}, u32[]{:S(2)}) async-start(bf16[8,16,896]{2,1,0:T(8,128)(2,1)} %shard_map.76), calls=%async_computation.2 | async-start | bytes 458752 | tf_op jit(solution)/shard_map/all_to_all | solution.py:368
  47.6 6.5 %copy-start = (bf16[768,768]{1,0:T(8,128)(2,1)S(1)}, bf16[768,768]{1,0:T(8,128)(2,1)}, u32[]{:S(2)}) copy-start(bf16[768,768]{1,0:T(8,128)(2,1)} %weight_ref.1) | copy-start | bytes 3538948
